TPU v7x, 512 devices: a whole 4x8x8 slice. The times are simulated.
512 devices in a mesh: group: 8 (over x, core), vocab: 64 (over y, z).
Axes of the slice: x: 4, y: 8, z: 8, core: 2. Of those that a mesh axis runs over, the one named last changes fastest.
Arguments:
- shard_ids: int32 [65536, 1], P(('group', 'vocab')), may hold values from 0 to 63; in each aligned block of 128 rows (0 to 127, 128 to 255, ...) at most 4 rows name the same one
- row_ids: int32 [65536], P(('group', 'vocab')), may hold values from 0 to 1001
- table: bfloat16 [64128, 4096], P('vocab', 'group'), may hold values from -6 to 6
- cotangent: bfloat16 [65536, 4096], P(('group', 'vocab')), may hold values from -6 to 6
Outputs:
- embeds: bfloat16 [65536, 4096], P(('group', 'vocab'))
- table_grad: bfloat16 [64128, 4096], P('vocab', 'group')
Inputs may be any that keep to these rules, and one draw needn't show every extreme that they name: `shard_ids`: in each aligned block of 128 rows (the rows of one device), no shard is named by more than 4 rows, and in some blocks one shard is named by exactly 4.
All inputs are finite; a program needn't handle non-finite values.
Results may differ from a plain program's by a relative error of at most 0.001.
Values may be sent and summed in bfloat16 or wider, within the bound.
No kernel may reach another device: no remote copies, remote signals or barrier semaphores. Data moves between devices by JAX's collectives and lax.ppermute only.
A program may use at most 64 MiB of HBM per device.

v0:
```python
import jax
import jax.numpy as jnp
from jax import lax
from jax.sharding import PartitionSpec as P


def in_order(parts, dim):
    lengths = list(parts.shape[1:])
    lengths[dim] *= parts.shape[0]
    return jnp.moveaxis(parts, 0, dim).reshape(lengths)


def from_everyone(x, axis):
    copies = jnp.broadcast_to(x, (lax.axis_size(axis), *x.shape))
    return lax.all_to_all(copies, axis, split_axis=0, concat_axis=0, tiled=True)


def gather_directly(x, axis, dim):
    return in_order(from_everyone(x, axis), dim)


def split_up(x, dim, peers):
    before, after = (x.shape[:dim], x.shape[dim + 1 :])
    return jnp.moveaxis(x.reshape(*before, peers, -1, *after), dim, 0)


def exchange_both(x, axis, axes, splits, concats):
    sizes = [lax.axis_size(a) for a in axes]
    parts = split_up(x, splits[0], sizes[0])
    parts = jnp.moveaxis(split_up(parts, splits[1] + 1, sizes[1]), 0, 1)
    inside = parts.shape[2:]
    parts = parts.reshape(-1, *inside)
    parts = lax.all_to_all(parts, axis, split_axis=0, concat_axis=0, tiled=True)
    parts = in_order(parts.reshape(*sizes, *inside), concats[0] + 1)
    return in_order(parts, concats[1])


def per_device(shard_ids, row_ids, table, cotangent):
    tokens = cotangent.shape[0]
    width = cotangent.shape[1]
    owners = lax.axis_size("vocab")
    per_owner = 2 * tokens // owners
    slots = owners * per_owner
    rows_here = table.shape[0]
    shard = shard_ids[:, 0]
    owner_hot = (shard[:, None] == jnp.arange(owners, dtype=jnp.int32)[None, :]).astype(jnp.int32)
    ranking = jnp.sum(jnp.cumsum(owner_hot, axis=0) * owner_hot, axis=1) - 1
    slot_index = shard * per_owner + ranking
    slot_hot = slot_index[:, None] == jnp.arange(slots, dtype=jnp.int32)[None, :]
    outgoing = jnp.sum(jnp.where(slot_hot, (row_ids + 1)[:, None], 0), axis=0) - 1
    id_table = gather_directly(outgoing.reshape(1, owners, per_owner), "group", 0)
    received = lax.all_to_all(id_table, "vocab", split_axis=1, concat_axis=1, tiled=True)
    count = received.shape[0]
    flat = received.reshape(-1)
    picker = (flat[:, None] == jnp.arange(rows_here, dtype=jnp.int32)[None, :]).astype(jnp.bfloat16)
    found = jnp.dot(picker, table, preferred_element_type=jnp.float32).astype(jnp.bfloat16)
    found, picker = (
        found.reshape(received.shape + (table.shape[1],)),
        picker.reshape(count, -1, rows_here),
    )
    joined = exchange_both(found, ("group", "vocab"), ("group", "vocab"), (0, 1), (3, 1))
    buffer = joined.reshape(slots, width)
    embeds = jnp.take(buffer, slot_index, axis=0)
    slot_mask = slot_hot.astype(jnp.bfloat16)
    placed = lax.dot_general(
        slot_mask, cotangent, (((0,), (0,)), ((), ())), preferred_element_type=jnp.float32
    )
    sectioned = placed.astype(jnp.bfloat16).reshape(1, owners, per_owner, width)
    arrived = exchange_both(sectioned, ("group", "vocab"), ("group", "vocab"), (3, 1), (0, 1))
    flat_grads = arrived.reshape(-1, arrived.shape[3])
    flat_picker = picker.reshape(-1, rows_here)
    table_grad = lax.dot_general(
        flat_picker, flat_grads, (((0,), (0,)), ((), ())), preferred_element_type=jnp.float32
    )
    return (embeds, table_grad.astype(jnp.bfloat16))


def solution(mesh):
    in_specs = (
        P(("group", "vocab"), None),
        P(("group", "vocab")),
        P("vocab", "group"),
        P(("group", "vocab"), None),
    )
    out_specs = (P(("group", "vocab"), None), P("vocab", "group"))
    return jax.shard_map(
        per_device, mesh=mesh, in_specs=in_specs, out_specs=out_specs, check_vma=False
    )
```

profile of v0, /device:TPU:1, one launch (start us, length us, event | category | flops | bytes accessed | tf_op | source)
XLA Modules:
  0.0 186.0 jit_solution(4610712231551641404)
XLA Ops:
  0.6 0.7 broadcast_add_fusion.1
  1.4 0.7 fusion.7
  2.1 0.2 reduce_window_sum.11
  2.3 0.8 select_reduce_fusion.1
  3.1 0.7 and_bitcast_fusion
  3.8 0.1 select_reduce_fusion
  3.9 0.1 sub.14
  4.1 0.1 reshape.51
  4.2 13.8 %all_to_all.20 = s32[8,1,256]{2,1,0:T(1,128)S(1)} all-to-all(s32[8,1,256]{2,1,0:T(1,128)S(1)} %reshape.51), channel_id=1, replica_groups=mesh['group'=8,'vocab'=64] {'group'}, dimensions={0} | all-to-all | bytes 16384 | tf_op jit(solution)/shard_map/all_to_all | solution.py:15
  18.1 0.5 broadcast.53
  18.6 0.7 reduce
  19.3 0.8 copy.20
  20.1 12.7 %all-to-all-start.1 = ((s32[8,64,4]{0,2,1:T(4,128)}), s32[8,64,4]{0,2,1:T(4,128)S(1)}, u32[]{:S(2)}, u32[]{:S(2)}) async-start(s32[8,64,4]{0,2,1:T(4,128)} %copy.20), calls=%async_computation.1 | async-start | bytes 262144 | tf_op jit(solution)/shard_map/all_to_all | solution.py:52
  32.8 0.8 convolution_convert_fusion
  33.6 0.9 copy.27
  34.5 1.2 copy.24
  35.7 2.9 %copy.25 = bf16[512,1,1,4,512]{4,3,2,1,0:T(4,128)(2,1)} copy(bf16[512,1,1,4,512]{4,0,3,2,1:T(8,128)(2,1)S(1)} %bitcast.44) | data formatting | bytes 4194304 | tf_op jit(solution)/shard_map/reshape;transpose;transpose;reshape | solution.py:32
  38.6 5.7 %all-to-all-done.1 = s32[8,64,4]{0,2,1:T(4,128)S(1)} async-done(((s32[8,64,4]{0,2,1:T(4,128)}), s32[8,64,4]{0,2,1:T(4,128)S(1)}, u32[]{:S(2)}, u32[]{:S(2)}) %all-to-all-start.1) | async-done | bytes 8224 | tf_op jit(solution)/shard_map/all_to_all | solution.py:52
  44.3 10.4 %all-to-all-start.3 = ((bf16[512,1,1,4,512]{4,3,2,1,0:T(4,128)(2,1)}), bf16[512,1,1,4,512]{4,3,2,1,0:T(4,128)(2,1)S(1)}, u32[]{:S(2)}, u32[]{:S(2)}) async-start(bf16[512,1,1,4,512]{4,3,2,1,0:T(4,128)(2,1)} %copy.25), calls=%async_computation.3 | async-start | bytes 4194304 | tf_op jit(solution)/shard_map/all_to_all | solution.py:33
  54.7 0.5 copy.21
  55.2 0.2 eq.53
  55.3 4.9 %fusion.4 = bf16[2048,512]{1,0:T(8,128)(2,1)} fusion(bf16[1002,512]{1,0:T(8,128)(2,1)} %param.6, s32[2048]{0:T(1024)S(1)} %eq.53), kind=kOutput, calls=%fused_computation.7 | convolution fusion | flops 2104446976 | bytes 3131392 | tf_op jit(solution)/shard_map/dot_general | solution.py:56
  60.2 4.0 %reshape_transpose_transpose_reshape_reshape_reshape.3 = bf16[512,1,1,4,512]{4,3,0,2,1:T(4,128)(2,1)} reshape(bf16[2048,512]{1,0:T(8,128)(2,1)} %fusion.4) | data formatting | bytes 4194304 | tf_op jit(solution)/shard_map/reshape;transpose;transpose;reshape;reshape;reshape | solution.py:32
  64.2 47.3 %all-to-all-done.3 = bf16[512,1,1,4,512]{4,3,2,1,0:T(4,128)(2,1)S(1)} async-done(((bf16[512,1,1,4,512]{4,3,2,1,0:T(4,128)(2,1)}), bf16[512,1,1,4,512]{4,3,2,1,0:T(4,128)(2,1)S(1)}, u32[]{:S(2)}, u32[]{:S(2)}) %all-to-all-start.3) | async-done | bytes 2097184 | tf_op jit(solution)/shard_map/all_to_all | solution.py:33
  111.4 11.3 %all-to-all-start.2 = ((bf16[512,1,1,4,512]{4,3,2,1,0:T(4,128)(2,1)}), bf16[512,1,1,4,512]{4,3,2,1,0:T(4,128)(2,1)}, u32[]{:S(2)}, u32[]{:S(2)}) async-start(bf16[512,1,1,4,512]{4,3,2,1,0:T(4,128)(2,1)} %bitcast.42), calls=%async_computation.2 | async-start | bytes 4194304 | tf_op jit(solution)/shard_map/all_to_all | solution.py:33
  122.8 2.1 %reshape_reshape.7 = bf16[2048,512]{1,0:T(8,128)(2,1)} reshape(bf16[8,64,1,4,512]{4,3,1,0,2:T(4,128)(2,1)S(1)} %bitcast.41) | data formatting | bytes 4194304 | tf_op jit(solution)/shard_map/reshape;reshape | solution.py:70
  124.8 5.3 %fusion.5 = bf16[1002,512]{1,0:T(8,128)(2,1)} fusion(bf16[2048,512]{1,0:T(8,128)(2,1)} %reshape_reshape.7, s32[2048]{0:T(1024)S(1)} %eq.53), kind=kOutput, calls=%fused_computation.8 | convolution fusion | flops 2103911424 | bytes 3131392 | tf_op jit(solution)/shard_map/dot_general | solution.py:72
  130.1 46.6 %all-to-all-done.2 = bf16[512,1,1,4,512]{4,3,2,1,0:T(4,128)(2,1)} async-done(((bf16[512,1,1,4,512]{4,3,2,1,0:T(4,128)(2,1)}), bf16[512,1,1,4,512]{4,3,2,1,0:T(4,128)(2,1)}, u32[]{:S(2)}, u32[]{:S(2)}) %all-to-all-start.2) | async-done | bytes 2097184 | tf_op jit(solution)/shard_map/all_to_all | solution.py:33
  176.8 3.8 %copy.23 = bf16[8,64,1,1,4,512]{5,0,4,1,3,2:T(8,128)(2,1)S(1)} copy(bf16[8,64,1,1,4,512]{5,4,1,0,3,2:T(4,128)(2,1)} %bitcast.6) | data formatting | bytes 4194304 | tf_op jit(solution)/shard_map/reshape | solution.py:34
  180.6 0.9 copy.26
  181.5 2.2 %gather_fusion = bf16[128,4096]{1,0:T(8,128)(2,1)} fusion(bf16[256,4096]{1,0:T(8,128)(2,1)S(1)} %bitcast.40, s32[1024]{0:T(1024)S(1)} %pad_clamp_fusion), kind=kCustom, calls=%fused_computation | custom fusion | bytes 2097664 | tf_op jit(solution)/shard_map/jit(_take)/gather | solution.py:63
  183.6 2.4 %broadcast_select_fusion = bf16[128,4096]{1,0:T(8,128)(2,1)} fusion(bf16[128,4096]{1,0:T(8,128)(2,1)} %gather_fusion, pred[128]{0:T(512)(128)(4,1)S(1)} %get-tuple-element.2), kind=kLoop, calls=%fused_computation.9 | loop fusion | flops 524288 | bytes 2097280 | tf_op jit(solution)/shard_map/jit(_take)/select_n | solution.py:63
  (9 shorter events, 0.2 us)
Async XLA Ops:
  0.6 32.1 %copy-start = (bf16[128,4096]{1,0:T(8,128)(2,1)S(1)}, bf16[128,4096]{1,0:T(8,128)(2,1)}, u32[]{:S(2)}) copy-start(bf16[128,4096]{1,0:T(8,128)(2,1)} %param.7) | copy-start | bytes 3145732
  20.1 24.2 %all-to-all-start.1 = ((s32[8,64,4]{0,2,1:T(4,128)}), s32[8,64,4]{0,2,1:T(4,128)S(1)}, u32[]{:S(2)}, u32[]{:S(2)}) async-start(s32[8,64,4]{0,2,1:T(4,128)} %copy.20), calls=%async_computation.1 | async-start | bytes 262144 | tf_op jit(solution)/shard_map/all_to_all | solution.py:52
  44.3 67.1 %all-to-all-start.3 = ((bf16[512,1,1,4,512]{4,3,2,1,0:T(4,128)(2,1)}), bf16[512,1,1,4,512]{4,3,2,1,0:T(4,128)(2,1)S(1)}, u32[]{:S(2)}, u32[]{:S(2)}) async-start(bf16[512,1,1,4,512]{4,3,2,1,0:T(4,128)(2,1)} %copy.25), calls=%async_computation.3 | async-start | bytes 4194304 | tf_op jit(solution)/shard_map/all_to_all | solution.py:33
  111.4 65.3 %all-to-all-start.2 = ((bf16[512,1,1,4,512]{4,3,2,1,0:T(4,128)(2,1)}), bf16[512,1,1,4,512]{4,3,2,1,0:T(4,128)(2,1)}, u32[]{:S(2)}, u32[]{:S(2)}) async-start(bf16[512,1,1,4,512]{4,3,2,1,0:T(4,128)(2,1)} %bitcast.42), calls=%async_computation.2 | async-start | bytes 4194304 | tf_op jit(solution)/shard_map/all_to_all | solution.py:33
where the time goes:
time: 187 us; the launch traced here: 186 us
  waiting for transfers between devices  99.6 us (53%)
  starting transfers between devices  34.4 us (18%)
  local copies, waits for them, and re-layouts  20.2 us (11%)
  blocking collectives  13.8 us (7%)
  matrix products  11 us (6%)
  other arithmetic  6.3 us (3%)
    all_to_all x2, waiting for transfers between devices, exchange_both(): parts = lax.all_to_all(parts, axis, split_axis=0, concat_axis=0, tiled=True)  93.9 us
    all_to_all x2, starting transfers between devices, exchange_both(): parts = lax.all_to_all(parts, axis, split_axis=0, concat_axis=0, tiled=True)  21.7 us
    all_to_all x1, blocking collectives, from_everyone(): return lax.all_to_all(copies, axis, split_axis=0, concat_axis=0, tiled=True)  13.8 us
    all_to_all x1, starting transfers between devices, per_device(): lax.all_to_all(id_table, 'vocab', split_axis=1, concat_axis=1, tiled=True)  12.7 us
    another operation x2, local copies, waits for them, and re-layouts, exchange_both(): parts = parts.reshape(-1, *inside)  6.89 us
    all_to_all x1, waiting for transfers between devices, per_device(): lax.all_to_all(id_table, 'vocab', split_axis=1, concat_axis=1, tiled=True)  5.7 us
    dot_general x1, matrix products, per_device(): lax.dot_general(flat_picker, flat_grads, (((0,), (0,)), ((), ())), prefer...  5.27 us
    dot_general x1, matrix products, per_device(): jnp.dot(picker, table, preferred_element_type=jnp.float32)  4.86 us
  transfers between devices with their start and end apart: 3, of which 3 were waited for; matrix products, arithmetic and copies ran while one was open for 12% of the time, Pallas kernels for 0%

commit v1 on v0

v1 whole, which is shorter than its diff:
```python
import functools

import jax
import jax.numpy as jnp
from jax import lax
from jax.experimental import pallas as pl
from jax.experimental.pallas import tpu as pltpu
from jax.sharding import PartitionSpec as P

LANES = 128


def to_column(row):
    n = row.shape[1]
    here = lax.broadcasted_iota(jnp.int32, (n, n), 0)
    there = lax.broadcasted_iota(jnp.int32, (n, n), 1)
    return jnp.sum(jnp.where(here == there, row, 0), axis=1, keepdims=True)


def pack_kernel(cap, pieces, owners, shard_ref, row_ref, cot_ref, out_ref, ids_ref, slot_ref, hot):
    tokens = shard_ref.shape[1]
    rows = hot.shape[0]

    @pl.when(pl.program_id(0) == 0)
    def _():
        shard = shard_ref[...]
        column = to_column(shard)
        i = lax.broadcasted_iota(jnp.int32, (tokens, tokens), 0)
        j = lax.broadcasted_iota(jnp.int32, (tokens, tokens), 1)
        earlier = jnp.where((column == shard) & (i < j), 1, 0)
        slot = shard * cap + jnp.sum(earlier, axis=0, keepdims=True)
        slot_ref[...] = slot
        target = lax.broadcasted_iota(jnp.int32, (tokens, owners * cap), 1)
        named = jnp.where(to_column(slot) == target, to_column(row_ref[...]) + 1, 0)
        ids_ref[...] = jnp.sum(named, axis=0, keepdims=True) - 1
        line = lax.broadcasted_iota(jnp.int32, (rows, tokens), 0)
        for c in range(pieces):
            hot[:, c * tokens : (c + 1) * tokens] = jnp.where(
                line == slot * pieces + c, 1.0, 0.0
            ).astype(jnp.bfloat16)

    groups = cot_ref.shape[1] // (pieces * LANES)
    right = []
    for g in range(groups):
        right.append(
            jnp.concatenate(
                [cot_ref[:, (g * pieces + c) * LANES : (g * pieces + c + 1) * LANES] for c in range(pieces)],
                axis=0,
            )
        )
    placed = jnp.dot(hot[...], jnp.concatenate(right, axis=1), preferred_element_type=jnp.float32)
    placed = placed.astype(jnp.bfloat16)
    for g in range(groups):
        block = placed[:, g * LANES : (g + 1) * LANES]
        out_ref[g * owners : (g + 1) * owners] = block.reshape(owners, rows // owners, LANES)


def pack(shard, row, cotangent, groups, owners, cap):
    tokens, width = cotangent.shape
    pieces = width // groups // LANES
    rows = owners * cap * pieces
    step = 2
    return pl.pallas_call(
        functools.partial(pack_kernel, cap, pieces, owners),
        grid=(groups // step,),
        in_specs=[
            pl.BlockSpec((1, tokens), lambda g: (0, 0)),
            pl.BlockSpec((1, tokens), lambda g: (0, 0)),
            pl.BlockSpec((tokens, step * pieces * LANES), lambda g: (0, g)),
        ],
        out_specs=[
            pl.BlockSpec((step * owners, cap * pieces, LANES), lambda g: (g, 0, 0)),
            pl.BlockSpec((1, owners * cap), lambda g: (0, 0)),
            pl.BlockSpec((1, tokens), lambda g: (0, 0)),
        ],
        out_shape=[
            jax.ShapeDtypeStruct((groups * owners, cap * pieces, LANES), jnp.bfloat16),
            jax.ShapeDtypeStruct((1, owners * cap), jnp.int32),
            jax.ShapeDtypeStruct((1, tokens), jnp.int32),
        ],
        scratch_shapes=[pltpu.VMEM((rows, pieces * tokens), jnp.bfloat16)],
        name="pack",
    )(shard, row, cotangent)


def unpack_kernel(pieces, slot_ref, got_ref, out_ref, hot):
    tokens = slot_ref.shape[1]
    rows = hot.shape[1]

    @pl.when(pl.program_id(0) == 0)
    def _():
        slot = to_column(slot_ref[...])
        line = lax.broadcasted_iota(jnp.int32, (tokens, rows), 1)
        for c in range(pieces):
            hot[c * tokens : (c + 1) * tokens, :] = jnp.where(
                line == slot * pieces + c, 1.0, 0.0
            ).astype(jnp.bfloat16)

    groups = out_ref.shape[1] // (pieces * LANES)
    owners = got_ref.shape[0] // groups
    right = [got_ref[g * owners : (g + 1) * owners].reshape(rows, LANES) for g in range(groups)]
    picked = jnp.dot(hot[...], jnp.concatenate(right, axis=1), preferred_element_type=jnp.float32)
    picked = picked.astype(jnp.bfloat16)
    for g in range(groups):
        for c in range(pieces):
            out_ref[:, (g * pieces + c) * LANES : (g * pieces + c + 1) * LANES] = picked[
                c * tokens : (c + 1) * tokens, g * LANES : (g + 1) * LANES
            ]


def unpack(slot, got, groups, width):
    tokens = slot.shape[1]
    pieces = width // groups // LANES
    owners = got.shape[0] // groups
    rows = owners * got.shape[1]
    step = 2
    return pl.pallas_call(
        functools.partial(unpack_kernel, pieces),
        grid=(groups // step,),
        in_specs=[
            pl.BlockSpec((1, tokens), lambda g: (0, 0)),
            pl.BlockSpec((step * owners, got.shape[1], LANES), lambda g: (g, 0, 0)),
        ],
        out_specs=pl.BlockSpec((tokens, step * pieces * LANES), lambda g: (0, g)),
        out_shape=jax.ShapeDtypeStruct((tokens, width), jnp.bfloat16),
        scratch_shapes=[pltpu.VMEM((pieces * tokens, rows), jnp.bfloat16)],
        name="unpack",
    )(slot, got)


def exchange(x):
    return lax.all_to_all(x, ("group", "vocab"), split_axis=0, concat_axis=0, tiled=True)


def per_device(shard_ids, row_ids, table, cotangent):
    tokens, width = cotangent.shape
    groups = lax.axis_size("group")
    owners = lax.axis_size("vocab")
    cap = 2 * tokens // owners
    peers = groups * owners
    rows_here, columns = table.shape
    packed, outgoing, slot = pack(
        shard_ids.reshape(1, tokens), row_ids.reshape(1, tokens), cotangent, groups, owners, cap
    )
    arrived = exchange(packed)
    near = lax.all_gather(outgoing, "group", axis=0, tiled=True)
    every = lax.all_gather(near, "vocab", axis=0)
    mine = lax.dynamic_slice_in_dim(every, lax.axis_index("vocab") * cap, cap, axis=2)
    wanted = jnp.moveaxis(mine, 0, 1).reshape(-1)
    picker = (wanted[:, None] == jnp.arange(rows_here, dtype=jnp.int32)[None, :]).astype(jnp.bfloat16)
    found = jnp.dot(picker, table, preferred_element_type=jnp.float32).astype(jnp.bfloat16)
    got = exchange(found.reshape(peers, cap * columns // LANES, LANES))
    table_grad = lax.dot_general(
        picker,
        arrived.reshape(peers * cap, columns),
        (((0,), (0,)), ((), ())),
        preferred_element_type=jnp.float32,
    )
    embeds = unpack(slot, got, groups, width)
    return (embeds, table_grad.astype(jnp.bfloat16))


def solution(mesh):
    in_specs = (
        P(("group", "vocab"), None),
        P(("group", "vocab")),
        P("vocab", "group"),
        P(("group", "vocab"), None),
    )
    out_specs = (P(("group", "vocab"), None), P("vocab", "group"))
    return jax.shard_map(
        per_device, mesh=mesh, in_specs=in_specs, out_specs=out_specs, check_vma=False
    )
```

time: 187 us -> 203 us (1.086)
  blocking collectives: 13.8 us -> 80.3 us
  waiting for transfers between devices: 99.6 us -> 46.8 us
  starting transfers between devices: 34.4 us -> 48.7 us
  local copies, waits for them, and re-layouts: 20.2 us -> 7.27 us
  Pallas kernels: 0 us -> 9.92 us
  other arithmetic: 6.3 us -> 0 us
  matrix products: 11 us -> 8.9 us
    all_gather x0 -> x2, blocking collectives: none -> 80.3 us  [the longest x1 68.4 us: per_device(): every = lax.all_gather(near, 'vocab', axis=0)]
    all_to_all x3 -> x2, waiting for transfers between devices: 99.6 us -> 46.8 us  [exchange(): lax.all_to_all(x, ('group', 'vocab'), split_axis=0, concat_axis=0, tiled=...]
    all_to_all x3 -> x2, starting transfers between devices: 34.4 us -> 48.7 us  [exchange(): lax.all_to_all(x, ('group', 'vocab'), split_axis=0, concat_axis=0, tiled=...]
    all_to_all x1 -> x0, blocking collectives: 13.8 us -> none  [from_everyone(): return lax.all_to_all(copies, axis, split_axis=0, concat_axis=0, tiled=True)]
    another operation x4 -> x0, local copies, waits for them, and re-layouts: 10.1 us -> none  [the longest x2 6.89 us: exchange_both(): parts = parts.reshape(-1, *inside)]
    pallas_call x0 -> x2, Pallas kernels: none -> 9.92 us  [the longest x1 5.22 us: pack(): pl.pallas_call(functools.partial(pack_kernel, cap, pieces, owners), grid=...]
    select_n x2 -> x0, other arithmetic: 2.36 us -> none  [per_device(): embeds = jnp.take(buffer, slot_index, axis=0)]
    reshape x3 -> x2, local copies, waits for them, and re-layouts: 4.59 us -> 6.91 us  [the longest x1 4.34 us: per_device(): got = exchange(found.reshape(peers, cap * columns // LANES, LANES))]
  transfers between devices with their start and end apart: 3 -> 2, of which waited for: 3 -> 1; matrix products, arithmetic and copies ran while one was open for 12% -> 8% of each run, Pallas kernels for 0% -> 0%
where the time goes in v1:
time: 203 us
  blocking collectives  80.3 us (40%)
  starting transfers between devices  48.7 us (24%)
  waiting for transfers between devices  46.8 us (23%)
  Pallas kernels  9.92 us (5%)
  matrix products  8.9 us (4%)
  local copies, waits for them, and re-layouts  7.27 us (4%)
    all_gather x1, blocking collectives, per_device(): every = lax.all_gather(near, 'vocab', axis=0)  68.4 us
    all_to_all x2, starting transfers between devices, exchange(): lax.all_to_all(x, ('group', 'vocab'), split_axis=0, concat_axis=0, tiled=...  48.7 us
    all_to_all x2, waiting for transfers between devices, exchange(): lax.all_to_all(x, ('group', 'vocab'), split_axis=0, concat_axis=0, tiled=...  46.8 us
    all_gather x1, blocking collectives, per_device(): near = lax.all_gather(outgoing, 'group', axis=0, tiled=True)  12 us
    dot_general x1, matrix products, per_device(): lax.dot_general(picker, arrived.reshape(peers * cap, columns), (((0,), (0...  5.27 us
    pallas_call x1, Pallas kernels, pack(): pl.pallas_call(functools.partial(pack_kernel, cap, pieces, owners), grid=...  5.22 us
    pallas_call x1, Pallas kernels, unpack(): pl.pallas_call(functools.partial(unpack_kernel, pieces), grid=(groups //...  4.7 us
    reshape x1, local copies, waits for them, and re-layouts, per_device(): got = exchange(found.reshape(peers, cap * columns // LANES, LANES))  4.34 us
  transfers between devices with their start and end apart: 2, of which 1 were waited for; matrix products, arithmetic and copies ran while one was open for 8% of the time, Pallas kernels for 0%

profile of v1, /device:TPU:1, one launch (start us, length us, event | category | flops | bytes accessed | tf_op | source)
XLA Modules:
  0.0 202.6 jit_solution(8843355919929845050)
XLA Ops:
  0.6 0.0 copy-start
  0.6 5.2 %pack.1 = (bf16[512,16,128]{2,1,0:T(8,128)(2,1)}, s32[1,256]{1,0:T(1,128)}, s32[1,128]{1,0:T(1,128)}) custom-call(s32[1,128]{1,0:T(1,128)} %bitcast.14, s32[1,128]{1,0:T(1,128)} %bitcast.15, bf16[128,4096]{1,0:T(8,128)(2,1)} %cot_ref.1), custom_call_target="tpu_custom_call" | custom-call | tf_op jit(solution)/shard_map/pack/pallas_call | solution.py:63
  5.9 0.0 copy-start.1
  5.9 22.2 %all-to-all-start.1 = ((bf16[512,16,128]{2,1,0:T(8,128)(2,1)}), bf16[512,16,128]{2,1,0:T(8,128)(2,1)S(1)}, u32[]{:S(2)}, u32[]{:S(2)}) async-start(bf16[512,16,128]{2,1,0:T(8,128)(2,1)} %get-tuple-element.7), calls=%async_computation.1 | async-start | bytes 4194304 | tf_op jit(solution)/shard_map/all_to_all | solution.py:132
  28.0 0.0 copy-done.1
  28.1 12.0 %all-gather.1 = s32[8,1,256]{2,1,0:T(1,128)S(1)} all-gather(s32[1,1,256]{2,1,0:T(1,128)S(1)} %bitcast.13), channel_id=1, replica_groups=mesh['group'=8,'vocab'=64] {'group'}, dimensions={0}, use_global_device_ids=true | all-gather | bytes 9216 | tf_op jit(solution)/shard_map/all_gather | solution.py:146
  40.0 68.4 %all-gather = s32[512,256]{1,0:T(8,128)S(1)} all-gather(s32[8,256]{1,0:T(8,128)S(1)} %bitcast.12), channel_id=2, replica_groups=mesh['group'=8,'vocab'=64] {'vocab'}, dimensions={0}, use_global_device_ids=true | all-gather | bytes 532480 | tf_op jit(solution)/shard_map/all_gather | solution.py:147
  108.4 0.1 dynamic-slice_bitcast_fusion
  108.5 0.1 copy.7
  108.6 0.2 eq.15
  108.7 0.0 copy-done
  108.8 3.6 %fusion.4 = bf16[2048,512]{1,0:T(8,128)(2,1)} fusion(bf16[1002,512]{1,0:T(8,128)(2,1)S(1)} %copy-done, s32[2048]{0:T(1024)S(1)} %eq.15), kind=kOutput, calls=%fused_computation.5 | convolution fusion | flops 2104446976 | bytes 3131392 | tf_op jit(solution)/shard_map/dot_general | solution.py:151
  112.4 4.3 %reshape.19 = bf16[512,16,128]{2,1,0:T(8,128)(2,1)} reshape(bf16[2048,512]{1,0:T(8,128)(2,1)} %fusion.4) | data formatting | bytes 4194304 | tf_op jit(solution)/shard_map/reshape | solution.py:152
  116.7 0.0 all-to-all-done.1
  116.7 26.5 %all-to-all-start = ((bf16[512,16,128]{2,1,0:T(8,128)(2,1)}), bf16[512,16,128]{2,1,0:T(8,128)(2,1)}, u32[]{:S(2)}, u32[]{:S(2)}) async-start(bf16[512,16,128]{2,1,0:T(8,128)(2,1)} %reshape.19), calls=%async_computation | async-start | bytes 4194304 | tf_op jit(solution)/shard_map/all_to_all | solution.py:132
  143.3 2.6 %reshape.20 = bf16[2048,512]{1,0:T(8,128)(2,1)} reshape(bf16[512,16,128]{2,1,0:T(8,128)(2,1)S(1)} %all-to-all-done.1) | data formatting | bytes 4194304 | tf_op jit(solution)/shard_map/reshape | solution.py:155
  145.8 5.3 %fusion.5 = bf16[1002,512]{1,0:T(8,128)(2,1)} fusion(bf16[2048,512]{1,0:T(8,128)(2,1)} %reshape.20, s32[2048]{0:T(1024)S(1)} %eq.15), kind=kOutput, calls=%fused_computation.6 | convolution fusion | flops 2103911424 | bytes 3131392 | tf_op jit(solution)/shard_map/dot_general | solution.py:153
  151.1 46.8 %all-to-all-done.got_ref = bf16[512,16,128]{2,1,0:T(8,128)(2,1)} async-done(((bf16[512,16,128]{2,1,0:T(8,128)(2,1)}), bf16[512,16,128]{2,1,0:T(8,128)(2,1)}, u32[]{:S(2)}, u32[]{:S(2)}) %all-to-all-start) | async-done | bytes 2097184 | tf_op jit(solution)/shard_map/all_to_all | solution.py:132
  197.9 4.7 %unpack.1 = bf16[128,4096]{1,0:T(8,128)(2,1)} custom-call(s32[1,128]{1,0:T(1,128)} %get-tuple-element.5.slot_ref, bf16[512,16,128]{2,1,0:T(8,128)(2,1)} %all-to-all-done.got_ref), custom_call_target="tpu_custom_call" | custom-call | tf_op jit(solution)/shard_map/unpack/pallas_call | solution.py:117
  (1 shorter events, 0.0 us)
Async XLA Ops:
  0.6 108.1 %copy-start = (bf16[1002,512]{1,0:T(8,128)(2,1)S(1)}, bf16[1002,512]{1,0:T(8,128)(2,1)}, u32[]{:S(2)}) copy-start(bf16[1002,512]{1,0:T(8,128)(2,1)} %param.6) | copy-start | bytes 3078148
  5.9 22.2 %copy-start.1 = (s32[1,256]{1,0:T(1,128)S(1)}, s32[1,256]{1,0:T(1,128)}, u32[]{:S(2)}) copy-start(s32[1,256]{1,0:T(1,128)} %get-tuple-element.6) | copy-start | bytes 3076
  5.9 110.9 %all-to-all-start.1 = ((bf16[512,16,128]{2,1,0:T(8,128)(2,1)}), bf16[512,16,128]{2,1,0:T(8,128)(2,1)S(1)}, u32[]{:S(2)}, u32[]{:S(2)}) async-start(bf16[512,16,128]{2,1,0:T(8,128)(2,1)} %get-tuple-element.7), calls=%async_computation.1 | async-start | bytes 4194304 | tf_op jit(solution)/shard_map/all_to_all | solution.py:132
  116.7 81.1 %all-to-all-start = ((bf16[512,16,128]{2,1,0:T(8,128)(2,1)}), bf16[512,16,128]{2,1,0:T(8,128)(2,1)}, u32[]{:S(2)}, u32[]{:S(2)}) async-start(bf16[512,16,128]{2,1,0:T(8,128)(2,1)} %reshape.19), calls=%async_computation | async-start | bytes 4194304 | tf_op jit(solution)/shard_map/all_to_all | solution.py:132

commit v2 on v1

--- a/solution.py
+++ b/solution.py
@@ -5,6 +5,7 @@
 from jax import lax
 from jax.experimental import pallas as pl
 from jax.experimental.pallas import tpu as pltpu
+from jax.sharding import Mesh
 from jax.sharding import PartitionSpec as P
 
 LANES = 128
@@ -30,9 +31,10 @@
         earlier = jnp.where((column == shard) & (i < j), 1, 0)
         slot = shard * cap + jnp.sum(earlier, axis=0, keepdims=True)
         slot_ref[...] = slot
-        target = lax.broadcasted_iota(jnp.int32, (tokens, owners * cap), 1)
-        named = jnp.where(to_column(slot) == target, to_column(row_ref[...]) + 1, 0)
-        ids_ref[...] = jnp.sum(named, axis=0, keepdims=True) - 1
+        target = 2 * lax.broadcasted_iota(jnp.int32, (tokens, owners * cap // 2), 1)
+        place, name = to_column(slot), to_column(row_ref[...]) + 1
+        named = jnp.where(place == target, name, 0) + jnp.where(place == target + 1, name << 16, 0)
+        ids_ref[...] = jnp.sum(named, axis=0, keepdims=True)
         line = lax.broadcasted_iota(jnp.int32, (rows, tokens), 0)
         for c in range(pieces):
             hot[:, c * tokens : (c + 1) * tokens] = jnp.where(
@@ -70,12 +72,12 @@
         ],
         out_specs=[
             pl.BlockSpec((step * owners, cap * pieces, LANES), lambda g: (g, 0, 0)),
-            pl.BlockSpec((1, owners * cap), lambda g: (0, 0)),
+            pl.BlockSpec((1, owners * cap // 2), lambda g: (0, 0)),
             pl.BlockSpec((1, tokens), lambda g: (0, 0)),
         ],
         out_shape=[
             jax.ShapeDtypeStruct((groups * owners, cap * pieces, LANES), jnp.bfloat16),
-            jax.ShapeDtypeStruct((1, owners * cap), jnp.int32),
+            jax.ShapeDtypeStruct((1, owners * cap // 2), jnp.int32),
             jax.ShapeDtypeStruct((1, tokens), jnp.int32),
         ],
         scratch_shapes=[pltpu.VMEM((rows, pieces * tokens), jnp.bfloat16)],
@@ -129,13 +131,13 @@
 
 
 def exchange(x):
-    return lax.all_to_all(x, ("group", "vocab"), split_axis=0, concat_axis=0, tiled=True)
+    return lax.all_to_all(x, ("group", "outer", "inner"), split_axis=0, concat_axis=0, tiled=True)
 
 
 def per_device(shard_ids, row_ids, table, cotangent):
     tokens, width = cotangent.shape
     groups = lax.axis_size("group")
-    owners = lax.axis_size("vocab")
+    owners = lax.axis_size("outer") * lax.axis_size("inner")
     cap = 2 * tokens // owners
     peers = groups * owners
     rows_here, columns = table.shape
@@ -143,10 +145,12 @@
         shard_ids.reshape(1, tokens), row_ids.reshape(1, tokens), cotangent, groups, owners, cap
     )
     arrived = exchange(packed)
-    near = lax.all_gather(outgoing, "group", axis=0, tiled=True)
-    every = lax.all_gather(near, "vocab", axis=0)
-    mine = lax.dynamic_slice_in_dim(every, lax.axis_index("vocab") * cap, cap, axis=2)
-    wanted = jnp.moveaxis(mine, 0, 1).reshape(-1)
+    words = lax.all_gather(outgoing, "inner", axis=0, tiled=True)
+    words = lax.all_gather(words, "outer", axis=0, tiled=True)
+    words = lax.all_gather(words, "group", axis=0, tiled=True)
+    here = lax.axis_index("outer") * lax.axis_size("inner") + lax.axis_index("inner")
+    mine = lax.dynamic_slice_in_dim(words, here * (cap // 2), cap // 2, axis=1)
+    wanted = jnp.stack([mine & 0xFFFF, mine >> 16], axis=2).reshape(-1) - 1
     picker = (wanted[:, None] == jnp.arange(rows_here, dtype=jnp.int32)[None, :]).astype(jnp.bfloat16)
     found = jnp.dot(picker, table, preferred_element_type=jnp.float32).astype(jnp.bfloat16)
     got = exchange(found.reshape(peers, cap * columns // LANES, LANES))
@@ -161,13 +165,12 @@
 
 
 def solution(mesh):
-    in_specs = (
-        P(("group", "vocab"), None),
-        P(("group", "vocab")),
-        P("vocab", "group"),
-        P(("group", "vocab"), None),
+    groups, owners = mesh.shape["group"], mesh.shape["vocab"]
+    inner = 1 << (owners.bit_length() - 1) // 2
+    grid = Mesh(mesh.devices.reshape(groups, owners // inner, inner), ("group", "outer", "inner"))
+    vocab = ("outer", "inner")
+    in_specs = (P(("group", *vocab), None), P(("group", *vocab)), P(vocab, "group"), P(("group", *vocab), None))
+    out_specs = (P(("group", *vocab), None), P(vocab, "group"))
+    return jax.shard_map(
+        per_device, mesh=grid, in_specs=in_specs, out_specs=out_specs, check_vma=False
     )
-    out_specs = (P(("group", "vocab"), None), P("vocab", "group"))
-    return jax.shard_map(
-        per_device, mesh=mesh, in_specs=in_specs, out_specs=out_specs, check_vma=False
-    )

time: 203 us -> 210 us (1.034)
  blocking collectives: 80.3 us -> 95 us
  starting transfers between devices: 48.7 us -> 37 us
  local copies, waits for them, and re-layouts: 7.27 us -> 10.8 us
    all_gather x2 -> x3, blocking collectives: 80.3 us -> 95 us  [the longest x1 38.5 us: per_device(): words = lax.all_gather(outgoing, 'inner', axis=0, tiled=True)]
    all_to_all x2, starting transfers between devices: 48.7 us -> 37 us  [exchange(): lax.all_to_all(x, ('group', 'outer', 'inner'), split_axis=0, concat_axis=...]
    sub x0 -> x2, local copies, waits for them, and re-layouts: none -> 2.68 us  [per_device(): wanted = jnp.stack([mine & 65535, mine >> 16], axis=2).reshape(-1) - 1]
  transfers between devices with their start and end apart: 2 -> 2, of which waited for: 1 -> 1; matrix products, arithmetic and copies ran while one was open for 8% -> 10% of each run, Pallas kernels for 0% -> 0%
where the time goes in v2:
time: 210 us
  blocking collectives  95 us (45%)
  waiting for transfers between devices  46.8 us (22%)
  starting transfers between devices  37 us (18%)
  local copies, waits for them, and re-layouts  10.8 us (5%)
  Pallas kernels  9.9 us (5%)
  matrix products  8.91 us (4%)
    all_to_all x2, waiting for transfers between devices, exchange(): lax.all_to_all(x, ('group', 'outer', 'inner'), split_axis=0, concat_axis=...  46.8 us
    all_gather x1, blocking collectives, per_device(): words = lax.all_gather(outgoing, 'inner', axis=0, tiled=True)  38.5 us
    all_to_all x2, starting transfers between devices, exchange(): lax.all_to_all(x, ('group', 'outer', 'inner'), split_axis=0, concat_axis=...  37 us
    all_gather x1, blocking collectives, per_device(): words = lax.all_gather(words, 'outer', axis=0, tiled=True)  33.2 us
    all_gather x1, blocking collectives, per_device(): words = lax.all_gather(words, 'group', axis=0, tiled=True)  23.3 us
    dot_general x1, matrix products, per_device(): lax.dot_general(picker, arrived.reshape(peers * cap, columns), (((0,), (0...  5.27 us
    pallas_call x1, Pallas kernels, pack(): pl.pallas_call(functools.partial(pack_kernel, cap, pieces, owners), grid=...  5.2 us
    pallas_call x1, Pallas kernels, unpack(): pl.pallas_call(functools.partial(unpack_kernel, pieces), grid=(groups //...  4.7 us
  transfers between devices with their start and end apart: 2, of which 1 were waited for; matrix products, arithmetic and copies ran while one was open for 10% of the time, Pallas kernels for 0%

profile of v2, /device:TPU:1, one launch (start us, length us, event | category | flops | bytes accessed | tf_op | source)
XLA Modules:
  0.0 209.9 jit_solution(6622795416701374475)
XLA Ops:
  0.6 0.0 copy-start
  0.6 5.2 %pack.1 = (bf16[512,16,128]{2,1,0:T(8,128)(2,1)}, s32[1,128]{1,0:T(1,128)}, s32[1,128]{1,0:T(1,128)}) custom-call(s32[1,128]{1,0:T(1,128)} %bitcast.11, s32[1,128]{1,0:T(1,128)} %bitcast.12, bf16[128,4096]{1,0:T(8,128)(2,1)} %cot_ref.1), custom_call_target="tpu_custom_call" | custom-call | tf_op jit(solution)/shard_map/pack/pallas_call | solution.py:65
  5.8 0.0 copy-start.1
  5.9 22.2 %all-to-all-start.1 = ((bf16[512,16,128]{2,1,0:T(8,128)(2,1)}), bf16[512,16,128]{2,1,0:T(8,128)(2,1)S(1)}, u32[]{:S(2)}, u32[]{:S(2)}) async-start(bf16[512,16,128]{2,1,0:T(8,128)(2,1)} %get-tuple-element.7), calls=%async_computation.1 | async-start | bytes 4194304 | tf_op jit(solution)/shard_map/all_to_all | solution.py:134
  28.0 0.0 copy-done.1
  28.0 38.5 %all-gather = s32[8,1,128]{2,1,0:T(1,128)S(1)} all-gather(s32[1,1,128]{2,1,0:T(1,128)S(1)} %bitcast.13), channel_id=1, replica_groups=mesh['group'=8,'outer'=8,'inner'=8] {'inner'}, dimensions={0}, use_global_device_ids=true | all-gather | bytes 4608 | tf_op jit(solution)/shard_map/all_gather | solution.py:148
  66.5 33.2 %all_gather.10 = s32[64,128]{1,0:T(8,128)S(1)} all-gather(s32[8,128]{1,0:T(8,128)S(1)} %bitcast.10), channel_id=1, replica_groups=mesh['group'=8,'outer'=8,'inner'=8] {'outer'}, dimensions={0}, use_global_device_ids=true | all-gather | bytes 36864 | tf_op jit(solution)/shard_map/all_gather | solution.py:149
  99.7 23.3 %all_gather.11 = s32[512,128]{1,0:T(8,128)S(1)} all-gather(s32[64,128]{1,0:T(8,128)S(1)} %all_gather.10), channel_id=1, replica_groups=mesh['group'=8,'outer'=8,'inner'=8] {'group'}, dimensions={0}, use_global_device_ids=true | all-gather | bytes 294912 | tf_op jit(solution)/shard_map/all_gather | solution.py:150
  123.0 0.8 and_bitcast_fusion
  123.8 1.1 copy.7
  124.9 0.1 copy.8
  125.1 1.0 copy.9
  126.1 1.7 sub.7
  127.7 0.0 copy-done
  127.7 3.6 %fusion.4 = bf16[2048,512]{1,0:T(8,128)(2,1)} fusion(bf16[1002,512]{1,0:T(8,128)(2,1)S(1)} %copy-done, s32[2048]{0:T(1024)S(1)} %sub.7), kind=kOutput, calls=%fused_computation.5 | convolution fusion | flops 2104446976 | bytes 3131392 | tf_op jit(solution)/shard_map/dot_general | solution.py:155
  131.4 4.3 %reshape.26 = bf16[512,16,128]{2,1,0:T(8,128)(2,1)} reshape(bf16[2048,512]{1,0:T(8,128)(2,1)} %fusion.4) | data formatting | bytes 4194304 | tf_op jit(solution)/shard_map/reshape | solution.py:156
  135.7 0.0 all-to-all-done.1
  135.7 14.8 %all-to-all-start = ((bf16[512,16,128]{2,1,0:T(8,128)(2,1)}), bf16[512,16,128]{2,1,0:T(8,128)(2,1)}, u32[]{:S(2)}, u32[]{:S(2)}) async-start(bf16[512,16,128]{2,1,0:T(8,128)(2,1)} %reshape.26), calls=%async_computation | async-start | bytes 4194304 | tf_op jit(solution)/shard_map/all_to_all | solution.py:134
  150.6 2.6 %reshape.27 = bf16[2048,512]{1,0:T(8,128)(2,1)} reshape(bf16[512,16,128]{2,1,0:T(8,128)(2,1)S(1)} %all-to-all-done.1) | data formatting | bytes 4194304 | tf_op jit(solution)/shard_map/reshape | solution.py:159
  153.1 5.3 %fusion.5 = bf16[1002,512]{1,0:T(8,128)(2,1)} fusion(bf16[2048,512]{1,0:T(8,128)(2,1)} %reshape.27, s32[2048]{0:T(1024)S(1)} %sub.7), kind=kOutput, calls=%fused_computation.6 | convolution fusion | flops 2103911424 | bytes 3131392 | tf_op jit(solution)/shard_map/dot_general | solution.py:157
  158.4 46.8 %all-to-all-done.got_ref = bf16[512,16,128]{2,1,0:T(8,128)(2,1)} async-done(((bf16[512,16,128]{2,1,0:T(8,128)(2,1)}), bf16[512,16,128]{2,1,0:T(8,128)(2,1)}, u32[]{:S(2)}, u32[]{:S(2)}) %all-to-all-start) | async-done | bytes 2097184 | tf_op jit(solution)/shard_map/all_to_all | solution.py:134
  205.2 4.7 %unpack.1 = bf16[128,4096]{1,0:T(8,128)(2,1)} custom-call(s32[1,128]{1,0:T(1,128)} %get-tuple-element.5.slot_ref, bf16[512,16,128]{2,1,0:T(8,128)(2,1)} %all-to-all-done.got_ref), custom_call_target="tpu_custom_call" | custom-call | tf_op jit(solution)/shard_map/unpack/pallas_call | solution.py:119
  (1 shorter events, 0.0 us)
Async XLA Ops:
  0.6 127.1 %copy-start = (bf16[1002,512]{1,0:T(8,128)(2,1)S(1)}, bf16[1002,512]{1,0:T(8,128)(2,1)}, u32[]{:S(2)}) copy-start(bf16[1002,512]{1,0:T(8,128)(2,1)} %param.6) | copy-start | bytes 3078148
  5.8 22.2 %copy-start.1 = (s32[1,128]{1,0:T(1,128)S(1)}, s32[1,128]{1,0:T(1,128)}, u32[]{:S(2)}) copy-start(s32[1,128]{1,0:T(1,128)} %get-tuple-element.6) | copy-start | bytes 1540
  5.9 129.9 %all-to-all-start.1 = ((bf16[512,16,128]{2,1,0:T(8,128)(2,1)}), bf16[512,16,128]{2,1,0:T(8,128)(2,1)S(1)}, u32[]{:S(2)}, u32[]{:S(2)}) async-start(bf16[512,16,128]{2,1,0:T(8,128)(2,1)} %get-tuple-element.7), calls=%async_computation.1 | async-start | bytes 4194304 | tf_op jit(solution)/shard_map/all_to_all | solution.py:134
  135.7 69.5 %all-to-all-start = ((bf16[512,16,128]{2,1,0:T(8,128)(2,1)}), bf16[512,16,128]{2,1,0:T(8,128)(2,1)}, u32[]{:S(2)}, u32[]{:S(2)}) async-start(bf16[512,16,128]{2,1,0:T(8,128)(2,1)} %reshape.26), calls=%async_computation | async-start | bytes 4194304 | tf_op jit(solution)/shard_map/all_to_all | solution.py:134

commit v3 on v2

--- a/solution.py
+++ b/solution.py
@@ -18,27 +18,42 @@
     return jnp.sum(jnp.where(here == there, row, 0), axis=1, keepdims=True)
 
 
-def pack_kernel(cap, pieces, owners, shard_ref, row_ref, cot_ref, out_ref, ids_ref, slot_ref, hot):
+def slots_kernel(cap, shard_ref, row_ref, ids_ref, slot_ref):
     tokens = shard_ref.shape[1]
+    words = ids_ref.shape[1]
+    shard = shard_ref[...]
+    i = lax.broadcasted_iota(jnp.int32, (tokens, tokens), 0)
+    j = lax.broadcasted_iota(jnp.int32, (tokens, tokens), 1)
+    earlier = jnp.where((to_column(shard) == shard) & (i < j), 1, 0)
+    slot = shard * cap + jnp.sum(earlier, axis=0, keepdims=True)
+    slot_ref[...] = slot
+    target = 2 * lax.broadcasted_iota(jnp.int32, (tokens, words), 1)
+    place, name = to_column(slot), to_column(row_ref[...]) + 1
+    named = jnp.where(place == target, name, 0) + jnp.where(place == target + 1, name << 16, 0)
+    ids_ref[...] = jnp.sum(named, axis=0, keepdims=True)
+
+
+def slots(shard, row, owners, cap):
+    return pl.pallas_call(
+        functools.partial(slots_kernel, cap),
+        out_shape=[
+            jax.ShapeDtypeStruct((1, owners * cap // 2), jnp.int32),
+            jax.ShapeDtypeStruct(shard.shape, jnp.int32),
+        ],
+        name="slots",
+    )(shard, row)
+
+
+def pack_kernel(pieces, owners, slot_ref, cot_ref, out_ref, hot):
+    tokens = slot_ref.shape[1]
     rows = hot.shape[0]
 
     @pl.when(pl.program_id(0) == 0)
     def _():
-        shard = shard_ref[...]
-        column = to_column(shard)
-        i = lax.broadcasted_iota(jnp.int32, (tokens, tokens), 0)
-        j = lax.broadcasted_iota(jnp.int32, (tokens, tokens), 1)
-        earlier = jnp.where((column == shard) & (i < j), 1, 0)
-        slot = shard * cap + jnp.sum(earlier, axis=0, keepdims=True)
-        slot_ref[...] = slot
-        target = 2 * lax.broadcasted_iota(jnp.int32, (tokens, owners * cap // 2), 1)
-        place, name = to_column(slot), to_column(row_ref[...]) + 1
-        named = jnp.where(place == target, name, 0) + jnp.where(place == target + 1, name << 16, 0)
-        ids_ref[...] = jnp.sum(named, axis=0, keepdims=True)
         line = lax.broadcasted_iota(jnp.int32, (rows, tokens), 0)
         for c in range(pieces):
             hot[:, c * tokens : (c + 1) * tokens] = jnp.where(
-                line == slot * pieces + c, 1.0, 0.0
+                line == slot_ref[...] * pieces + c, 1.0, 0.0
             ).astype(jnp.bfloat16)
 
     groups = cot_ref.shape[1] // (pieces * LANES)
@@ -57,32 +72,116 @@
         out_ref[g * owners : (g + 1) * owners] = block.reshape(owners, rows // owners, LANES)
 
 
-def pack(shard, row, cotangent, groups, owners, cap):
+def pack(slot, cotangent, groups, owners, cap):
     tokens, width = cotangent.shape
     pieces = width // groups // LANES
     rows = owners * cap * pieces
     step = 2
     return pl.pallas_call(
-        functools.partial(pack_kernel, cap, pieces, owners),
+        functools.partial(pack_kernel, pieces, owners),
         grid=(groups // step,),
         in_specs=[
             pl.BlockSpec((1, tokens), lambda g: (0, 0)),
-            pl.BlockSpec((1, tokens), lambda g: (0, 0)),
             pl.BlockSpec((tokens, step * pieces * LANES), lambda g: (0, g)),
         ],
-        out_specs=[
-            pl.BlockSpec((step * owners, cap * pieces, LANES), lambda g: (g, 0, 0)),
-            pl.BlockSpec((1, owners * cap // 2), lambda g: (0, 0)),
-            pl.BlockSpec((1, tokens), lambda g: (0, 0)),
-        ],
-        out_shape=[
-            jax.ShapeDtypeStruct((groups * owners, cap * pieces, LANES), jnp.bfloat16),
-            jax.ShapeDtypeStruct((1, owners * cap // 2), jnp.int32),
-            jax.ShapeDtypeStruct((1, tokens), jnp.int32),
-        ],
+        out_specs=pl.BlockSpec((step * owners, cap * pieces, LANES), lambda g: (g, 0, 0)),
+        out_shape=jax.ShapeDtypeStruct((groups * owners, cap * pieces, LANES), jnp.bfloat16),
         scratch_shapes=[pltpu.VMEM((rows, pieces * tokens), jnp.bfloat16)],
+        cost_estimate=pl.CostEstimate(
+            flops=2 * rows * pieces * tokens * groups * LANES,
+            bytes_accessed=2 * (tokens * width + groups * rows * LANES),
+            transcendentals=0,
+        ),
         name="pack",
-    )(shard, row, cotangent)
+    )(slot, cotangent)
+
+
+def pick_kernel(inner, here_ref, below_ref, near_ref, above_ref, out_ref):
+    outer_at, inner_at = here_ref[0], here_ref[1]
+    rows = jnp.concatenate([below_ref[inner:, :], near_ref[...], above_ref[...]], axis=0)
+    owners, lanes = rows.shape
+    each = lanes // owners
+    lane = lax.broadcasted_iota(jnp.int32, (owners, lanes), 1)
+    line = lax.broadcasted_iota(jnp.int32, (owners, lanes), 0)
+    far = lax.rem(outer_at + line // inner + owners // inner - 3, owners // inner)
+    close = lax.rem(inner_at + lax.rem(line, inner) + inner - 3, inner)
+    device = far * inner + close
+    out = jnp.zeros((owners, lanes), jnp.int32)
+    for w in range(each):
+        mine = jnp.where(lane == (outer_at * inner + inner_at) * each + w, rows, 0)
+        out = out + jnp.where(lane == w * owners + device, jnp.sum(mine, axis=1, keepdims=True), 0)
+    out_ref[...] = jnp.sum(out, axis=0, keepdims=True)
+
+
+def pick(here, below, near, above, inner):
+    return pl.pallas_call(
+        functools.partial(pick_kernel, inner),
+        in_specs=[pl.BlockSpec(memory_space=pltpu.SMEM)] + [pl.BlockSpec(memory_space=pltpu.VMEM)] * 3,
+        out_specs=pl.BlockSpec(memory_space=pltpu.VMEM),
+        out_shape=jax.ShapeDtypeStruct((1, near.shape[1]), jnp.int32),
+        name="pick",
+    )(here, below, near, above)
+
+
+def lookup_kernel(cap, words_ref, table_ref, out_ref, lines):
+    groups = words_ref.shape[0]
+    devices = out_ref.shape[0]
+    rows, columns = table_ref.shape
+    owners = devices // groups
+    pieces = columns // LANES
+    here = lax.broadcasted_iota(jnp.int32, (owners, cap // 2 * owners), 0)
+    there = lax.broadcasted_iota(jnp.int32, (owners, cap // 2 * owners), 1)
+    row = lax.broadcasted_iota(jnp.int32, (devices, rows), 1) + 1
+    for w in range(cap // 2):
+        word = jnp.concatenate(
+            [
+                jnp.sum(jnp.where(there == here + w * owners, words_ref[g], 0), axis=1, keepdims=True)
+                for g in range(groups)
+            ],
+            axis=0,
+        )
+        for half in range(2):
+            name = word >> 16 if half else word & 0xFFFF
+            hot = jnp.where(name == row, 1.0, 0.0).astype(jnp.bfloat16)
+            found = jnp.dot(hot, table_ref[...], preferred_element_type=jnp.float32)
+            for c in range(pieces):
+                line = (2 * w + half) * pieces + c
+                lines[pl.ds(line, devices, stride=cap * pieces), :] = found[:, c * LANES : (c + 1) * LANES]
+    out_ref[...] = lines[...].astype(jnp.bfloat16).reshape(out_ref.shape)
+
+
+def lookup(words, table, owners, cap):
+    groups = words.shape[0]
+    rows, columns = table.shape
+    pieces = columns // LANES
+    step = 2
+    return pl.pallas_call(
+        functools.partial(lookup_kernel, cap),
+        grid=(groups // step,),
+        in_specs=[
+            pl.BlockSpec((step, 1, words.shape[2]), lambda g: (g, 0, 0)),
+            pl.BlockSpec((rows, columns), lambda g: (0, 0)),
+        ],
+        out_specs=pl.BlockSpec((step * owners, cap * pieces, LANES), lambda g: (g, 0, 0)),
+        out_shape=jax.ShapeDtypeStruct((groups * owners, cap * pieces, LANES), jnp.bfloat16),
+        scratch_shapes=[pltpu.VMEM((step * owners * cap * pieces, LANES), jnp.float32)],
+        cost_estimate=pl.CostEstimate(
+            flops=2 * groups * owners * cap * rows * columns,
+            bytes_accessed=2 * (rows * columns + groups * owners * cap * columns),
+            transcendentals=0,
+        ),
+        name="lookup",
+    )(words, table)
+
+
+def shifted(x, axis, offset):
+    size = lax.axis_size(axis)
+    return lax.ppermute(x, axis, [(i, (i - offset) % size) for i in range(size)])
+
+
+def neighbours(x, axis):
+    near = jnp.concatenate([shifted(x, axis, -1), x, shifted(x, axis, 1)], axis=0)
+    return shifted(near, axis, -3), near, shifted(near, axis, 3)
 
 
 def unpack_kernel(pieces, slot_ref, got_ref, out_ref, hot):
@@ -141,19 +240,20 @@
     cap = 2 * tokens // owners
     peers = groups * owners
     rows_here, columns = table.shape
-    packed, outgoing, slot = pack(
-        shard_ids.reshape(1, tokens), row_ids.reshape(1, tokens), cotangent, groups, owners, cap
-    )
+    outgoing, slot = slots(shard_ids.reshape(1, tokens), row_ids.reshape(1, tokens), owners, cap)
+    below, near, above = neighbours(outgoing, "inner")
+    packed = pack(slot, cotangent, groups, owners, cap)
+    line, packed = lax.optimization_barrier((jnp.concatenate([below[1:], near, above], axis=0), packed))
     arrived = exchange(packed)
-    words = lax.all_gather(outgoing, "inner", axis=0, tiled=True)
-    words = lax.all_gather(words, "outer", axis=0, tiled=True)
-    words = lax.all_gather(words, "group", axis=0, tiled=True)
-    here = lax.axis_index("outer") * lax.axis_size("inner") + lax.axis_index("inner")
-    mine = lax.dynamic_slice_in_dim(words, here * (cap // 2), cap // 2, axis=1)
-    wanted = jnp.stack([mine & 0xFFFF, mine >> 16], axis=2).reshape(-1) - 1
+    below, near, above = neighbours(line, "outer")
+    here = jnp.stack([lax.axis_index("outer"), lax.axis_index("inner")]).astype(jnp.int32)
+    mine = pick(here, below, near, above, lax.axis_size("inner"))
+    words = lax.all_gather(mine, "group", axis=0)
+    got = exchange(lookup(words, table, owners, cap))
+    words = words.reshape(groups, cap // 2, owners)
+    wanted = jnp.stack([words & 0xFFFF, words >> 16], axis=2).reshape(groups, cap, owners)
+    wanted = jnp.swapaxes(wanted, 1, 2).reshape(-1) - 1
     picker = (wanted[:, None] == jnp.arange(rows_here, dtype=jnp.int32)[None, :]).astype(jnp.bfloat16)
-    found = jnp.dot(picker, table, preferred_element_type=jnp.float32).astype(jnp.bfloat16)
-    got = exchange(found.reshape(peers, cap * columns // LANES, LANES))
     table_grad = lax.dot_general(
         picker,
         arrived.reshape(peers * cap, columns),
@@ -166,7 +266,7 @@
 
 def solution(mesh):
     groups, owners = mesh.shape["group"], mesh.shape["vocab"]
-    inner = 1 << (owners.bit_length() - 1) // 2
+    inner = 8
     grid = Mesh(mesh.devices.reshape(groups, owners // inner, inner), ("group", "outer", "inner"))
     vocab = ("outer", "inner")
     in_specs = (P(("group", *vocab), None), P(("group", *vocab)), P(vocab, "group"), P(("group", *vocab), None))

time: 210 us -> 202 us (0.962)
  blocking collectives: 95 us -> 13.7 us
  waiting for transfers between devices: 46.8 us -> 91 us
  starting transfers between devices: 37 us -> 67.1 us
  Pallas kernels: 9.9 us -> 18.6 us
  local copies, waits for them, and re-layouts: 10.8 us -> 3.69 us
  matrix products: 8.91 us -> 5.27 us
    all_gather x3 -> x1, blocking collectives: 95 us -> 13.7 us  [per_device(): words = lax.all_gather(mine, 'group', axis=0)]
    ppermute x0 -> x8, waiting for transfers between devices: none -> 44.8 us  [shifted(): lax.ppermute(x, axis, [(i, (i - offset) % size) for i in range(size)])]
    ppermute x0 -> x8, starting transfers between devices: none -> 35.7 us  [shifted(): lax.ppermute(x, axis, [(i, (i - offset) % size) for i in range(size)])]
    pallas_call x1 -> x4, Pallas kernels: 5.2 us -> 13.9 us  [the longest x1 6.41 us: lookup(): pl.pallas_call(functools.partial(lookup_kernel, cap), grid=(groups // ste...]
    all_to_all x2, starting transfers between devices: 37 us -> 31.4 us  [exchange(): lax.all_to_all(x, ('group', 'outer', 'inner'), split_axis=0, concat_axis=...]
    reshape x1 -> x0, local copies, waits for them, and re-layouts: 4.34 us -> none  [per_device(): got = exchange(found.reshape(peers, cap * columns // LANES, LANES))]
    dot_general x1 -> x0, matrix products: 3.64 us -> none  [per_device(): jnp.dot(picker, table, preferred_element_type=jnp.float32)]
    sub x2, local copies, waits for them, and re-layouts: 2.68 us -> 0.32 us  [per_device(): wanted = jnp.swapaxes(wanted, 1, 2).reshape(-1) - 1]
  transfers between devices with their start and end apart: 2 -> 10, of which waited for: 1 -> 5; matrix products, arithmetic and copies ran while one was open for 10% -> 4% of each run, Pallas kernels for 0% -> 6%
where the time goes in v3:
time: 202 us
  waiting for transfers between devices  91 us (45%)
  starting transfers between devices  67.1 us (33%)
  Pallas kernels  18.6 us (9%)
  blocking collectives  13.7 us (7%)
  matrix products  5.27 us (3%)
  local copies, waits for them, and re-layouts  3.69 us (2%)
    all_to_all x2, waiting for transfers between devices, exchange(): lax.all_to_all(x, ('group', 'outer', 'inner'), split_axis=0, concat_axis=...  46.2 us
    ppermute x8, waiting for transfers between devices, shifted(): lax.ppermute(x, axis, [(i, (i - offset) % size) for i in range(size)])  44.8 us
    ppermute x8, starting transfers between devices, shifted(): lax.ppermute(x, axis, [(i, (i - offset) % size) for i in range(size)])  35.7 us
    all_to_all x2, starting transfers between devices, exchange(): lax.all_to_all(x, ('group', 'outer', 'inner'), split_axis=0, concat_axis=...  31.4 us
    all_gather x1, blocking collectives, per_device(): words = lax.all_gather(mine, 'group', axis=0)  13.7 us
    pallas_call x1, Pallas kernels, lookup(): pl.pallas_call(functools.partial(lookup_kernel, cap), grid=(groups // ste...  6.41 us
    dot_general x1, matrix products, per_device(): lax.dot_general(picker, arrived.reshape(peers * cap, columns), (((0,), (0...  5.27 us
    pallas_call x1, Pallas kernels, unpack(): pl.pallas_call(functools.partial(unpack_kernel, pieces), grid=(groups //...  4.7 us
  transfers between devices with their start and end apart: 10, of which 5 were waited for; matrix products, arithmetic and copies ran while one was open for 4% of the time, Pallas kernels for 6%

profile of v3, /device:TPU:1, one launch (start us, length us, event | category | flops | bytes accessed | tf_op | source)
XLA Modules:
  0.0 201.6 jit_solution(3911505199331832532)
XLA Ops:
  0.6 1.4 slots.1
  2.1 11.6 %collective-permute-start.1 = (s32[1,128]{1,0:T(1,128)}, s32[1,128]{1,0:T(1,128)S(1)}, u32[]{:S(2)}, u32[]{:S(2)}) collective-permute-start(s32[1,128]{1,0:T(1,128)} %get-tuple-element.7), channel_id=1, source_target_pairs={{0,7},{1,0},{2,1},{3,2},{4,3},{5,4},{6,5},{7,6},{8,15},{9,8},{10,9... | collective-permute-start | bytes 1544 | tf_op jit(solution)/shard_map/ppermute | solution.py:179
  13.7 1.9 collective-permute-start
  15.6 3.7 %collective-permute-done = s32[1,128]{1,0:T(1,128)S(1)} collective-permute-done((s32[1,128]{1,0:T(1,128)}, s32[1,128]{1,0:T(1,128)S(1)}, u32[]{:S(2)}, u32[]{:S(2)}) %collective-permute-start) | collective-permute-done | bytes 544 | tf_op jit(solution)/shard_map/ppermute | solution.py:179
  19.3 0.7 pad_add_fusion
  20.0 1.9 collective-permute-start.3
  21.9 5.2 %collective-permute-start.2 = (s32[3,128]{1,0:T(4,128)S(1)}, s32[3,128]{1,0:T(4,128)S(1)}, u32[]{:S(2)}, u32[]{:S(2)}) collective-permute-start(s32[3,128]{1,0:T(4,128)S(1)} %pad_add_fusion), channel_id=1, source_target_pairs={{0,3},{1,4},{2,5},{3,6},{4,7},{5,0},{6,1},{7,2},{8,11},{9,12},{10,... | collective-permute-start | bytes 4616 | tf_op jit(solution)/shard_map/ppermute | solution.py:179
  27.1 4.7 %pack.1 = bf16[512,16,128]{2,1,0:T(8,128)(2,1)} custom-call(s32[1,128]{1,0:T(1,128)} %get-tuple-element.6.slot_ref, bf16[128,4096]{1,0:T(8,128)(2,1)} %cot_ref.1), custom_call_target="tpu_custom_call" | custom-call | flops 1073741824 | bytes 3145728 | tf_op jit(solution)/shard_map/pack/pallas_call | solution.py:80
  31.8 0.0 collective-permute-done.3
  31.8 15.6 %all-to-all-start.1 = ((bf16[512,16,128]{2,1,0:T(8,128)(2,1)}), bf16[512,16,128]{2,1,0:T(8,128)(2,1)S(1)}, u32[]{:S(2)}, u32[]{:S(2)}) async-start(bf16[512,16,128]{2,1,0:T(8,128)(2,1)} %pack.1), calls=%async_computation.1 | async-start | bytes 4194304 | tf_op jit(solution)/shard_map/all_to_all | solution.py:233
  47.4 3.3 %collective-permute-start.4 = (s32[8,128]{1,0:T(8,128)S(1)}, s32[8,128]{1,0:T(8,128)S(1)}, u32[]{:S(2)}, u32[]{:S(2)}) collective-permute-start(s32[8,128]{1,0:T(8,128)S(1)} %concatenate.11), channel_id=1, source_target_pairs={{0,8},{8,16},{16,24},{24,32},{32,40},{40,48},{48,56},{56,0},{1,9},... | collective-permute-start | bytes 12296 | tf_op jit(solution)/shard_map/ppermute | solution.py:179
  50.7 3.5 %collective-permute-start.5 = (s32[8,128]{1,0:T(8,128)S(1)}, s32[8,128]{1,0:T(8,128)S(1)}, u32[]{:S(2)}, u32[]{:S(2)}) collective-permute-start(s32[8,128]{1,0:T(8,128)S(1)} %concatenate.11), channel_id=1, source_target_pairs={{0,56},{8,0},{16,8},{24,16},{32,24},{40,32},{48,40},{56,48},{1,57}... | collective-permute-start | bytes 12296 | tf_op jit(solution)/shard_map/ppermute | solution.py:179
  54.2 36.1 %collective-permute-done.4 = s32[8,128]{1,0:T(8,128)S(1)} collective-permute-done((s32[8,128]{1,0:T(8,128)S(1)}, s32[8,128]{1,0:T(8,128)S(1)}, u32[]{:S(2)}, u32[]{:S(2)}) %collective-permute-start.4) | collective-permute-done | bytes 4128 | tf_op jit(solution)/shard_map/ppermute | solution.py:179
  90.3 0.3 collective-permute-done.5
  90.6 6.1 %collective-permute-start.7 = (s32[24,128]{1,0:T(8,128)S(1)}, s32[24,128]{1,0:T(8,128)S(1)}, u32[]{:S(2)}, u32[]{:S(2)}) collective-permute-start(s32[24,128]{1,0:T(8,128)S(1)} %constant_dynamic-update-slice_fusion.near_ref), channel_id=1, source_target_pairs={{0,40},{8,48},{16,56},{24,0},{32,8},{40,16},{48,24},{56,32},{1,41}... | collective-permute-start | bytes 36872 | tf_op jit(solution)/shard_map/ppermute | solution.py:179
  96.7 2.2 %collective-permute-start.6 = (s32[24,128]{1,0:T(8,128)S(1)}, s32[24,128]{1,0:T(8,128)S(1)}, u32[]{:S(2)}, u32[]{:S(2)}) collective-permute-start(s32[24,128]{1,0:T(8,128)S(1)} %constant_dynamic-update-slice_fusion.near_ref), channel_id=1, source_target_pairs={{0,24},{8,32},{16,40},{24,48},{32,56},{40,0},{48,8},{56,16},{1,25}... | collective-permute-start | bytes 36872 | tf_op jit(solution)/shard_map/ppermute | solution.py:179
  98.9 0.6 pad_add_fusion.1.here_ref
  99.5 0.0 collective-permute-done.7.above_ref
  99.5 4.7 %collective-permute-done.6.below_ref = s32[24,128]{1,0:T(8,128)S(1)} collective-permute-done((s32[24,128]{1,0:T(8,128)S(1)}, s32[24,128]{1,0:T(8,128)S(1)}, u32[]{:S(2)}, u32[]{:S(2)}) %collective-permute-start.6) | collective-permute-done | bytes 12320 | tf_op jit(solution)/shard_map/ppermute | solution.py:179
  104.2 0.6 copy-done.3
  104.8 1.4 pick.1
  106.3 13.7 %all-gather.1.words_ref = s32[8,1,128]{2,1,0:T(1,128)} all-gather(s32[1,1,128]{2,1,0:T(1,128)} %bitcast.10), channel_id=2, replica_groups=mesh['group'=8,'outer'=8,'inner'=8] {'group'}, dimensions={0}, use_global_device_ids=true | all-gather | bytes 4608 | tf_op jit(solution)/shard_map/all_gather | solution.py:251
  120.0 6.4 %lookup.1 = bf16[512,16,128]{2,1,0:T(8,128)(2,1)} custom-call(s32[8,1,128]{2,1,0:T(1,128)} %all-gather.1.words_ref, bf16[1002,512]{1,0:T(8,128)(2,1)} %table_ref.1), custom_call_target="tpu_custom_call" | custom-call | flops 2101346304 | bytes 3123200 | tf_op jit(solution)/shard_map/lookup/pallas_call | solution.py:158
  126.4 15.8 %all-to-all-start = ((bf16[512,16,128]{2,1,0:T(8,128)(2,1)}), bf16[512,16,128]{2,1,0:T(8,128)(2,1)}, u32[]{:S(2)}, u32[]{:S(2)}) async-start(bf16[512,16,128]{2,1,0:T(8,128)(2,1)} %lookup.1), calls=%async_computation | async-start | bytes 4194304 | tf_op jit(solution)/shard_map/all_to_all | solution.py:233
  142.3 0.1 and.20
  142.4 0.1 shift_right_arithmetic.18
  142.5 0.2 copy.14
  142.6 0.2 sub.13
  142.8 2.6 %reshape.51 = bf16[2048,512]{1,0:T(8,128)(2,1)} reshape(bf16[512,16,128]{2,1,0:T(8,128)(2,1)S(1)} %all-to-all-done.1) | data formatting | bytes 4194304 | tf_op jit(solution)/shard_map/reshape | solution.py:259
  145.4 5.3 %fusion.2 = bf16[1002,512]{1,0:T(8,128)(2,1)} fusion(bf16[2048,512]{1,0:T(8,128)(2,1)} %reshape.51, s32[2048]{0:T(1024)S(1)} %sub.13), kind=kOutput, calls=%fused_computation.3 | convolution fusion | flops 2103911424 | bytes 3131392 | tf_op jit(solution)/shard_map/dot_general | solution.py:257
  150.6 46.2 %all-to-all-done.got_ref = bf16[512,16,128]{2,1,0:T(8,128)(2,1)} async-done(((bf16[512,16,128]{2,1,0:T(8,128)(2,1)}), bf16[512,16,128]{2,1,0:T(8,128)(2,1)}, u32[]{:S(2)}, u32[]{:S(2)}) %all-to-all-start) | async-done | bytes 2097184 | tf_op jit(solution)/shard_map/all_to_all | solution.py:233
  196.9 4.7 %unpack.1 = bf16[128,4096]{1,0:T(8,128)(2,1)} custom-call(s32[1,128]{1,0:T(1,128)} %get-tuple-element.6.slot_ref, bf16[512,16,128]{2,1,0:T(8,128)(2,1)} %all-to-all-done.got_ref), custom_call_target="tpu_custom_call" | custom-call | tf_op jit(solution)/shard_map/unpack/pallas_call | solution.py:218
  (21 shorter events, 0.1 us)
Async XLA Ops:
  2.1 29.7 %copy-start.4 = (s32[1,128]{1,0:T(1,128)S(1)}, s32[1,128]{1,0:T(1,128)}, u32[]{:S(2)}) copy-start(s32[1,128]{1,0:T(1,128)} %get-tuple-element.7) | copy-start | bytes 1540
  2.1 13.6 %collective-permute-start.1 = (s32[1,128]{1,0:T(1,128)}, s32[1,128]{1,0:T(1,128)S(1)}, u32[]{:S(2)}, u32[]{:S(2)}) collective-permute-start(s32[1,128]{1,0:T(1,128)} %get-tuple-element.7), channel_id=1, source_target_pairs={{0,7},{1,0},{2,1},{3,2},{4,3},{5,4},{6,5},{7,6},{8,15},{9,8},{10,9... | collective-permute-start | bytes 1544 | tf_op jit(solution)/shard_map/ppermute | solution.py:179
  13.7 5.6 %collective-permute-start = (s32[1,128]{1,0:T(1,128)}, s32[1,128]{1,0:T(1,128)S(1)}, u32[]{:S(2)}, u32[]{:S(2)}) collective-permute-start(s32[1,128]{1,0:T(1,128)} %get-tuple-element.7), channel_id=1, source_target_pairs={{0,1},{1,2},{2,3},{3,4},{4,5},{5,6},{6,7},{7,0},{8,9},{9,10},{10,1... | collective-permute-start | bytes 1544 | tf_op jit(solution)/shard_map/ppermute | solution.py:179
  20.0 11.8 %collective-permute-start.3 = (s32[3,128]{1,0:T(4,128)S(1)}, s32[3,128]{1,0:T(4,128)S(1)}, u32[]{:S(2)}, u32[]{:S(2)}) collective-permute-start(s32[3,128]{1,0:T(4,128)S(1)} %pad_add_fusion), channel_id=1, source_target_pairs={{0,5},{1,6},{2,7},{3,0},{4,1},{5,2},{6,3},{7,4},{8,13},{9,14},{10,... | collective-permute-start | bytes 4616 | tf_op jit(solution)/shard_map/ppermute | solution.py:179
  21.9 9.8 %collective-permute-start.2 = (s32[3,128]{1,0:T(4,128)S(1)}, s32[3,128]{1,0:T(4,128)S(1)}, u32[]{:S(2)}, u32[]{:S(2)}) collective-permute-start(s32[3,128]{1,0:T(4,128)S(1)} %pad_add_fusion), channel_id=1, source_target_pairs={{0,3},{1,4},{2,5},{3,6},{4,7},{5,0},{6,1},{7,2},{8,11},{9,12},{10,... | collective-permute-start | bytes 4616 | tf_op jit(solution)/shard_map/ppermute | solution.py:179
  31.8 94.6 %all-to-all-start.1 = ((bf16[512,16,128]{2,1,0:T(8,128)(2,1)}), bf16[512,16,128]{2,1,0:T(8,128)(2,1)S(1)}, u32[]{:S(2)}, u32[]{:S(2)}) async-start(bf16[512,16,128]{2,1,0:T(8,128)(2,1)} %pack.1), calls=%async_computation.1 | async-start | bytes 4194304 | tf_op jit(solution)/shard_map/all_to_all | solution.py:233
  47.4 42.8 %collective-permute-start.4 = (s32[8,128]{1,0:T(8,128)S(1)}, s32[8,128]{1,0:T(8,128)S(1)}, u32[]{:S(2)}, u32[]{:S(2)}) collective-permute-start(s32[8,128]{1,0:T(8,128)S(1)} %concatenate.11), channel_id=1, source_target_pairs={{0,8},{8,16},{16,24},{24,32},{32,40},{40,48},{48,56},{56,0},{1,9},... | collective-permute-start | bytes 12296 | tf_op jit(solution)/shard_map/ppermute | solution.py:179
  50.7 39.9 %collective-permute-start.5 = (s32[8,128]{1,0:T(8,128)S(1)}, s32[8,128]{1,0:T(8,128)S(1)}, u32[]{:S(2)}, u32[]{:S(2)}) collective-permute-start(s32[8,128]{1,0:T(8,128)S(1)} %concatenate.11), channel_id=1, source_target_pairs={{0,56},{8,0},{16,8},{24,16},{32,24},{40,32},{48,40},{56,48},{1,57}... | collective-permute-start | bytes 12296 | tf_op jit(solution)/shard_map/ppermute | solution.py:179
  90.6 13.6 %copy-start = (s32[24,128]{1,0:T(8,128)}, s32[24,128]{1,0:T(8,128)S(1)}, u32[]{:S(2)}) copy-start(s32[24,128]{1,0:T(8,128)S(1)} %constant_dynamic-update-slice_fusion.near_ref) | copy-start | bytes 36868
  90.6 8.9 %collective-permute-start.7 = (s32[24,128]{1,0:T(8,128)S(1)}, s32[24,128]{1,0:T(8,128)S(1)}, u32[]{:S(2)}, u32[]{:S(2)}) collective-permute-start(s32[24,128]{1,0:T(8,128)S(1)} %constant_dynamic-update-slice_fusion.near_ref), channel_id=1, source_target_pairs={{0,40},{8,48},{16,56},{24,0},{32,8},{40,16},{48,24},{56,32},{1,41}... | collective-permute-start | bytes 36872 | tf_op jit(solution)/shard_map/ppermute | solution.py:179
  96.7 7.5 %collective-permute-start.6 = (s32[24,128]{1,0:T(8,128)S(1)}, s32[24,128]{1,0:T(8,128)S(1)}, u32[]{:S(2)}, u32[]{:S(2)}) collective-permute-start(s32[24,128]{1,0:T(8,128)S(1)} %constant_dynamic-update-slice_fusion.near_ref), channel_id=1, source_target_pairs={{0,24},{8,32},{16,40},{24,48},{32,56},{40,0},{48,8},{56,16},{1,25}... | collective-permute-start | bytes 36872 | tf_op jit(solution)/shard_map/ppermute | solution.py:179
  99.5 4.7 %copy-start.2 = (s32[24,128]{1,0:T(8,128)}, s32[24,128]{1,0:T(8,128)S(1)}, u32[]{:S(2)}) copy-start(s32[24,128]{1,0:T(8,128)S(1)} %collective-permute-done.7.above_ref) | copy-start | bytes 36868
  104.2 0.6 copy-start.3
  126.4 15.9 %copy-start.1 = (s32[8,1,128]{2,1,0:T(1,128)S(1)}, s32[8,1,128]{2,1,0:T(1,128)}, u32[]{:S(2)}) copy-start(s32[8,1,128]{2,1,0:T(1,128)} %all-gather.1.words_ref) | copy-start | bytes 12292
  126.4 70.5 %all-to-all-start = ((bf16[512,16,128]{2,1,0:T(8,128)(2,1)}), bf16[512,16,128]{2,1,0:T(8,128)(2,1)}, u32[]{:S(2)}, u32[]{:S(2)}) async-start(bf16[512,16,128]{2,1,0:T(8,128)(2,1)} %lookup.1), calls=%async_computation | async-start | bytes 4194304 | tf_op jit(solution)/shard_map/all_to_all | solution.py:233

commit v4 on v3

--- a/solution.py
+++ b/solution.py
@@ -5,7 +5,6 @@
 from jax import lax
 from jax.experimental import pallas as pl
 from jax.experimental.pallas import tpu as pltpu
-from jax.sharding import Mesh
 from jax.sharding import PartitionSpec as P
 
 LANES = 128
@@ -20,24 +19,28 @@
 
 def slots_kernel(cap, shard_ref, row_ref, ids_ref, slot_ref):
     tokens = shard_ref.shape[1]
-    words = ids_ref.shape[1]
+    owners = ids_ref.shape[0]
     shard = shard_ref[...]
     i = lax.broadcasted_iota(jnp.int32, (tokens, tokens), 0)
     j = lax.broadcasted_iota(jnp.int32, (tokens, tokens), 1)
     earlier = jnp.where((to_column(shard) == shard) & (i < j), 1, 0)
     slot = shard * cap + jnp.sum(earlier, axis=0, keepdims=True)
     slot_ref[...] = slot
-    target = 2 * lax.broadcasted_iota(jnp.int32, (tokens, words), 1)
-    place, name = to_column(slot), to_column(row_ref[...]) + 1
-    named = jnp.where(place == target, name, 0) + jnp.where(place == target + 1, name << 16, 0)
-    ids_ref[...] = jnp.sum(named, axis=0, keepdims=True)
+    first = cap * lax.broadcasted_iota(jnp.int32, (owners, tokens), 0)
+    lane = lax.broadcasted_iota(jnp.int32, (owners, LANES), 1)
+    name = row_ref[...] + 1
+    ids = jnp.zeros((owners, LANES), jnp.int32)
+    for w in range(cap // 2):
+        named = jnp.where(slot == first + 2 * w, name, 0) + jnp.where(slot == first + 2 * w + 1, name << 16, 0)
+        ids = jnp.where(lane == w, jnp.sum(named, axis=1, keepdims=True), ids)
+    ids_ref[...] = ids
 
 
 def slots(shard, row, owners, cap):
     return pl.pallas_call(
         functools.partial(slots_kernel, cap),
         out_shape=[
-            jax.ShapeDtypeStruct((1, owners * cap // 2), jnp.int32),
+            jax.ShapeDtypeStruct((owners, LANES), jnp.int32),
             jax.ShapeDtypeStruct(shard.shape, jnp.int32),
         ],
         name="slots",
@@ -96,31 +99,25 @@
     )(slot, cotangent)
 
 
-def pick_kernel(inner, here_ref, below_ref, near_ref, above_ref, out_ref):
-    outer_at, inner_at = here_ref[0], here_ref[1]
-    rows = jnp.concatenate([below_ref[inner:, :], near_ref[...], above_ref[...]], axis=0)
-    owners, lanes = rows.shape
-    each = lanes // owners
+def pick_kernel(ids_ref, out_ref):
+    ids = ids_ref[...]
+    owners, lanes = ids.shape
     lane = lax.broadcasted_iota(jnp.int32, (owners, lanes), 1)
     line = lax.broadcasted_iota(jnp.int32, (owners, lanes), 0)
-    far = lax.rem(outer_at + line // inner + owners // inner - 3, owners // inner)
-    close = lax.rem(inner_at + lax.rem(line, inner) + inner - 3, inner)
-    device = far * inner + close
     out = jnp.zeros((owners, lanes), jnp.int32)
-    for w in range(each):
-        mine = jnp.where(lane == (outer_at * inner + inner_at) * each + w, rows, 0)
-        out = out + jnp.where(lane == w * owners + device, jnp.sum(mine, axis=1, keepdims=True), 0)
+    for w in range(out_ref.shape[1] // owners):
+        word = jnp.sum(jnp.where(lane == w, ids, 0), axis=1, keepdims=True)
+        out = jnp.where(lane == w * owners + line, word, out)
     out_ref[...] = jnp.sum(out, axis=0, keepdims=True)
 
 
-def pick(here, below, near, above, inner):
-    return pl.pallas_call(
-        functools.partial(pick_kernel, inner),
-        in_specs=[pl.BlockSpec(memory_space=pltpu.SMEM)] + [pl.BlockSpec(memory_space=pltpu.VMEM)] * 3,
-        out_specs=pl.BlockSpec(memory_space=pltpu.VMEM),
-        out_shape=jax.ShapeDtypeStruct((1, near.shape[1]), jnp.int32),
+def pick(ids, cap):
+    owners = ids.shape[0]
+    return pl.pallas_call(
+        pick_kernel,
+        out_shape=jax.ShapeDtypeStruct((1, cap // 2 * owners), jnp.int32),
         name="pick",
-    )(here, below, near, above)
+    )(ids)
 
 
 def lookup_kernel(cap, words_ref, table_ref, out_ref, lines):
@@ -229,27 +226,24 @@
     )(slot, got)
 
 
-def exchange(x):
-    return lax.all_to_all(x, ("group", "outer", "inner"), split_axis=0, concat_axis=0, tiled=True)
+def exchange(x, axes):
+    return lax.all_to_all(x, axes, split_axis=0, concat_axis=0, tiled=True)
 
 
 def per_device(shard_ids, row_ids, table, cotangent):
     tokens, width = cotangent.shape
     groups = lax.axis_size("group")
-    owners = lax.axis_size("outer") * lax.axis_size("inner")
+    owners = lax.axis_size("vocab")
     cap = 2 * tokens // owners
     peers = groups * owners
     rows_here, columns = table.shape
     outgoing, slot = slots(shard_ids.reshape(1, tokens), row_ids.reshape(1, tokens), owners, cap)
-    below, near, above = neighbours(outgoing, "inner")
+    ids = exchange(outgoing.reshape(owners, 1, LANES), "vocab")
     packed = pack(slot, cotangent, groups, owners, cap)
-    line, packed = lax.optimization_barrier((jnp.concatenate([below[1:], near, above], axis=0), packed))
-    arrived = exchange(packed)
-    below, near, above = neighbours(line, "outer")
-    here = jnp.stack([lax.axis_index("outer"), lax.axis_index("inner")]).astype(jnp.int32)
-    mine = pick(here, below, near, above, lax.axis_size("inner"))
-    words = lax.all_gather(mine, "group", axis=0)
-    got = exchange(lookup(words, table, owners, cap))
+    ids, packed = lax.optimization_barrier((ids, packed))
+    arrived = exchange(packed, ("group", "vocab"))
+    words = lax.all_gather(pick(ids.reshape(owners, LANES), cap), "group", axis=0)
+    got = exchange(lookup(words, table, owners, cap), ("group", "vocab"))
     words = words.reshape(groups, cap // 2, owners)
     wanted = jnp.stack([words & 0xFFFF, words >> 16], axis=2).reshape(groups, cap, owners)
     wanted = jnp.swapaxes(wanted, 1, 2).reshape(-1) - 1
@@ -265,12 +259,13 @@
 
 
 def solution(mesh):
-    groups, owners = mesh.shape["group"], mesh.shape["vocab"]
-    inner = 8
-    grid = Mesh(mesh.devices.reshape(groups, owners // inner, inner), ("group", "outer", "inner"))
-    vocab = ("outer", "inner")
-    in_specs = (P(("group", *vocab), None), P(("group", *vocab)), P(vocab, "group"), P(("group", *vocab), None))
-    out_specs = (P(("group", *vocab), None), P(vocab, "group"))
+    in_specs = (
+        P(("group", "vocab"), None),
+        P(("group", "vocab")),
+        P("vocab", "group"),
+        P(("group", "vocab"), None),
+    )
+    out_specs = (P(("group", "vocab"), None), P("vocab", "group"))
     return jax.shard_map(
-        per_device, mesh=grid, in_specs=in_specs, out_specs=out_specs, check_vma=False
+        per_device, mesh=mesh, in_specs=in_specs, out_specs=out_specs, check_vma=False
     )

time: 202 us -> 169 us (0.84)
  starting transfers between devices: 67.1 us -> 39.9 us
  waiting for transfers between devices: 91 us -> 87.8 us
    ppermute x8 -> x0, waiting for transfers between devices: 44.8 us -> none  [shifted(): lax.ppermute(x, axis, [(i, (i - offset) % size) for i in range(size)])]
    all_to_all x2 -> x3, waiting for transfers between devices: 46.2 us -> 87.8 us  [exchange(): return lax.all_to_all(x, axes, split_axis=0, concat_axis=0, tiled=True)]
    ppermute x8 -> x0, starting transfers between devices: 35.7 us -> none  [shifted(): lax.ppermute(x, axis, [(i, (i - offset) % size) for i in range(size)])]
    all_to_all x2 -> x3, starting transfers between devices: 31.4 us -> 39.9 us  [exchange(): return lax.all_to_all(x, axes, split_axis=0, concat_axis=0, tiled=True)]
  transfers between devices with their start and end apart: 10 -> 3, of which waited for: 5 -> 3; matrix products, arithmetic and copies ran while one was open for 4% -> 5% of each run, Pallas kernels for 6% -> 7%
where the time goes in v4:
time: 169 us; the launch traced here: 168 us
  waiting for transfers between devices  87.8 us (52%)
  starting transfers between devices  39.9 us (24%)
  Pallas kernels  18.7 us (11%)
  blocking collectives  12.7 us (8%)
  matrix products  5.28 us (3%)
  local copies, waits for them, and re-layouts  3.07 us (2%)
    all_to_all x3, waiting for transfers between devices, exchange(): return lax.all_to_all(x, axes, split_axis=0, concat_axis=0, tiled=True)  87.8 us
    all_to_all x3, starting transfers between devices, exchange(): return lax.all_to_all(x, axes, split_axis=0, concat_axis=0, tiled=True)  39.9 us
    all_gather x1, blocking collectives, per_device(): lax.all_gather(pick(ids.reshape(owners, LANES), cap), 'group', axis=0)  12.7 us
    pallas_call x1, Pallas kernels, lookup(): pl.pallas_call(functools.partial(lookup_kernel, cap), grid=(groups // ste...  6.4 us
    dot_general x1, matrix products, per_device(): lax.dot_general(picker, arrived.reshape(peers * cap, columns), (((0,), (0...  5.28 us
    pallas_call x1, Pallas kernels, unpack(): pl.pallas_call(functools.partial(unpack_kernel, pieces), grid=(groups //...  4.7 us
    pallas_call x1, Pallas kernels, pack(): pl.pallas_call(functools.partial(pack_kernel, pieces, owners), grid=(grou...  4.65 us
  transfers between devices with their start and end apart: 3, of which 3 were waited for; matrix products, arithmetic and copies ran while one was open for 5% of the time, Pallas kernels for 7%

profile of v4, /device:TPU:1, one launch (start us, length us, event | category | flops | bytes accessed | tf_op | source)
XLA Modules:
  0.0 168.1 jit_solution(2157942423084090108)
XLA Ops:
  0.6 1.5 slots.1
  2.2 17.1 %all-to-all-start = ((s32[64,1,128]{2,1,0:T(1,128)}), s32[64,1,128]{2,1,0:T(1,128)S(1)}, u32[]{:S(2)}, u32[]{:S(2)}) async-start(s32[64,1,128]{2,1,0:T(1,128)} %bitcast.13), calls=%async_computation | async-start | bytes 65536 | tf_op jit(solution)/shard_map/all_to_all | solution.py:230
  19.3 4.7 %pack.1 = bf16[512,16,128]{2,1,0:T(8,128)(2,1)} custom-call(s32[1,128]{1,0:T(1,128)} %get-tuple-element.6.slot_ref, bf16[128,4096]{1,0:T(8,128)(2,1)} %cot_ref.1), custom_call_target="tpu_custom_call" | custom-call | flops 1073741824 | bytes 3145728 | tf_op jit(solution)/shard_map/pack/pallas_call | solution.py:83
  24.0 6.1 %all-to-all-done = s32[64,1,128]{2,1,0:T(1,128)S(1)} async-done(((s32[64,1,128]{2,1,0:T(1,128)}), s32[64,1,128]{2,1,0:T(1,128)S(1)}, u32[]{:S(2)}, u32[]{:S(2)}) %all-to-all-start) | async-done | bytes 32800 | tf_op jit(solution)/shard_map/all_to_all | solution.py:230
  30.1 0.0 copy-start
  30.1 11.6 %all-to-all-start.2 = ((bf16[512,16,128]{2,1,0:T(8,128)(2,1)}), bf16[512,16,128]{2,1,0:T(8,128)(2,1)S(1)}, u32[]{:S(2)}, u32[]{:S(2)}) async-start(bf16[512,16,128]{2,1,0:T(8,128)(2,1)} %pack.1), calls=%async_computation.2 | async-start | bytes 4194304 | tf_op jit(solution)/shard_map/all_to_all | solution.py:230
  41.7 0.0 copy-done
  41.7 1.4 pick.1
  43.1 12.7 %all-gather.1.words_ref = s32[8,1,128]{2,1,0:T(1,128)} all-gather(s32[1,1,128]{2,1,0:T(1,128)} %bitcast.14), channel_id=2, replica_groups=mesh['group'=8,'vocab'=64] {'group'}, dimensions={0}, use_global_device_ids=true | all-gather | bytes 4608 | tf_op jit(solution)/shard_map/all_gather | solution.py:245
  55.8 6.4 %lookup.1 = bf16[512,16,128]{2,1,0:T(8,128)(2,1)} custom-call(s32[8,1,128]{2,1,0:T(1,128)} %all-gather.1.words_ref, bf16[1002,512]{1,0:T(8,128)(2,1)} %table_ref.1), custom_call_target="tpu_custom_call" | custom-call | flops 2101346304 | bytes 3123200 | tf_op jit(solution)/shard_map/lookup/pallas_call | solution.py:155
  62.2 0.0 copy-start.1
  62.2 36.1 %all-to-all-done.2 = bf16[512,16,128]{2,1,0:T(8,128)(2,1)S(1)} async-done(((bf16[512,16,128]{2,1,0:T(8,128)(2,1)}), bf16[512,16,128]{2,1,0:T(8,128)(2,1)S(1)}, u32[]{:S(2)}, u32[]{:S(2)}) %all-to-all-start.2) | async-done | bytes 2097184 | tf_op jit(solution)/shard_map/all_to_all | solution.py:230
  98.3 11.1 %all-to-all-start.1 = ((bf16[512,16,128]{2,1,0:T(8,128)(2,1)}), bf16[512,16,128]{2,1,0:T(8,128)(2,1)}, u32[]{:S(2)}, u32[]{:S(2)}) async-start(bf16[512,16,128]{2,1,0:T(8,128)(2,1)} %lookup.1), calls=%async_computation.1 | async-start | bytes 4194304 | tf_op jit(solution)/shard_map/all_to_all | solution.py:230
  109.4 0.0 copy-done.1
  109.4 0.1 and.18
  109.5 0.1 shift_right_arithmetic.18
  109.6 0.2 copy.17
  109.8 0.2 sub.13
  109.9 2.6 %reshape.59 = bf16[2048,512]{1,0:T(8,128)(2,1)} reshape(bf16[512,16,128]{2,1,0:T(8,128)(2,1)S(1)} %all-to-all-done.2) | data formatting | bytes 4194304 | tf_op jit(solution)/shard_map/reshape | solution.py:253
  112.5 5.3 %fusion.2 = bf16[1002,512]{1,0:T(8,128)(2,1)} fusion(bf16[2048,512]{1,0:T(8,128)(2,1)} %reshape.59, s32[2048]{0:T(1024)S(1)} %sub.13), kind=kOutput, calls=%fused_computation.3 | convolution fusion | flops 2103911424 | bytes 3131392 | tf_op jit(solution)/shard_map/dot_general | solution.py:251
  117.8 45.6 %all-to-all-done.1.got_ref = bf16[512,16,128]{2,1,0:T(8,128)(2,1)} async-done(((bf16[512,16,128]{2,1,0:T(8,128)(2,1)}), bf16[512,16,128]{2,1,0:T(8,128)(2,1)}, u32[]{:S(2)}, u32[]{:S(2)}) %all-to-all-start.1) | async-done | bytes 2097184 | tf_op jit(solution)/shard_map/all_to_all | solution.py:230
  163.4 4.7 %unpack.1 = bf16[128,4096]{1,0:T(8,128)(2,1)} custom-call(s32[1,128]{1,0:T(1,128)} %get-tuple-element.6.slot_ref, bf16[512,16,128]{2,1,0:T(8,128)(2,1)} %all-to-all-done.1.got_ref), custom_call_target="tpu_custom_call" | custom-call | tf_op jit(solution)/shard_map/unpack/pallas_call | solution.py:215
  (4 shorter events, 0.0 us)
Async XLA Ops:
  2.2 27.9 %all-to-all-start = ((s32[64,1,128]{2,1,0:T(1,128)}), s32[64,1,128]{2,1,0:T(1,128)S(1)}, u32[]{:S(2)}, u32[]{:S(2)}) async-start(s32[64,1,128]{2,1,0:T(1,128)} %bitcast.13), calls=%async_computation | async-start | bytes 65536 | tf_op jit(solution)/shard_map/all_to_all | solution.py:230
  30.1 11.6 %copy-start = (s32[64,1,128]{2,1,0:T(1,128)}, s32[64,1,128]{2,1,0:T(1,128)S(1)}, u32[]{:S(2)}) copy-start(s32[64,1,128]{2,1,0:T(1,128)S(1)} %all-to-all-done) | copy-start | bytes 98308
  30.1 68.2 %all-to-all-start.2 = ((bf16[512,16,128]{2,1,0:T(8,128)(2,1)}), bf16[512,16,128]{2,1,0:T(8,128)(2,1)S(1)}, u32[]{:S(2)}, u32[]{:S(2)}) async-start(bf16[512,16,128]{2,1,0:T(8,128)(2,1)} %pack.1), calls=%async_computation.2 | async-start | bytes 4194304 | tf_op jit(solution)/shard_map/all_to_all | solution.py:230
  62.2 47.2 %copy-start.1 = (s32[8,1,128]{2,1,0:T(1,128)S(1)}, s32[8,1,128]{2,1,0:T(1,128)}, u32[]{:S(2)}) copy-start(s32[8,1,128]{2,1,0:T(1,128)} %all-gather.1.words_ref) | copy-start | bytes 12292
  98.3 65.1 %all-to-all-start.1 = ((bf16[512,16,128]{2,1,0:T(8,128)(2,1)}), bf16[512,16,128]{2,1,0:T(8,128)(2,1)}, u32[]{:S(2)}, u32[]{:S(2)}) async-start(bf16[512,16,128]{2,1,0:T(8,128)(2,1)} %lookup.1), calls=%async_computation.1 | async-start | bytes 4194304 | tf_op jit(solution)/shard_map/all_to_all | solution.py:230

commit v5 on v0

v5 whole, which is shorter than its diff:
```python
import functools

import jax
import jax.numpy as jnp
from jax import lax
from jax.experimental import pallas as pl
from jax.experimental.pallas import tpu as pltpu
from jax.sharding import PartitionSpec as P

LANES = 128
EXTRA = 8
VMEM = pl.BlockSpec(memory_space=pltpu.VMEM)
SMEM = pl.BlockSpec(memory_space=pltpu.SMEM)


def to_column(row):
    n = row.shape[1]
    here = lax.broadcasted_iota(jnp.int32, (n, n), 0)
    there = lax.broadcasted_iota(jnp.int32, (n, n), 1)
    return jnp.sum(jnp.where(here == there, row, 0), axis=1, keepdims=True)


def slots_kernel(cap, shard_ref, row_ref, ids_ref, slot_ref):
    tokens = shard_ref.shape[1]
    groups, owners, _ = ids_ref.shape
    shard = shard_ref[...]
    i = lax.broadcasted_iota(jnp.int32, (tokens, tokens), 0)
    j = lax.broadcasted_iota(jnp.int32, (tokens, tokens), 1)
    earlier = jnp.where((to_column(shard) == shard) & (i < j), 1, 0)
    slot = shard * cap + jnp.sum(earlier, axis=0, keepdims=True)
    slot_ref[...] = slot
    first = cap * lax.broadcasted_iota(jnp.int32, (owners, tokens), 0)
    lane = lax.broadcasted_iota(jnp.int32, (owners, LANES), 1)
    name = row_ref[...] + 1
    ids = jnp.zeros((owners, LANES), jnp.int32)
    for w in range(cap // 2):
        named = jnp.where(slot == first + 2 * w, name, 0) + jnp.where(slot == first + 2 * w + 1, name << 16, 0)
        ids = jnp.where(lane == w, jnp.sum(named, axis=1, keepdims=True), ids)
    for g in range(groups):
        ids_ref[g] = ids


def slots(shard, row, groups, owners, cap):
    return pl.pallas_call(
        functools.partial(slots_kernel, cap),
        out_shape=[
            jax.ShapeDtypeStruct((groups, owners, LANES), jnp.int32),
            jax.ShapeDtypeStruct(shard.shape, jnp.int32),
        ],
        name="slots",
    )(shard, row)


def lookup_kernel(cap, me_ref, ids_ref, table_ref, out_ref, lines_ref):
    groups, owners, _ = ids_ref.shape
    rows = table_ref.shape[0]
    lane = lax.broadcasted_iota(jnp.int32, (owners, LANES), 1)
    for d in range(groups):
        ids = ids_ref[lax.rem(me_ref[0] + groups - d, groups)]
        for w in range(cap // 2):
            word = jnp.sum(jnp.where(lane == w, ids, 0), axis=1, keepdims=True)
            word = jnp.broadcast_to(word, (owners, LANES))
            at = d * cap + 2 * w
            lines_ref[pl.ds(at, owners, stride=groups * cap), :] = word & 0xFFFF
            lines_ref[pl.ds(at + 1, owners, stride=groups * cap), :] = word >> 16
    chunk = 256
    row = lax.broadcasted_iota(jnp.int32, (chunk, rows), 1) + 1
    for m in range(0, out_ref.shape[0], chunk):
        hot = jnp.where(lines_ref[m : m + chunk, :1] == row, 1.0, 0.0).astype(jnp.bfloat16)
        found = jnp.dot(hot, table_ref[...], preferred_element_type=jnp.float32)
        out_ref[m : m + chunk] = found.astype(jnp.bfloat16)


def lookup(me, ids, table, cap):
    groups, owners, _ = ids.shape
    count = groups * owners * cap
    return pl.pallas_call(
        functools.partial(lookup_kernel, cap),
        in_specs=[SMEM, VMEM, VMEM],
        out_specs=[VMEM, VMEM],
        out_shape=[
            jax.ShapeDtypeStruct((count, table.shape[1]), jnp.bfloat16),
            jax.ShapeDtypeStruct((count, LANES), jnp.int32),
        ],
        name="lookup",
    )(me, ids, table)


def cut_kernel(me_ref, slot_ref, cot_ref, *out_refs):
    groups = len(out_refs)
    tokens, width = cot_ref.shape
    columns = width // groups
    slot = jnp.broadcast_to(slot_ref[...].astype(jnp.float32), (EXTRA, tokens)).astype(jnp.bfloat16)
    for d, out_ref in enumerate(out_refs):
        at = pl.multiple_of(lax.rem(me_ref[0] + d, groups) * columns, columns)
        out_ref[:tokens, :] = cot_ref[:, pl.ds(at, columns)]
        out_ref[tokens:, :] = jnp.concatenate([slot] * (columns // tokens), axis=1)


def cut(me, slot, cotangent, groups):
    tokens, width = cotangent.shape
    piece = jax.ShapeDtypeStruct((tokens + EXTRA, width // groups), jnp.bfloat16)
    return pl.pallas_call(
        cut_kernel,
        in_specs=[SMEM, VMEM, VMEM],
        out_specs=[VMEM] * groups,
        out_shape=[piece] * groups,
        name="cut",
    )(me, slot, cotangent)


def target_line(slot, cap, part, parts):
    return lax.div(slot, cap) * (parts * cap) + part * cap + lax.rem(slot, cap)


def slots_of(piece_ref):
    tokens = piece_ref.shape[0] - EXTRA
    return piece_ref[tokens:, :tokens].astype(jnp.float32)[:1].astype(jnp.int32)


def pack_kernel(cap, *refs):
    piece_refs, out_ref = refs[:-1], refs[-1]
    groups = len(piece_refs)
    owners = out_ref.shape[0]
    tokens = piece_refs[0].shape[0] - EXTRA
    columns = out_ref.shape[2]
    parts = groups // 2
    line = lax.broadcasted_iota(jnp.int32, (owners * parts * cap, tokens), 0)
    for half in range(2):
        group = piece_refs[half * parts : (half + 1) * parts]
        hot = jnp.concatenate(
            [
                jnp.where(line == target_line(slots_of(ref), cap, part, parts), 1.0, 0.0).astype(jnp.bfloat16)
                for part, ref in enumerate(group)
            ],
            axis=1,
        )
        right = jnp.concatenate([ref[:tokens, :] for ref in group], axis=0)
        placed = jnp.dot(hot, right, preferred_element_type=jnp.float32).astype(jnp.bfloat16)
        out_ref[:, half * parts * cap : (half + 1) * parts * cap, :] = placed.reshape(owners, parts * cap, columns)


def pack(pieces, owners, cap):
    groups = len(pieces)
    return pl.pallas_call(
        functools.partial(pack_kernel, cap),
        in_specs=[VMEM] * groups,
        out_specs=VMEM,
        out_shape=jax.ShapeDtypeStruct((owners, groups * cap, pieces[0].shape[1]), jnp.bfloat16),
        name="pack",
    )(*pieces)


def unpack_kernel(cap, groups, *refs):
    piece_refs, got_ref, out_refs = refs[:groups], refs[groups], refs[groups + 1 :]
    owners, _, columns = got_ref.shape
    tokens = out_refs[0].shape[0]
    parts = groups // 2
    line = lax.broadcasted_iota(jnp.int32, (tokens, owners * parts * cap), 1)
    for half in range(2):
        group = piece_refs[half * parts : (half + 1) * parts]
        hot = jnp.concatenate(
            [
                jnp.where(
                    line == to_column(target_line(slots_of(ref), cap, part, parts)), 1.0, 0.0
                ).astype(jnp.bfloat16)
                for part, ref in enumerate(group)
            ],
            axis=0,
        )
        right = got_ref[:, half * parts * cap : (half + 1) * parts * cap, :].reshape(-1, columns)
        picked = jnp.dot(hot, right, preferred_element_type=jnp.float32).astype(jnp.bfloat16)
        for part in range(parts):
            out_refs[half * parts + part][...] = picked[part * tokens : (part + 1) * tokens]


def unpack(pieces, got, cap):
    groups = len(pieces)
    tokens = pieces[0].shape[0] - EXTRA
    return pl.pallas_call(
        functools.partial(unpack_kernel, cap, groups),
        in_specs=[VMEM] * (groups + 1),
        out_specs=[VMEM] * groups,
        out_shape=[jax.ShapeDtypeStruct((tokens, got.shape[2]), jnp.bfloat16)] * groups,
        name="unpack",
    )(*pieces, got)


def join_kernel(me_ref, *refs):
    out_ref = refs[-1]
    groups = len(refs) - 1
    for d, ref in enumerate(refs[:-1]):
        columns = ref.shape[1]
        at = pl.multiple_of(lax.rem(me_ref[0] + d, groups) * columns, columns)
        out_ref[:, pl.ds(at, columns)] = ref[...]


def join(me, pieces):
    tokens, columns = pieces[0].shape
    return pl.pallas_call(
        join_kernel,
        in_specs=[SMEM] + [VMEM] * len(pieces),
        out_specs=VMEM,
        out_shape=jax.ShapeDtypeStruct((tokens, columns * len(pieces)), jnp.bfloat16),
        name="join",
    )(me, *pieces)


def exchange(x, axes):
    return lax.all_to_all(x, axes, split_axis=0, concat_axis=0, tiled=True)


def pass_on(pieces, sign):
    size = len(pieces)
    moved = [lax.ppermute(pieces[d], "group", [(i, (i + sign * d) % size) for i in range(size)]) for d in range(1, size)]
    return [pieces[0], *moved]


def per_device(shard_ids, row_ids, table, cotangent):
    tokens, width = cotangent.shape
    groups = lax.axis_size("group")
    owners = lax.axis_size("vocab")
    cap = 2 * tokens // owners
    rows_here, columns = table.shape
    me = lax.axis_index("group").astype(jnp.int32).reshape(1)
    ids, slot = slots(shard_ids.reshape(1, tokens), row_ids.reshape(1, tokens), groups, owners, cap)
    ids = exchange(ids.reshape(groups * owners, 1, LANES), ("group", "vocab"))
    pieces = cut(me, slot, cotangent, groups)
    found, lines = lookup(me, ids.reshape(groups, owners, LANES), table, cap)
    found, pieces = lax.optimization_barrier((found, pieces))
    got = exchange(found.reshape(owners, groups * cap, columns), "vocab")
    pieces = pass_on(pieces, 1)
    packed = pack(pieces, owners, cap)
    got, packed = lax.optimization_barrier((got, packed))
    arrived = exchange(packed, "vocab")
    embeds = join(me, pass_on(unpack(pieces, got, cap), -1))
    wanted = lines[:, 0] - 1
    picker = (wanted[:, None] == jnp.arange(rows_here, dtype=jnp.int32)[None, :]).astype(jnp.bfloat16)
    table_grad = lax.dot_general(
        picker, arrived.reshape(-1, columns), (((0,), (0,)), ((), ())), preferred_element_type=jnp.float32
    )
    return (embeds, table_grad.astype(jnp.bfloat16))


def solution(mesh):
    in_specs = (
        P(("group", "vocab"), None),
        P(("group", "vocab")),
        P("vocab", "group"),
        P(("group", "vocab"), None),
    )
    out_specs = (P(("group", "vocab"), None), P("vocab", "group"))
    return jax.shard_map(
        per_device, mesh=mesh, in_specs=in_specs, out_specs=out_specs, check_vma=False
    )
```

time: 187 us -> 178 us (0.952)
  the two profiles are of different devices: /device:TPU:1 before, /device:TPU:28 now
where the time goes in v5:
time: 178 us; the launch traced here: 177 us
  waiting for transfers between devices  73.7 us (41%)
  starting transfers between devices  72.9 us (41%)
  Pallas kernels  20.5 us (12%)
  matrix products  5.27 us (3%)
  local copies, waits for them, and re-layouts  3.58 us (2%)
    all_to_all x3, waiting for transfers between devices, exchange(): return lax.all_to_all(x, axes, split_axis=0, concat_axis=0, tiled=True)  63 us
    all_to_all x3, starting transfers between devices, exchange(): return lax.all_to_all(x, axes, split_axis=0, concat_axis=0, tiled=True)  39.1 us
    ppermute x14, starting transfers between devices, pass_on(): lax.ppermute(pieces[d], 'group', [(i, (i + sign * d) % size) for i in ran...  33.9 us
    ppermute x14, waiting for transfers between devices, pass_on(): lax.ppermute(pieces[d], 'group', [(i, (i + sign * d) % size) for i in ran...  10.7 us
    pallas_call x1, Pallas kernels, lookup(): pl.pallas_call(functools.partial(lookup_kernel, cap), in_specs=[SMEM, VME...  5.85 us
    dot_general x1, matrix products, per_device(): lax.dot_general(picker, arrived.reshape(-1, columns), (((0,), (0,)), ((),...  5.27 us
    pallas_call x1, Pallas kernels, unpack(): pl.pallas_call(functools.partial(unpack_kernel, cap, groups), in_specs=[V...  4.45 us
    pallas_call x1, Pallas kernels, pack(): pl.pallas_call(functools.partial(pack_kernel, cap), in_specs=[VMEM] * gro...  3.92 us
  transfers between devices with their start and end apart: 17, of which 9 were waited for; matrix products, arithmetic and copies ran while one was open for 0% of the time, Pallas kernels for 7%

profile of v5, /device:TPU:28, one launch (start us, length us, event | category | flops | bytes accessed | tf_op | source)
XLA Modules:
  0.0 177.3 jit_solution(8008945852411173880)
XLA Ops:
  0.6 1.6 slots.1
  2.3 20.9 %all-to-all-start = ((s32[512,1,128]{2,1,0:T(1,128)}), s32[512,1,128]{2,1,0:T(1,128)S(1)}, u32[]{:S(2)}, u32[]{:S(2)}) async-start(s32[512,1,128]{2,1,0:T(1,128)} %bitcast.12), calls=%async_computation | async-start | bytes 524288 | tf_op jit(solution)/shard_map/all_to_all | solution.py:210
  23.2 2.4 %cut.1 = (bf16[136,512]{1,0:T(8,128)(2,1)}, bf16[136,512]{1,0:T(8,128)(2,1)}, bf16[136,512]{1,0:T(8,128)(2,1)}, bf16[136,512]{1,0:T(8,128)(2,1)}, bf16[136,512]{...) custom-call(s32[1]{0:T(128)} %bitcast.me_ref, ...), custom_call_target="tpu_custom_call" | custom-call | tf_op jit(solution)/shard_map/cut/pallas_call | solution.py:103
  25.5 10.6 %all-to-all-done = s32[512,1,128]{2,1,0:T(1,128)S(1)} async-done(((s32[512,1,128]{2,1,0:T(1,128)}), s32[512,1,128]{2,1,0:T(1,128)S(1)}, u32[]{:S(2)}, u32[]{:S(2)}) %all-to-all-start) | async-done | bytes 262176 | tf_op jit(solution)/shard_map/all_to_all | solution.py:210
  36.2 0.7 copy-done.2
  36.9 5.8 %lookup.1 = (bf16[2048,512]{1,0:T(8,128)(2,1)}, s32[2048,128]{1,0:T(8,128)}) custom-call(s32[1]{0:T(128)} %bitcast.me_ref, s32[8,64,128]{2,1,0:T(8,128)} %bitcast.11, bf16[1002,512]{1,0:T(8,128)(2,1)} %table_ref.1), custom_call_target="tpu_custom_call" | custom-call | tf_op jit(solution)/shard_map/lookup/pallas_call | solution.py:77
  42.8 7.5 %all-to-all-start.1 = ((bf16[64,32,512]{2,1,0:T(8,128)(2,1)}), bf16[64,32,512]{2,1,0:T(8,128)(2,1)S(1)}, u32[]{:S(2)}, u32[]{:S(2)}) async-start(bf16[64,32,512]{2,1,0:T(8,128)(2,1)} %bitcast.10), calls=%async_computation.1 | async-start | bytes 4194304 | tf_op jit(solution)/shard_map/all_to_all | solution.py:210
  50.3 3.4 %collective-permute-start.1 = (bf16[136,512]{1,0:T(8,128)(2,1)S(1)}, bf16[136,512]{1,0:T(8,128)(2,1)S(1)}, u32[]{:S(2)}, u32[]{:S(2)}) collective-permute-start(bf16[136,512]{1,0:T(8,128)(2,1)S(1)} %copy-done.20), channel_id=1, source_target_pairs={{0,128},{64,192},{128,256},{192,320},{256,384},{320,448},{384,0},{... | collective-permute-start | bytes 417800 | tf_op jit(solution)/shard_map/ppermute | solution.py:215
  53.8 4.0 %collective-permute-start.2 = (bf16[136,512]{1,0:T(8,128)(2,1)}, bf16[136,512]{1,0:T(8,128)(2,1)S(1)}, u32[]{:S(2)}, u32[]{:S(2)}) collective-permute-start(bf16[136,512]{1,0:T(8,128)(2,1)} %get-tuple-element.47), channel_id=1, source_target_pairs={{0,192},{64,256},{128,320},{192,384},{256,448},{320,0},{384,64},{4... | collective-permute-start | bytes 417800 | tf_op jit(solution)/shard_map/ppermute | solution.py:215
  57.8 2.7 %collective-permute-start.3 = (bf16[136,512]{1,0:T(8,128)(2,1)}, bf16[136,512]{1,0:T(8,128)(2,1)S(1)}, u32[]{:S(2)}, u32[]{:S(2)}) collective-permute-start(bf16[136,512]{1,0:T(8,128)(2,1)} %get-tuple-element.48), channel_id=1, source_target_pairs={{0,256},{64,320},{128,384},{192,448},{256,0},{320,64},{384,128},{4... | collective-permute-start | bytes 417800 | tf_op jit(solution)/shard_map/ppermute | solution.py:215
  60.5 3.8 %collective-permute-start.4 = (bf16[136,512]{1,0:T(8,128)(2,1)S(1)}, bf16[136,512]{1,0:T(8,128)(2,1)S(1)}, u32[]{:S(2)}, u32[]{:S(2)}) collective-permute-start(bf16[136,512]{1,0:T(8,128)(2,1)S(1)} %copy-done.19), channel_id=1, source_target_pairs={{0,320},{64,384},{128,448},{192,0},{256,64},{320,128},{384,192},{4... | collective-permute-start | bytes 417800 | tf_op jit(solution)/shard_map/ppermute | solution.py:215
  64.3 3.7 %collective-permute-start.5 = (bf16[136,512]{1,0:T(8,128)(2,1)S(1)}, bf16[136,512]{1,0:T(8,128)(2,1)S(1)}, u32[]{:S(2)}, u32[]{:S(2)}) collective-permute-start(bf16[136,512]{1,0:T(8,128)(2,1)S(1)} %copy-done.18), channel_id=1, source_target_pairs={{0,384},{64,448},{128,0},{192,64},{256,128},{320,192},{384,256},{4... | collective-permute-start | bytes 417800 | tf_op jit(solution)/shard_map/ppermute | solution.py:215
  68.0 1.2 collective-permute-start.6
  69.3 3.8 %collective-permute-done.5.refs_6_ = bf16[136,512]{1,0:T(8,128)(2,1)S(1)} collective-permute-done((bf16[136,512]{1,0:T(8,128)(2,1)S(1)}, bf16[136,512]{1,0:T(8,128)(2,1)S(1)}, u32[]{:S(2)}, u32[]{:S(2)}) %collective-permute-start.5) | collective-permute-done | bytes 139296 | tf_op jit(solution)/shard_map/ppermute | solution.py:215
  73.7 0.7 copy-done.9
  74.3 3.9 %pack.1 = bf16[64,32,512]{2,1,0:T(8,128)(2,1)} custom-call(bf16[136,512]{1,0:T(8,128)(2,1)} %get-tuple-element.44.refs_0_, bf16[136,512]{1,0:T(8,128)(2,1)} %copy-done.3, bf16[136,512]{1,0:T(8,128)(2,1)} %copy-done.4, bf16[136,512]{1,0:T(8,128)(2,1)} %copy-done.5, bf16[136,512]{1,0:T(8,128)(2,1)} %copy-done.6, bf16[136,512]{1,0:T(8,128)(2,1)} %copy-done.7, ...), custom_call_target="tpu_custom_call" | custom-call | tf_op jit(solution)/shard_map/pack/pallas_call | solution.py:145
  78.3 27.6 %all-to-all-done.1.refs_8_ = bf16[64,32,512]{2,1,0:T(8,128)(2,1)S(1)} async-done(((bf16[64,32,512]{2,1,0:T(8,128)(2,1)}), bf16[64,32,512]{2,1,0:T(8,128)(2,1)S(1)}, u32[]{:S(2)}, u32[]{:S(2)}) %all-to-all-start.1) | async-done | bytes 2097184 | tf_op jit(solution)/shard_map/all_to_all | solution.py:210
  105.8 1.4 copy-done
  107.2 10.6 %all-to-all-start.2 = ((bf16[64,32,512]{2,1,0:T(8,128)(2,1)}), bf16[64,32,512]{2,1,0:T(8,128)(2,1)}, u32[]{:S(2)}, u32[]{:S(2)}) async-start(bf16[64,32,512]{2,1,0:T(8,128)(2,1)} %pack.1), calls=%async_computation.2 | async-start | bytes 4194304 | tf_op jit(solution)/shard_map/all_to_all | solution.py:210
  117.9 4.4 %unpack.1 = (bf16[128,512]{1,0:T(8,128)(2,1)}, bf16[128,512]{1,0:T(8,128)(2,1)}, bf16[128,512]{1,0:T(8,128)(2,1)}, bf16[128,512]{1,0:T(8,128)(2,1)}, bf16[128,51...) custom-call(bf16[136,512]{1,0:T(8,128)(2,1)} %get-tuple-element.44.refs_0_, ...), custom_call_target="tpu_custom_call" | custom-call | tf_op jit(solution)/shard_map/unpack/pallas_call | solution.py:180
  122.3 1.9 %collective-permute-start.8 = (bf16[128,512]{1,0:T(8,128)(2,1)}, bf16[128,512]{1,0:T(8,128)(2,1)S(1)}, u32[]{:S(2)}, u32[]{:S(2)}) collective-permute-start(bf16[128,512]{1,0:T(8,128)(2,1)} %get-tuple-element.56), channel_id=1, source_target_pairs={{0,384},{64,448},{128,0},{192,64},{256,128},{320,192},{384,256},{4... | collective-permute-start | bytes 393224 | tf_op jit(solution)/shard_map/ppermute | solution.py:215
  124.2 2.1 %collective-permute-start.9 = (bf16[128,512]{1,0:T(8,128)(2,1)}, bf16[128,512]{1,0:T(8,128)(2,1)S(1)}, u32[]{:S(2)}, u32[]{:S(2)}) collective-permute-start(bf16[128,512]{1,0:T(8,128)(2,1)} %get-tuple-element.57), channel_id=1, source_target_pairs={{0,320},{64,384},{128,448},{192,0},{256,64},{320,128},{384,192},{4... | collective-permute-start | bytes 393224 | tf_op jit(solution)/shard_map/ppermute | solution.py:215
  126.3 5.4 %collective-permute-start.10 = (bf16[128,512]{1,0:T(8,128)(2,1)}, bf16[128,512]{1,0:T(8,128)(2,1)S(1)}, u32[]{:S(2)}, u32[]{:S(2)}) collective-permute-start(bf16[128,512]{1,0:T(8,128)(2,1)} %get-tuple-element.58), channel_id=1, source_target_pairs={{0,256},{64,320},{128,384},{192,448},{256,0},{320,64},{384,128},{4... | collective-permute-start | bytes 393224 | tf_op jit(solution)/shard_map/ppermute | solution.py:215
  131.7 2.3 %collective-permute-start.11 = (bf16[128,512]{1,0:T(8,128)(2,1)}, bf16[128,512]{1,0:T(8,128)(2,1)S(1)}, u32[]{:S(2)}, u32[]{:S(2)}) collective-permute-start(bf16[128,512]{1,0:T(8,128)(2,1)} %get-tuple-element.59), channel_id=1, source_target_pairs={{0,192},{64,256},{128,320},{192,384},{256,448},{320,0},{384,64},{4... | collective-permute-start | bytes 393224 | tf_op jit(solution)/shard_map/ppermute | solution.py:215
  134.0 3.5 %collective-permute-start.12 = (bf16[128,512]{1,0:T(8,128)(2,1)}, bf16[128,512]{1,0:T(8,128)(2,1)S(1)}, u32[]{:S(2)}, u32[]{:S(2)}) collective-permute-start(bf16[128,512]{1,0:T(8,128)(2,1)} %get-tuple-element.60), channel_id=1, source_target_pairs={{0,128},{64,192},{128,256},{192,320},{256,384},{320,448},{384,0},{... | collective-permute-start | bytes 393224 | tf_op jit(solution)/shard_map/ppermute | solution.py:215
  137.9 1.9 %collective-permute-done.11.refs_5_ = bf16[128,512]{1,0:T(8,128)(2,1)S(1)} collective-permute-done((bf16[128,512]{1,0:T(8,128)(2,1)}, bf16[128,512]{1,0:T(8,128)(2,1)S(1)}, u32[]{:S(2)}, u32[]{:S(2)}) %collective-permute-start.11) | collective-permute-done | bytes 131104 | tf_op jit(solution)/shard_map/ppermute | solution.py:215
  139.8 3.1 %collective-permute-done.12.refs_6_ = bf16[128,512]{1,0:T(8,128)(2,1)S(1)} collective-permute-done((bf16[128,512]{1,0:T(8,128)(2,1)}, bf16[128,512]{1,0:T(8,128)(2,1)S(1)}, u32[]{:S(2)}, u32[]{:S(2)}) %collective-permute-start.12) | collective-permute-done | bytes 131104 | tf_op jit(solution)/shard_map/ppermute | solution.py:215
  143.0 1.3 collective-permute-done.13.refs_7_
  144.3 0.6 copy-done.16
  144.9 2.3 %join.1 = bf16[128,4096]{1,0:T(8,128)(2,1)} custom-call(s32[1]{0:T(128)} %bitcast.me_ref, bf16[128,512]{1,0:T(8,128)(2,1)} %get-tuple-element.54.refs_0_, bf16[128,512]{1,0:T(8,128)(2,1)} %copy-done.10, bf16[128,512]{1,0:T(8,128)(2,1)} %copy-done.11, bf16[128,512]{1,0:T(8,128)(2,1)} %copy-done.12, bf16[128,512]{1,0:T(8,128)(2,1)} %copy-done.13, ...), custom_call_target="tpu_custom_call" | custom-call | tf_op jit(solution)/shard_map/join/pallas_call | solution.py:200
  147.3 24.8 %all-to-all-done.2 = bf16[64,32,512]{2,1,0:T(8,128)(2,1)} async-done(((bf16[64,32,512]{2,1,0:T(8,128)(2,1)}), bf16[64,32,512]{2,1,0:T(8,128)(2,1)}, u32[]{:S(2)}, u32[]{:S(2)}) %all-to-all-start.2) | async-done | bytes 2097184 | tf_op jit(solution)/shard_map/all_to_all | solution.py:210
  172.0 5.3 %fusion.2 = bf16[1002,512]{1,0:T(8,128)(2,1)} fusion(bf16[2048,512]{1,0:T(8,128)(2,1)} %bitcast.7, s32[2048]{0:T(1024)S(1)} %add_reduce_fusion), kind=kOutput, calls=%fused_computation.3 | convolution fusion | flops 2103911424 | bytes 3131392 | tf_op jit(solution)/shard_map/dot_general | solution.py:239
  (54 shorter events, 1.2 us)
Async XLA Ops:
  2.3 33.9 %all-to-all-start = ((s32[512,1,128]{2,1,0:T(1,128)}), s32[512,1,128]{2,1,0:T(1,128)S(1)}, u32[]{:S(2)}, u32[]{:S(2)}) async-start(s32[512,1,128]{2,1,0:T(1,128)} %bitcast.12), calls=%async_computation | async-start | bytes 524288 | tf_op jit(solution)/shard_map/all_to_all | solution.py:210
  42.7 7.6 %copy-start.21 = (bf16[136,512]{1,0:T(8,128)(2,1)S(1)}, bf16[136,512]{1,0:T(8,128)(2,1)}, u32[]{:S(2)}) copy-start(bf16[136,512]{1,0:T(8,128)(2,1)} %get-tuple-element.45) | copy-start | bytes 417796
  42.7 7.6 %copy-start.20 = (bf16[136,512]{1,0:T(8,128)(2,1)S(1)}, bf16[136,512]{1,0:T(8,128)(2,1)}, u32[]{:S(2)}) copy-start(bf16[136,512]{1,0:T(8,128)(2,1)} %get-tuple-element.46) | copy-start | bytes 417796
  42.7 17.8 %copy-start.19 = (bf16[136,512]{1,0:T(8,128)(2,1)S(1)}, bf16[136,512]{1,0:T(8,128)(2,1)}, u32[]{:S(2)}) copy-start(bf16[136,512]{1,0:T(8,128)(2,1)} %get-tuple-element.49) | copy-start | bytes 417796
  42.7 21.6 %copy-start.18 = (bf16[136,512]{1,0:T(8,128)(2,1)S(1)}, bf16[136,512]{1,0:T(8,128)(2,1)}, u32[]{:S(2)}) copy-start(bf16[136,512]{1,0:T(8,128)(2,1)} %get-tuple-element.50) | copy-start | bytes 417796
  42.7 25.3 %copy-start.17 = (bf16[136,512]{1,0:T(8,128)(2,1)S(1)}, bf16[136,512]{1,0:T(8,128)(2,1)}, u32[]{:S(2)}) copy-start(bf16[136,512]{1,0:T(8,128)(2,1)} %get-tuple-element.51) | copy-start | bytes 417796
  42.8 63.1 %all-to-all-start.1 = ((bf16[64,32,512]{2,1,0:T(8,128)(2,1)}), bf16[64,32,512]{2,1,0:T(8,128)(2,1)S(1)}, u32[]{:S(2)}, u32[]{:S(2)}) async-start(bf16[64,32,512]{2,1,0:T(8,128)(2,1)} %bitcast.10), calls=%async_computation.1 | async-start | bytes 4194304 | tf_op jit(solution)/shard_map/all_to_all | solution.py:210
  50.3 14.0 %collective-permute-start = (bf16[136,512]{1,0:T(8,128)(2,1)S(1)}, bf16[136,512]{1,0:T(8,128)(2,1)S(1)}, u32[]{:S(2)}, u32[]{:S(2)}) collective-permute-start(bf16[136,512]{1,0:T(8,128)(2,1)S(1)} %copy-done.21), channel_id=1, source_target_pairs={{0,64},{64,128},{128,192},{192,256},{256,320},{320,384},{384,448},... | collective-permute-start | bytes 417800 | tf_op jit(solution)/shard_map/ppermute | solution.py:215
  50.3 17.7 %collective-permute-start.1 = (bf16[136,512]{1,0:T(8,128)(2,1)S(1)}, bf16[136,512]{1,0:T(8,128)(2,1)S(1)}, u32[]{:S(2)}, u32[]{:S(2)}) collective-permute-start(bf16[136,512]{1,0:T(8,128)(2,1)S(1)} %copy-done.20), channel_id=1, source_target_pairs={{0,128},{64,192},{128,256},{192,320},{256,384},{320,448},{384,0},{... | collective-permute-start | bytes 417800 | tf_op jit(solution)/shard_map/ppermute | solution.py:215
  53.8 15.4 %collective-permute-start.2 = (bf16[136,512]{1,0:T(8,128)(2,1)}, bf16[136,512]{1,0:T(8,128)(2,1)S(1)}, u32[]{:S(2)}, u32[]{:S(2)}) collective-permute-start(bf16[136,512]{1,0:T(8,128)(2,1)} %get-tuple-element.47), channel_id=1, source_target_pairs={{0,192},{64,256},{128,320},{192,384},{256,448},{320,0},{384,64},{4... | collective-permute-start | bytes 417800 | tf_op jit(solution)/shard_map/ppermute | solution.py:215
  57.8 11.4 %collective-permute-start.3 = (bf16[136,512]{1,0:T(8,128)(2,1)}, bf16[136,512]{1,0:T(8,128)(2,1)S(1)}, u32[]{:S(2)}, u32[]{:S(2)}) collective-permute-start(bf16[136,512]{1,0:T(8,128)(2,1)} %get-tuple-element.48), channel_id=1, source_target_pairs={{0,256},{64,320},{128,384},{192,448},{256,0},{320,64},{384,128},{4... | collective-permute-start | bytes 417800 | tf_op jit(solution)/shard_map/ppermute | solution.py:215
  60.5 8.7 %collective-permute-start.4 = (bf16[136,512]{1,0:T(8,128)(2,1)S(1)}, bf16[136,512]{1,0:T(8,128)(2,1)S(1)}, u32[]{:S(2)}, u32[]{:S(2)}) collective-permute-start(bf16[136,512]{1,0:T(8,128)(2,1)S(1)} %copy-done.19), channel_id=1, source_target_pairs={{0,320},{64,384},{128,448},{192,0},{256,64},{320,128},{384,192},{4... | collective-permute-start | bytes 417800 | tf_op jit(solution)/shard_map/ppermute | solution.py:215
  64.3 9.2 %copy-start.3 = (bf16[136,512]{1,0:T(8,128)(2,1)}, bf16[136,512]{1,0:T(8,128)(2,1)S(1)}, u32[]{:S(2)}) copy-start(bf16[136,512]{1,0:T(8,128)(2,1)S(1)} %collective-permute-done.refs_1_) | copy-start | bytes 417796
  64.3 8.7 %collective-permute-start.5 = (bf16[136,512]{1,0:T(8,128)(2,1)S(1)}, bf16[136,512]{1,0:T(8,128)(2,1)S(1)}, u32[]{:S(2)}, u32[]{:S(2)}) collective-permute-start(bf16[136,512]{1,0:T(8,128)(2,1)S(1)} %copy-done.18), channel_id=1, source_target_pairs={{0,384},{64,448},{128,0},{192,64},{256,128},{320,192},{384,256},{4... | collective-permute-start | bytes 417800 | tf_op jit(solution)/shard_map/ppermute | solution.py:215
  68.0 5.5 %copy-start.4 = (bf16[136,512]{1,0:T(8,128)(2,1)}, bf16[136,512]{1,0:T(8,128)(2,1)S(1)}, u32[]{:S(2)}) copy-start(bf16[136,512]{1,0:T(8,128)(2,1)S(1)} %collective-permute-done.1.refs_2_) | copy-start | bytes 417796
  68.0 5.5 %collective-permute-start.6 = (bf16[136,512]{1,0:T(8,128)(2,1)S(1)}, bf16[136,512]{1,0:T(8,128)(2,1)S(1)}, u32[]{:S(2)}, u32[]{:S(2)}) collective-permute-start(bf16[136,512]{1,0:T(8,128)(2,1)S(1)} %copy-done.17), channel_id=1, source_target_pairs={{0,448},{64,0},{128,64},{192,128},{256,192},{320,256},{384,320},{4... | collective-permute-start | bytes 417800 | tf_op jit(solution)/shard_map/ppermute | solution.py:215
  69.2 4.3 %copy-start.5 = (bf16[136,512]{1,0:T(8,128)(2,1)}, bf16[136,512]{1,0:T(8,128)(2,1)S(1)}, u32[]{:S(2)}) copy-start(bf16[136,512]{1,0:T(8,128)(2,1)S(1)} %collective-permute-done.2.refs_3_) | copy-start | bytes 417796
  69.2 4.3 %copy-start.6 = (bf16[136,512]{1,0:T(8,128)(2,1)}, bf16[136,512]{1,0:T(8,128)(2,1)S(1)}, u32[]{:S(2)}) copy-start(bf16[136,512]{1,0:T(8,128)(2,1)S(1)} %collective-permute-done.3.refs_4_) | copy-start | bytes 417796
  107.2 64.8 %all-to-all-start.2 = ((bf16[64,32,512]{2,1,0:T(8,128)(2,1)}), bf16[64,32,512]{2,1,0:T(8,128)(2,1)}, u32[]{:S(2)}, u32[]{:S(2)}) async-start(bf16[64,32,512]{2,1,0:T(8,128)(2,1)} %pack.1), calls=%async_computation.2 | async-start | bytes 4194304 | tf_op jit(solution)/shard_map/all_to_all | solution.py:210
  117.9 19.7 %copy-start.1 = (s32[2048,128]{1,0:T(8,128)S(1)}, s32[2048,128]{1,0:T(8,128)}, u32[]{:S(2)}) copy-start(s32[2048,128]{1,0:T(8,128)} %get-tuple-element.62) | copy-start | bytes 3145732
  122.3 11.7 %collective-permute-start.7 = (bf16[128,512]{1,0:T(8,128)(2,1)}, bf16[128,512]{1,0:T(8,128)(2,1)S(1)}, u32[]{:S(2)}, u32[]{:S(2)}) collective-permute-start(bf16[128,512]{1,0:T(8,128)(2,1)} %get-tuple-element.55), channel_id=1, source_target_pairs={{0,448},{64,0},{128,64},{192,128},{256,192},{320,256},{384,320},{4... | collective-permute-start | bytes 393224 | tf_op jit(solution)/shard_map/ppermute | solution.py:215
  122.3 15.2 %collective-permute-start.8 = (bf16[128,512]{1,0:T(8,128)(2,1)}, bf16[128,512]{1,0:T(8,128)(2,1)S(1)}, u32[]{:S(2)}, u32[]{:S(2)}) collective-permute-start(bf16[128,512]{1,0:T(8,128)(2,1)} %get-tuple-element.56), channel_id=1, source_target_pairs={{0,384},{64,448},{128,0},{192,64},{256,128},{320,192},{384,256},{4... | collective-permute-start | bytes 393224 | tf_op jit(solution)/shard_map/ppermute | solution.py:215
  124.2 13.6 %collective-permute-start.9 = (bf16[128,512]{1,0:T(8,128)(2,1)}, bf16[128,512]{1,0:T(8,128)(2,1)S(1)}, u32[]{:S(2)}, u32[]{:S(2)}) collective-permute-start(bf16[128,512]{1,0:T(8,128)(2,1)} %get-tuple-element.57), channel_id=1, source_target_pairs={{0,320},{64,384},{128,448},{192,0},{256,64},{320,128},{384,192},{4... | collective-permute-start | bytes 393224 | tf_op jit(solution)/shard_map/ppermute | solution.py:215
  126.3 11.6 %collective-permute-start.10 = (bf16[128,512]{1,0:T(8,128)(2,1)}, bf16[128,512]{1,0:T(8,128)(2,1)S(1)}, u32[]{:S(2)}, u32[]{:S(2)}) collective-permute-start(bf16[128,512]{1,0:T(8,128)(2,1)} %get-tuple-element.58), channel_id=1, source_target_pairs={{0,256},{64,320},{128,384},{192,448},{256,0},{320,64},{384,128},{4... | collective-permute-start | bytes 393224 | tf_op jit(solution)/shard_map/ppermute | solution.py:215
  131.7 8.1 %collective-permute-start.11 = (bf16[128,512]{1,0:T(8,128)(2,1)}, bf16[128,512]{1,0:T(8,128)(2,1)S(1)}, u32[]{:S(2)}, u32[]{:S(2)}) collective-permute-start(bf16[128,512]{1,0:T(8,128)(2,1)} %get-tuple-element.59), channel_id=1, source_target_pairs={{0,192},{64,256},{128,320},{192,384},{256,448},{320,0},{384,64},{4... | collective-permute-start | bytes 393224 | tf_op jit(solution)/shard_map/ppermute | solution.py:215
  134.0 10.3 %copy-start.10 = (bf16[128,512]{1,0:T(8,128)(2,1)}, bf16[128,512]{1,0:T(8,128)(2,1)S(1)}, u32[]{:S(2)}) copy-start(bf16[128,512]{1,0:T(8,128)(2,1)S(1)} %collective-permute-done.7.refs_1_) | copy-start | bytes 393220
  134.0 8.9 %collective-permute-start.12 = (bf16[128,512]{1,0:T(8,128)(2,1)}, bf16[128,512]{1,0:T(8,128)(2,1)S(1)}, u32[]{:S(2)}, u32[]{:S(2)}) collective-permute-start(bf16[128,512]{1,0:T(8,128)(2,1)} %get-tuple-element.60), channel_id=1, source_target_pairs={{0,128},{64,192},{128,256},{192,320},{256,384},{320,448},{384,0},{... | collective-permute-start | bytes 393224 | tf_op jit(solution)/shard_map/ppermute | solution.py:215
  137.5 6.8 %copy-start.11 = (bf16[128,512]{1,0:T(8,128)(2,1)}, bf16[128,512]{1,0:T(8,128)(2,1)S(1)}, u32[]{:S(2)}) copy-start(bf16[128,512]{1,0:T(8,128)(2,1)S(1)} %collective-permute-done.8.refs_2_) | copy-start | bytes 393220
  137.5 6.8 %collective-permute-start.13 = (bf16[128,512]{1,0:T(8,128)(2,1)}, bf16[128,512]{1,0:T(8,128)(2,1)S(1)}, u32[]{:S(2)}, u32[]{:S(2)}) collective-permute-start(bf16[128,512]{1,0:T(8,128)(2,1)} %get-tuple-element.61), channel_id=1, source_target_pairs={{0,64},{64,128},{128,192},{192,256},{256,320},{320,384},{384,448},... | collective-permute-start | bytes 393224 | tf_op jit(solution)/shard_map/ppermute | solution.py:215
  137.9 6.4 %copy-start.12 = (bf16[128,512]{1,0:T(8,128)(2,1)}, bf16[128,512]{1,0:T(8,128)(2,1)S(1)}, u32[]{:S(2)}) copy-start(bf16[128,512]{1,0:T(8,128)(2,1)S(1)} %collective-permute-done.9.refs_3_) | copy-start | bytes 393220
  137.9 6.4 %copy-start.13 = (bf16[128,512]{1,0:T(8,128)(2,1)}, bf16[128,512]{1,0:T(8,128)(2,1)S(1)}, u32[]{:S(2)}) copy-start(bf16[128,512]{1,0:T(8,128)(2,1)S(1)} %collective-permute-done.10.refs_4_) | copy-start | bytes 393220
  139.8 4.5 %copy-start.14 = (bf16[128,512]{1,0:T(8,128)(2,1)}, bf16[128,512]{1,0:T(8,128)(2,1)S(1)}, u32[]{:S(2)}) copy-start(bf16[128,512]{1,0:T(8,128)(2,1)S(1)} %collective-permute-done.11.refs_5_) | copy-start | bytes 393220
  (7 other events, 9.7 us)

commit v6 on v5

--- a/solution.py
+++ b/solution.py
@@ -22,7 +22,7 @@
 
 def slots_kernel(cap, shard_ref, row_ref, ids_ref, slot_ref):
     tokens = shard_ref.shape[1]
-    groups, owners, _ = ids_ref.shape
+    owners = ids_ref.shape[0]
     shard = shard_ref[...]
     i = lax.broadcasted_iota(jnp.int32, (tokens, tokens), 0)
     j = lax.broadcasted_iota(jnp.int32, (tokens, tokens), 1)
@@ -36,52 +36,67 @@
     for w in range(cap // 2):
         named = jnp.where(slot == first + 2 * w, name, 0) + jnp.where(slot == first + 2 * w + 1, name << 16, 0)
         ids = jnp.where(lane == w, jnp.sum(named, axis=1, keepdims=True), ids)
-    for g in range(groups):
-        ids_ref[g] = ids
-
-
-def slots(shard, row, groups, owners, cap):
+    ids_ref[...] = ids
+
+
+def slots(shard, row, owners, cap):
     return pl.pallas_call(
         functools.partial(slots_kernel, cap),
         out_shape=[
-            jax.ShapeDtypeStruct((groups, owners, LANES), jnp.int32),
+            jax.ShapeDtypeStruct((owners, LANES), jnp.int32),
             jax.ShapeDtypeStruct(shard.shape, jnp.int32),
         ],
         name="slots",
     )(shard, row)
 
 
-def lookup_kernel(cap, me_ref, ids_ref, table_ref, out_ref, lines_ref):
+def lookup_kernel(cap, me_ref, ids_ref, table_ref, out_ref, names_ref, lines_ref):
     groups, owners, _ = ids_ref.shape
     rows = table_ref.shape[0]
-    lane = lax.broadcasted_iota(jnp.int32, (owners, LANES), 1)
-    for d in range(groups):
-        ids = ids_ref[lax.rem(me_ref[0] + groups - d, groups)]
-        for w in range(cap // 2):
-            word = jnp.sum(jnp.where(lane == w, ids, 0), axis=1, keepdims=True)
-            word = jnp.broadcast_to(word, (owners, LANES))
-            at = d * cap + 2 * w
-            lines_ref[pl.ds(at, owners, stride=groups * cap), :] = word & 0xFFFF
-            lines_ref[pl.ds(at + 1, owners, stride=groups * cap), :] = word >> 16
-    chunk = 256
+    chunk = out_ref.shape[0]
+
+    @pl.when(pl.program_id(0) == 0)
+    def _():
+        lane = lax.broadcasted_iota(jnp.int32, (owners, LANES), 1)
+        for d in range(groups):
+            ids = ids_ref[lax.rem(me_ref[0] + groups - d, groups)]
+            for w in range(cap // 2):
+                word = jnp.sum(jnp.where(lane == w, ids, 0), axis=1, keepdims=True)
+                word = jnp.broadcast_to(word, (owners, LANES))
+                at = d * cap + 2 * w
+                lines_ref[pl.ds(at, owners, stride=groups * cap), :] = word & 0xFFFF
+                lines_ref[pl.ds(at + 1, owners, stride=groups * cap), :] = word >> 16
+
+    names = lines_ref[pl.ds(pl.multiple_of(pl.program_id(0) * chunk, chunk), chunk), :]
+    names_ref[...] = names
     row = lax.broadcasted_iota(jnp.int32, (chunk, rows), 1) + 1
-    for m in range(0, out_ref.shape[0], chunk):
-        hot = jnp.where(lines_ref[m : m + chunk, :1] == row, 1.0, 0.0).astype(jnp.bfloat16)
-        found = jnp.dot(hot, table_ref[...], preferred_element_type=jnp.float32)
-        out_ref[m : m + chunk] = found.astype(jnp.bfloat16)
+    hot = jnp.where(names[:, :1] == row, 1.0, 0.0).astype(jnp.bfloat16)
+    found = jnp.dot(hot, table_ref[...], preferred_element_type=jnp.float32)
+    out_ref[...] = found.astype(jnp.bfloat16)
 
 
 def lookup(me, ids, table, cap):
     groups, owners, _ = ids.shape
+    rows, columns = table.shape
     count = groups * owners * cap
+    chunk = 256
     return pl.pallas_call(
         functools.partial(lookup_kernel, cap),
-        in_specs=[SMEM, VMEM, VMEM],
-        out_specs=[VMEM, VMEM],
+        grid=(count // chunk,),
+        in_specs=[
+            SMEM,
+            pl.BlockSpec(ids.shape, lambda m: (0, 0, 0)),
+            pl.BlockSpec(table.shape, lambda m: (0, 0)),
+        ],
+        out_specs=[
+            pl.BlockSpec((chunk, columns), lambda m: (m, 0)),
+            pl.BlockSpec((chunk, LANES), lambda m: (m, 0)),
+        ],
         out_shape=[
-            jax.ShapeDtypeStruct((count, table.shape[1]), jnp.bfloat16),
+            jax.ShapeDtypeStruct((count, columns), jnp.bfloat16),
             jax.ShapeDtypeStruct((count, LANES), jnp.int32),
         ],
+        scratch_shapes=[pltpu.VMEM((count, LANES), jnp.int32)],
         name="lookup",
     )(me, ids, table)
 
@@ -223,22 +238,20 @@
     cap = 2 * tokens // owners
     rows_here, columns = table.shape
     me = lax.axis_index("group").astype(jnp.int32).reshape(1)
-    ids, slot = slots(shard_ids.reshape(1, tokens), row_ids.reshape(1, tokens), groups, owners, cap)
-    ids = exchange(ids.reshape(groups * owners, 1, LANES), ("group", "vocab"))
+    ids, slot = slots(shard_ids.reshape(1, tokens), row_ids.reshape(1, tokens), owners, cap)
+    ids = exchange(ids.reshape(owners, 1, LANES), "vocab")
+    ids = lax.all_gather(ids.reshape(owners, LANES), "group", axis=0)
     pieces = cut(me, slot, cotangent, groups)
-    found, lines = lookup(me, ids.reshape(groups, owners, LANES), table, cap)
+    found, lines = lookup(me, ids, table, cap)
     found, pieces = lax.optimization_barrier((found, pieces))
     got = exchange(found.reshape(owners, groups * cap, columns), "vocab")
     pieces = pass_on(pieces, 1)
-    packed = pack(pieces, owners, cap)
-    got, packed = lax.optimization_barrier((got, packed))
-    arrived = exchange(packed, "vocab")
+    arrived = exchange(pack(pieces, owners, cap), "vocab")
     embeds = join(me, pass_on(unpack(pieces, got, cap), -1))
     wanted = lines[:, 0] - 1
-    picker = (wanted[:, None] == jnp.arange(rows_here, dtype=jnp.int32)[None, :]).astype(jnp.bfloat16)
-    table_grad = lax.dot_general(
-        picker, arrived.reshape(-1, columns), (((0,), (0,)), ((), ())), preferred_element_type=jnp.float32
-    )
+    picker = (jnp.arange(rows_here, dtype=jnp.int32)[:, None] == wanted[None, :]).astype(jnp.bfloat16)
+    picker = lax.optimization_barrier(picker)
+    table_grad = jnp.dot(picker, arrived.reshape(-1, columns), preferred_element_type=jnp.float32)
     return (embeds, table_grad.astype(jnp.bfloat16))
 
 

time: 178 us -> 187 us (1.051)
  the two profiles are of different devices: /device:TPU:28 before, /device:TPU:26 now
where the time goes in v6:
time: 187 us; the launch traced here: 186 us
  starting transfers between devices  68.6 us (37%)
  waiting for transfers between devices  68.4 us (37%)
  Pallas kernels  22 us (12%)
  blocking collectives  14 us (7%)
  matrix products  6.1 us (3%)
  other arithmetic  4.01 us (2%)
  local copies, waits for them, and re-layouts  1.95 us (1%)
    all_to_all x3, waiting for transfers between devices, exchange(): return lax.all_to_all(x, axes, split_axis=0, concat_axis=0, tiled=True)  61.5 us
    all_to_all x3, starting transfers between devices, exchange(): return lax.all_to_all(x, axes, split_axis=0, concat_axis=0, tiled=True)  35.4 us
    ppermute x14, starting transfers between devices, pass_on(): lax.ppermute(pieces[d], 'group', [(i, (i + sign * d) % size) for i in ran...  33.1 us
    all_gather x1, blocking collectives, per_device(): ids = lax.all_gather(ids.reshape(owners, LANES), 'group', axis=0)  14 us
    pallas_call x1, Pallas kernels, lookup(): pl.pallas_call(functools.partial(lookup_kernel, cap), grid=(count // chun...  7.48 us
    ppermute x14, waiting for transfers between devices, pass_on(): lax.ppermute(pieces[d], 'group', [(i, (i + sign * d) % size) for i in ran...  6.89 us
    dot_general x1, matrix products, per_device(): jnp.dot(picker, arrived.reshape(-1, columns), preferred_element_type=jnp....  6.1 us
    pallas_call x1, Pallas kernels, unpack(): pl.pallas_call(functools.partial(unpack_kernel, cap, groups), in_specs=[V...  4.42 us
  transfers between devices with their start and end apart: 17, of which 7 were waited for; matrix products, arithmetic and copies ran while one was open for 2% of the time, Pallas kernels for 7%

profile of v6, /device:TPU:26, one launch (start us, length us, event | category | flops | bytes accessed | tf_op | source)
XLA Modules:
  0.0 186.0 jit_solution(10845824857279083958)
XLA Ops:
  0.6 1.5 slots.1
  2.2 16.4 %all-to-all-start = ((s32[64,1,128]{2,1,0:T(1,128)}), s32[64,1,128]{2,1,0:T(1,128)S(1)}, u32[]{:S(2)}, u32[]{:S(2)}) async-start(s32[64,1,128]{2,1,0:T(1,128)} %bitcast.13), calls=%async_computation | async-start | bytes 65536 | tf_op jit(solution)/shard_map/all_to_all | solution.py:225
  18.6 2.3 %cut.1 = (bf16[136,512]{1,0:T(8,128)(2,1)}, bf16[136,512]{1,0:T(8,128)(2,1)}, bf16[136,512]{1,0:T(8,128)(2,1)}, bf16[136,512]{1,0:T(8,128)(2,1)}, bf16[136,512]{...) custom-call(s32[1]{0:T(128)} %bitcast.me_ref, ...), custom_call_target="tpu_custom_call" | custom-call | tf_op jit(solution)/shard_map/cut/pallas_call | solution.py:118
  20.9 6.9 %all-to-all-done = s32[64,1,128]{2,1,0:T(1,128)S(1)} async-done(((s32[64,1,128]{2,1,0:T(1,128)}), s32[64,1,128]{2,1,0:T(1,128)S(1)}, u32[]{:S(2)}, u32[]{:S(2)}) %all-to-all-start) | async-done | bytes 32800 | tf_op jit(solution)/shard_map/all_to_all | solution.py:225
  27.8 14.0 %all-gather = s32[512,1,128]{2,1,0:T(1,128)} all-gather(s32[64,1,128]{2,1,0:T(1,128)S(1)} %all-to-all-done), channel_id=2, replica_groups=mesh['group'=8,'vocab'=64] {'group'}, dimensions={0}, use_global_device_ids=true | all-gather | bytes 294912 | tf_op jit(solution)/shard_map/all_gather | solution.py:243
  41.8 7.5 %lookup.1 = (bf16[2048,512]{1,0:T(8,128)(2,1)}, s32[2048,128]{1,0:T(8,128)}) custom-call(s32[1]{0:T(128)} %bitcast.me_ref, s32[8,64,128]{2,1,0:T(8,128)} %bitcast.12, bf16[1002,512]{1,0:T(8,128)(2,1)} %table_ref.1), custom_call_target="tpu_custom_call" | custom-call | tf_op jit(solution)/shard_map/lookup/pallas_call | solution.py:83
  49.3 7.5 %all-to-all-start.1 = ((bf16[64,32,512]{2,1,0:T(8,128)(2,1)}), bf16[64,32,512]{2,1,0:T(8,128)(2,1)S(1)}, u32[]{:S(2)}, u32[]{:S(2)}) async-start(bf16[64,32,512]{2,1,0:T(8,128)(2,1)} %bitcast.11), calls=%async_computation.1 | async-start | bytes 4194304 | tf_op jit(solution)/shard_map/all_to_all | solution.py:225
  56.9 2.1 %collective-permute-start.1 = (bf16[136,512]{1,0:T(8,128)(2,1)S(1)}, bf16[136,512]{1,0:T(8,128)(2,1)S(1)}, u32[]{:S(2)}, u32[]{:S(2)}) collective-permute-start(bf16[136,512]{1,0:T(8,128)(2,1)S(1)} %copy-done.19), channel_id=1, source_target_pairs={{0,128},{64,192},{128,256},{192,320},{256,384},{320,448},{384,0},{... | collective-permute-start | bytes 417800 | tf_op jit(solution)/shard_map/ppermute | solution.py:230
  59.0 4.5 %collective-permute-start.2 = (bf16[136,512]{1,0:T(8,128)(2,1)}, bf16[136,512]{1,0:T(8,128)(2,1)S(1)}, u32[]{:S(2)}, u32[]{:S(2)}) collective-permute-start(bf16[136,512]{1,0:T(8,128)(2,1)} %get-tuple-element.45), channel_id=1, source_target_pairs={{0,192},{64,256},{128,320},{192,384},{256,448},{320,0},{384,64},{4... | collective-permute-start | bytes 417800 | tf_op jit(solution)/shard_map/ppermute | solution.py:230
  63.5 2.8 %collective-permute-start.3 = (bf16[136,512]{1,0:T(8,128)(2,1)}, bf16[136,512]{1,0:T(8,128)(2,1)S(1)}, u32[]{:S(2)}, u32[]{:S(2)}) collective-permute-start(bf16[136,512]{1,0:T(8,128)(2,1)} %get-tuple-element.46), channel_id=1, source_target_pairs={{0,256},{64,320},{128,384},{192,448},{256,0},{320,64},{384,128},{4... | collective-permute-start | bytes 417800 | tf_op jit(solution)/shard_map/ppermute | solution.py:230
  66.4 4.0 %collective-permute-start.4 = (bf16[136,512]{1,0:T(8,128)(2,1)S(1)}, bf16[136,512]{1,0:T(8,128)(2,1)S(1)}, u32[]{:S(2)}, u32[]{:S(2)}) collective-permute-start(bf16[136,512]{1,0:T(8,128)(2,1)S(1)} %copy-done.18), channel_id=1, source_target_pairs={{0,320},{64,384},{128,448},{192,0},{256,64},{320,128},{384,192},{4... | collective-permute-start | bytes 417800 | tf_op jit(solution)/shard_map/ppermute | solution.py:230
  70.4 3.7 %collective-permute-start.5 = (bf16[136,512]{1,0:T(8,128)(2,1)S(1)}, bf16[136,512]{1,0:T(8,128)(2,1)S(1)}, u32[]{:S(2)}, u32[]{:S(2)}) collective-permute-start(bf16[136,512]{1,0:T(8,128)(2,1)S(1)} %copy-done.17), channel_id=1, source_target_pairs={{0,384},{64,448},{128,0},{192,64},{256,128},{320,192},{384,256},{4... | collective-permute-start | bytes 417800 | tf_op jit(solution)/shard_map/ppermute | solution.py:230
  74.2 1.2 collective-permute-done.4.refs_5_
  75.5 3.4 %collective-permute-done.5.refs_6_ = bf16[136,512]{1,0:T(8,128)(2,1)S(1)} collective-permute-done((bf16[136,512]{1,0:T(8,128)(2,1)S(1)}, bf16[136,512]{1,0:T(8,128)(2,1)S(1)}, u32[]{:S(2)}, u32[]{:S(2)}) %collective-permute-start.5) | collective-permute-done | bytes 139296 | tf_op jit(solution)/shard_map/ppermute | solution.py:230
  78.9 0.6 copy-done.7
  79.5 0.7 copy-done.8
  80.2 3.9 %pack.1 = bf16[64,32,512]{2,1,0:T(8,128)(2,1)} custom-call(bf16[136,512]{1,0:T(8,128)(2,1)} %get-tuple-element.42.refs_0_, bf16[136,512]{1,0:T(8,128)(2,1)} %copy-done.2, bf16[136,512]{1,0:T(8,128)(2,1)} %copy-done.3, bf16[136,512]{1,0:T(8,128)(2,1)} %copy-done.4, bf16[136,512]{1,0:T(8,128)(2,1)} %copy-done.5, bf16[136,512]{1,0:T(8,128)(2,1)} %copy-done.6, ...), custom_call_target="tpu_custom_call" | custom-call | tf_op jit(solution)/shard_map/pack/pallas_call | solution.py:160
  84.1 31.0 %all-to-all-done.1.refs_8_ = bf16[64,32,512]{2,1,0:T(8,128)(2,1)S(1)} async-done(((bf16[64,32,512]{2,1,0:T(8,128)(2,1)}), bf16[64,32,512]{2,1,0:T(8,128)(2,1)S(1)}, u32[]{:S(2)}, u32[]{:S(2)}) %all-to-all-start.1) | async-done | bytes 2097184 | tf_op jit(solution)/shard_map/all_to_all | solution.py:225
  115.1 11.5 %all-to-all-start.2 = ((bf16[64,32,512]{2,1,0:T(8,128)(2,1)}), bf16[64,32,512]{2,1,0:T(8,128)(2,1)}, u32[]{:S(2)}, u32[]{:S(2)}) async-start(bf16[64,32,512]{2,1,0:T(8,128)(2,1)} %pack.1), calls=%async_computation.2 | async-start | bytes 4194304 | tf_op jit(solution)/shard_map/all_to_all | solution.py:225
  126.7 4.4 %unpack.1 = (bf16[128,512]{1,0:T(8,128)(2,1)}, bf16[128,512]{1,0:T(8,128)(2,1)}, bf16[128,512]{1,0:T(8,128)(2,1)}, bf16[128,512]{1,0:T(8,128)(2,1)}, bf16[128,51...) custom-call(bf16[136,512]{1,0:T(8,128)(2,1)} %get-tuple-element.42.refs_0_, ...), custom_call_target="tpu_custom_call" | custom-call | tf_op jit(solution)/shard_map/unpack/pallas_call | solution.py:195
  131.1 1.9 %collective-permute-start.8 = (bf16[128,512]{1,0:T(8,128)(2,1)}, bf16[128,512]{1,0:T(8,128)(2,1)S(1)}, u32[]{:S(2)}, u32[]{:S(2)}) collective-permute-start(bf16[128,512]{1,0:T(8,128)(2,1)} %get-tuple-element.53), channel_id=1, source_target_pairs={{0,384},{64,448},{128,0},{192,64},{256,128},{320,192},{384,256},{4... | collective-permute-start | bytes 393224 | tf_op jit(solution)/shard_map/ppermute | solution.py:230
  133.4 2.5 %collective-permute-start.9 = (bf16[128,512]{1,0:T(8,128)(2,1)}, bf16[128,512]{1,0:T(8,128)(2,1)S(1)}, u32[]{:S(2)}, u32[]{:S(2)}) collective-permute-start(bf16[128,512]{1,0:T(8,128)(2,1)} %get-tuple-element.54), channel_id=1, source_target_pairs={{0,320},{64,384},{128,448},{192,0},{256,64},{320,128},{384,192},{4... | collective-permute-start | bytes 393224 | tf_op jit(solution)/shard_map/ppermute | solution.py:230
  135.9 5.0 %collective-permute-start.10 = (bf16[128,512]{1,0:T(8,128)(2,1)}, bf16[128,512]{1,0:T(8,128)(2,1)S(1)}, u32[]{:S(2)}, u32[]{:S(2)}) collective-permute-start(bf16[128,512]{1,0:T(8,128)(2,1)} %get-tuple-element.55), channel_id=1, source_target_pairs={{0,256},{64,320},{128,384},{192,448},{256,0},{320,64},{384,128},{4... | collective-permute-start | bytes 393224 | tf_op jit(solution)/shard_map/ppermute | solution.py:230
  140.8 1.9 %collective-permute-start.11 = (bf16[128,512]{1,0:T(8,128)(2,1)}, bf16[128,512]{1,0:T(8,128)(2,1)S(1)}, u32[]{:S(2)}, u32[]{:S(2)}) collective-permute-start(bf16[128,512]{1,0:T(8,128)(2,1)} %get-tuple-element.56), channel_id=1, source_target_pairs={{0,192},{64,256},{128,320},{192,384},{256,448},{320,0},{384,64},{4... | collective-permute-start | bytes 393224 | tf_op jit(solution)/shard_map/ppermute | solution.py:230
  142.8 3.6 %collective-permute-start.12 = (bf16[128,512]{1,0:T(8,128)(2,1)}, bf16[128,512]{1,0:T(8,128)(2,1)S(1)}, u32[]{:S(2)}, u32[]{:S(2)}) collective-permute-start(bf16[128,512]{1,0:T(8,128)(2,1)} %get-tuple-element.57), channel_id=1, source_target_pairs={{0,128},{64,192},{128,256},{192,320},{256,384},{320,448},{384,0},{... | collective-permute-start | bytes 393224 | tf_op jit(solution)/shard_map/ppermute | solution.py:230
  146.5 0.9 collective-permute-start.13
  147.4 3.7 %fusion = bf16[1002,2048]{1,0:T(8,128)(2,1)} fusion(s32[2048]{0:T(1024)S(1)} %add_reduce_fusion), kind=kLoop, calls=%fused_computation.1 | loop fusion | flops 4104192 | bytes 4112384 | tf_op jit(solution)/shard_map/convert_element_type | solution.py:252
  151.2 2.1 %collective-permute-done.13.refs_7_ = bf16[128,512]{1,0:T(8,128)(2,1)S(1)} collective-permute-done((bf16[128,512]{1,0:T(8,128)(2,1)}, bf16[128,512]{1,0:T(8,128)(2,1)S(1)}, u32[]{:S(2)}, u32[]{:S(2)}) %collective-permute-start.13) | collective-permute-done | bytes 131104 | tf_op jit(solution)/shard_map/ppermute | solution.py:230
  153.4 0.6 copy-done.15
  154.0 2.3 %join.1 = bf16[128,4096]{1,0:T(8,128)(2,1)} custom-call(s32[1]{0:T(128)} %bitcast.me_ref, bf16[128,512]{1,0:T(8,128)(2,1)} %get-tuple-element.51.refs_0_, bf16[128,512]{1,0:T(8,128)(2,1)} %copy-done.9, bf16[128,512]{1,0:T(8,128)(2,1)} %copy-done.10, bf16[128,512]{1,0:T(8,128)(2,1)} %copy-done.11, bf16[128,512]{1,0:T(8,128)(2,1)} %copy-done.12, ...), custom_call_target="tpu_custom_call" | custom-call | tf_op jit(solution)/shard_map/join/pallas_call | solution.py:215
  156.3 23.6 %all-to-all-done.2 = bf16[64,32,512]{2,1,0:T(8,128)(2,1)} async-done(((bf16[64,32,512]{2,1,0:T(8,128)(2,1)}), bf16[64,32,512]{2,1,0:T(8,128)(2,1)}, u32[]{:S(2)}, u32[]{:S(2)}) %all-to-all-start.2) | async-done | bytes 2097184 | tf_op jit(solution)/shard_map/all_to_all | solution.py:225
  179.9 6.1 %convolution_convert_fusion = bf16[1002,512]{1,0:T(8,128)(2,1)} fusion(bf16[1002,2048]{1,0:T(8,128)(2,1)} %fusion, bf16[2048,512]{1,0:T(8,128)(2,1)} %bitcast.7), kind=kOutput, calls=%fused_computation.2 | convolution fusion | flops 2101859328 | bytes 7227392 | tf_op jit(solution)/shard_map/dot_general | solution.py:254
  (54 shorter events, 0.7 us)
Async XLA Ops:
  2.2 25.6 %all-to-all-start = ((s32[64,1,128]{2,1,0:T(1,128)}), s32[64,1,128]{2,1,0:T(1,128)S(1)}, u32[]{:S(2)}, u32[]{:S(2)}) async-start(s32[64,1,128]{2,1,0:T(1,128)} %bitcast.13), calls=%async_computation | async-start | bytes 65536 | tf_op jit(solution)/shard_map/all_to_all | solution.py:225
  49.2 7.5 %copy-start.20 = (bf16[136,512]{1,0:T(8,128)(2,1)S(1)}, bf16[136,512]{1,0:T(8,128)(2,1)}, u32[]{:S(2)}) copy-start(bf16[136,512]{1,0:T(8,128)(2,1)} %get-tuple-element.43) | copy-start | bytes 417796
  49.3 7.6 %copy-start.19 = (bf16[136,512]{1,0:T(8,128)(2,1)S(1)}, bf16[136,512]{1,0:T(8,128)(2,1)}, u32[]{:S(2)}) copy-start(bf16[136,512]{1,0:T(8,128)(2,1)} %get-tuple-element.44) | copy-start | bytes 417796
  49.3 17.1 %copy-start.18 = (bf16[136,512]{1,0:T(8,128)(2,1)S(1)}, bf16[136,512]{1,0:T(8,128)(2,1)}, u32[]{:S(2)}) copy-start(bf16[136,512]{1,0:T(8,128)(2,1)} %get-tuple-element.47) | copy-start | bytes 417796
  49.3 21.1 %copy-start.17 = (bf16[136,512]{1,0:T(8,128)(2,1)S(1)}, bf16[136,512]{1,0:T(8,128)(2,1)}, u32[]{:S(2)}) copy-start(bf16[136,512]{1,0:T(8,128)(2,1)} %get-tuple-element.48) | copy-start | bytes 417796
  49.3 24.9 %copy-start.16 = (bf16[136,512]{1,0:T(8,128)(2,1)S(1)}, bf16[136,512]{1,0:T(8,128)(2,1)}, u32[]{:S(2)}) copy-start(bf16[136,512]{1,0:T(8,128)(2,1)} %get-tuple-element.49) | copy-start | bytes 417796
  49.3 65.8 %all-to-all-start.1 = ((bf16[64,32,512]{2,1,0:T(8,128)(2,1)}), bf16[64,32,512]{2,1,0:T(8,128)(2,1)S(1)}, u32[]{:S(2)}, u32[]{:S(2)}) async-start(bf16[64,32,512]{2,1,0:T(8,128)(2,1)} %bitcast.11), calls=%async_computation.1 | async-start | bytes 4194304 | tf_op jit(solution)/shard_map/all_to_all | solution.py:225
  56.8 13.6 %collective-permute-start = (bf16[136,512]{1,0:T(8,128)(2,1)S(1)}, bf16[136,512]{1,0:T(8,128)(2,1)S(1)}, u32[]{:S(2)}, u32[]{:S(2)}) collective-permute-start(bf16[136,512]{1,0:T(8,128)(2,1)S(1)} %copy-done.20), channel_id=1, source_target_pairs={{0,64},{64,128},{128,192},{192,256},{256,320},{320,384},{384,448},... | collective-permute-start | bytes 417800 | tf_op jit(solution)/shard_map/ppermute | solution.py:230
  56.9 17.3 %collective-permute-start.1 = (bf16[136,512]{1,0:T(8,128)(2,1)S(1)}, bf16[136,512]{1,0:T(8,128)(2,1)S(1)}, u32[]{:S(2)}, u32[]{:S(2)}) collective-permute-start(bf16[136,512]{1,0:T(8,128)(2,1)S(1)} %copy-done.19), channel_id=1, source_target_pairs={{0,128},{64,192},{128,256},{192,320},{256,384},{320,448},{384,0},{... | collective-permute-start | bytes 417800 | tf_op jit(solution)/shard_map/ppermute | solution.py:230
  59.0 15.2 %collective-permute-start.2 = (bf16[136,512]{1,0:T(8,128)(2,1)}, bf16[136,512]{1,0:T(8,128)(2,1)S(1)}, u32[]{:S(2)}, u32[]{:S(2)}) collective-permute-start(bf16[136,512]{1,0:T(8,128)(2,1)} %get-tuple-element.45), channel_id=1, source_target_pairs={{0,192},{64,256},{128,320},{192,384},{256,448},{320,0},{384,64},{4... | collective-permute-start | bytes 417800 | tf_op jit(solution)/shard_map/ppermute | solution.py:230
  63.5 10.7 %collective-permute-start.3 = (bf16[136,512]{1,0:T(8,128)(2,1)}, bf16[136,512]{1,0:T(8,128)(2,1)S(1)}, u32[]{:S(2)}, u32[]{:S(2)}) collective-permute-start(bf16[136,512]{1,0:T(8,128)(2,1)} %get-tuple-element.46), channel_id=1, source_target_pairs={{0,256},{64,320},{128,384},{192,448},{256,0},{320,64},{384,128},{4... | collective-permute-start | bytes 417800 | tf_op jit(solution)/shard_map/ppermute | solution.py:230
  66.4 9.1 %collective-permute-start.4 = (bf16[136,512]{1,0:T(8,128)(2,1)S(1)}, bf16[136,512]{1,0:T(8,128)(2,1)S(1)}, u32[]{:S(2)}, u32[]{:S(2)}) collective-permute-start(bf16[136,512]{1,0:T(8,128)(2,1)S(1)} %copy-done.18), channel_id=1, source_target_pairs={{0,320},{64,384},{128,448},{192,0},{256,64},{320,128},{384,192},{4... | collective-permute-start | bytes 417800 | tf_op jit(solution)/shard_map/ppermute | solution.py:230
  70.4 8.4 %copy-start.2 = (bf16[136,512]{1,0:T(8,128)(2,1)}, bf16[136,512]{1,0:T(8,128)(2,1)S(1)}, u32[]{:S(2)}) copy-start(bf16[136,512]{1,0:T(8,128)(2,1)S(1)} %collective-permute-done.refs_1_) | copy-start | bytes 417796
  70.4 8.4 %collective-permute-start.5 = (bf16[136,512]{1,0:T(8,128)(2,1)S(1)}, bf16[136,512]{1,0:T(8,128)(2,1)S(1)}, u32[]{:S(2)}, u32[]{:S(2)}) collective-permute-start(bf16[136,512]{1,0:T(8,128)(2,1)S(1)} %copy-done.17), channel_id=1, source_target_pairs={{0,384},{64,448},{128,0},{192,64},{256,128},{320,192},{384,256},{4... | collective-permute-start | bytes 417800 | tf_op jit(solution)/shard_map/ppermute | solution.py:230
  74.2 4.7 %copy-start.3 = (bf16[136,512]{1,0:T(8,128)(2,1)}, bf16[136,512]{1,0:T(8,128)(2,1)S(1)}, u32[]{:S(2)}) copy-start(bf16[136,512]{1,0:T(8,128)(2,1)S(1)} %collective-permute-done.1.refs_2_) | copy-start | bytes 417796
  74.2 4.7 %collective-permute-start.6 = (bf16[136,512]{1,0:T(8,128)(2,1)S(1)}, bf16[136,512]{1,0:T(8,128)(2,1)S(1)}, u32[]{:S(2)}, u32[]{:S(2)}) collective-permute-start(bf16[136,512]{1,0:T(8,128)(2,1)S(1)} %copy-done.16), channel_id=1, source_target_pairs={{0,448},{64,0},{128,64},{192,128},{256,192},{320,256},{384,320},{4... | collective-permute-start | bytes 417800 | tf_op jit(solution)/shard_map/ppermute | solution.py:230
  74.2 4.7 %copy-start.4 = (bf16[136,512]{1,0:T(8,128)(2,1)}, bf16[136,512]{1,0:T(8,128)(2,1)S(1)}, u32[]{:S(2)}) copy-start(bf16[136,512]{1,0:T(8,128)(2,1)S(1)} %collective-permute-done.2.refs_3_) | copy-start | bytes 417796
  74.2 4.7 %copy-start.5 = (bf16[136,512]{1,0:T(8,128)(2,1)}, bf16[136,512]{1,0:T(8,128)(2,1)S(1)}, u32[]{:S(2)}) copy-start(bf16[136,512]{1,0:T(8,128)(2,1)S(1)} %collective-permute-done.3.refs_4_) | copy-start | bytes 417796
  75.5 3.4 %copy-start.6 = (bf16[136,512]{1,0:T(8,128)(2,1)}, bf16[136,512]{1,0:T(8,128)(2,1)S(1)}, u32[]{:S(2)}) copy-start(bf16[136,512]{1,0:T(8,128)(2,1)S(1)} %collective-permute-done.4.refs_5_) | copy-start | bytes 417796
  115.1 11.6 %copy-start = (bf16[64,32,512]{2,1,0:T(8,128)(2,1)}, bf16[64,32,512]{2,1,0:T(8,128)(2,1)S(1)}, u32[]{:S(2)}) copy-start(bf16[64,32,512]{2,1,0:T(8,128)(2,1)S(1)} %all-to-all-done.1.refs_8_) | copy-start | bytes 6291460
  115.1 64.8 %all-to-all-start.2 = ((bf16[64,32,512]{2,1,0:T(8,128)(2,1)}), bf16[64,32,512]{2,1,0:T(8,128)(2,1)}, u32[]{:S(2)}, u32[]{:S(2)}) async-start(bf16[64,32,512]{2,1,0:T(8,128)(2,1)} %pack.1), calls=%async_computation.2 | async-start | bytes 4194304 | tf_op jit(solution)/shard_map/all_to_all | solution.py:225
  126.7 6.4 %copy-start.1 = (s32[2048,128]{1,0:T(8,128)S(1)}, s32[2048,128]{1,0:T(8,128)}, u32[]{:S(2)}) copy-start(s32[2048,128]{1,0:T(8,128)} %get-tuple-element.59) | copy-start | bytes 3145732
  131.1 11.7 %collective-permute-start.7 = (bf16[128,512]{1,0:T(8,128)(2,1)}, bf16[128,512]{1,0:T(8,128)(2,1)S(1)}, u32[]{:S(2)}, u32[]{:S(2)}) collective-permute-start(bf16[128,512]{1,0:T(8,128)(2,1)} %get-tuple-element.52), channel_id=1, source_target_pairs={{0,448},{64,0},{128,64},{192,128},{256,192},{320,256},{384,320},{4... | collective-permute-start | bytes 393224 | tf_op jit(solution)/shard_map/ppermute | solution.py:230
  131.1 15.3 %collective-permute-start.8 = (bf16[128,512]{1,0:T(8,128)(2,1)}, bf16[128,512]{1,0:T(8,128)(2,1)S(1)}, u32[]{:S(2)}, u32[]{:S(2)}) collective-permute-start(bf16[128,512]{1,0:T(8,128)(2,1)} %get-tuple-element.53), channel_id=1, source_target_pairs={{0,384},{64,448},{128,0},{192,64},{256,128},{320,192},{384,256},{4... | collective-permute-start | bytes 393224 | tf_op jit(solution)/shard_map/ppermute | solution.py:230
  133.4 17.7 %collective-permute-start.9 = (bf16[128,512]{1,0:T(8,128)(2,1)}, bf16[128,512]{1,0:T(8,128)(2,1)S(1)}, u32[]{:S(2)}, u32[]{:S(2)}) collective-permute-start(bf16[128,512]{1,0:T(8,128)(2,1)} %get-tuple-element.54), channel_id=1, source_target_pairs={{0,320},{64,384},{128,448},{192,0},{256,64},{320,128},{384,192},{4... | collective-permute-start | bytes 393224 | tf_op jit(solution)/shard_map/ppermute | solution.py:230
  135.9 15.2 %collective-permute-start.10 = (bf16[128,512]{1,0:T(8,128)(2,1)}, bf16[128,512]{1,0:T(8,128)(2,1)S(1)}, u32[]{:S(2)}, u32[]{:S(2)}) collective-permute-start(bf16[128,512]{1,0:T(8,128)(2,1)} %get-tuple-element.55), channel_id=1, source_target_pairs={{0,256},{64,320},{128,384},{192,448},{256,0},{320,64},{384,128},{4... | collective-permute-start | bytes 393224 | tf_op jit(solution)/shard_map/ppermute | solution.py:230
  140.8 10.2 %collective-permute-start.11 = (bf16[128,512]{1,0:T(8,128)(2,1)}, bf16[128,512]{1,0:T(8,128)(2,1)S(1)}, u32[]{:S(2)}, u32[]{:S(2)}) collective-permute-start(bf16[128,512]{1,0:T(8,128)(2,1)} %get-tuple-element.56), channel_id=1, source_target_pairs={{0,192},{64,256},{128,320},{192,384},{256,448},{320,0},{384,64},{4... | collective-permute-start | bytes 393224 | tf_op jit(solution)/shard_map/ppermute | solution.py:230
  142.8 10.6 %copy-start.9 = (bf16[128,512]{1,0:T(8,128)(2,1)}, bf16[128,512]{1,0:T(8,128)(2,1)S(1)}, u32[]{:S(2)}) copy-start(bf16[128,512]{1,0:T(8,128)(2,1)S(1)} %collective-permute-done.7.refs_1_) | copy-start | bytes 393220
  142.8 8.4 %collective-permute-start.12 = (bf16[128,512]{1,0:T(8,128)(2,1)}, bf16[128,512]{1,0:T(8,128)(2,1)S(1)}, u32[]{:S(2)}, u32[]{:S(2)}) collective-permute-start(bf16[128,512]{1,0:T(8,128)(2,1)} %get-tuple-element.57), channel_id=1, source_target_pairs={{0,128},{64,192},{128,256},{192,320},{256,384},{320,448},{384,0},{... | collective-permute-start | bytes 393224 | tf_op jit(solution)/shard_map/ppermute | solution.py:230
  146.4 6.9 %copy-start.10 = (bf16[128,512]{1,0:T(8,128)(2,1)}, bf16[128,512]{1,0:T(8,128)(2,1)S(1)}, u32[]{:S(2)}) copy-start(bf16[128,512]{1,0:T(8,128)(2,1)S(1)} %collective-permute-done.8.refs_2_) | copy-start | bytes 393220
  146.5 6.9 %collective-permute-start.13 = (bf16[128,512]{1,0:T(8,128)(2,1)}, bf16[128,512]{1,0:T(8,128)(2,1)S(1)}, u32[]{:S(2)}, u32[]{:S(2)}) collective-permute-start(bf16[128,512]{1,0:T(8,128)(2,1)} %get-tuple-element.58), channel_id=1, source_target_pairs={{0,64},{64,128},{128,192},{192,256},{256,320},{320,384},{384,448},... | collective-permute-start | bytes 393224 | tf_op jit(solution)/shard_map/ppermute | solution.py:230
  151.0 2.3 %copy-start.11 = (bf16[128,512]{1,0:T(8,128)(2,1)}, bf16[128,512]{1,0:T(8,128)(2,1)S(1)}, u32[]{:S(2)}) copy-start(bf16[128,512]{1,0:T(8,128)(2,1)S(1)} %collective-permute-done.9.refs_3_) | copy-start | bytes 393220
  (6 other events, 8.7 us)

commit v7 on v4

--- a/solution.py
+++ b/solution.py
@@ -171,47 +171,33 @@
     )(words, table)
 
 
-def shifted(x, axis, offset):
-    size = lax.axis_size(axis)
-    return lax.ppermute(x, axis, [(i, (i - offset) % size) for i in range(size)])
-
-
-def neighbours(x, axis):
-    near = jnp.concatenate([shifted(x, axis, -1), x, shifted(x, axis, 1)], axis=0)
-    return shifted(near, axis, -3), near, shifted(near, axis, 3)
-
-
-def unpack_kernel(pieces, slot_ref, got_ref, out_ref, hot):
-    tokens = slot_ref.shape[1]
-    rows = hot.shape[1]
+def unpack_kernel(pieces, slot_ref, got_ref, out_ref, hot, wide):
+    tokens, places = hot.shape
+    lines = wide.shape[0]
 
     @pl.when(pl.program_id(0) == 0)
     def _():
-        slot = to_column(slot_ref[...])
-        line = lax.broadcasted_iota(jnp.int32, (tokens, rows), 1)
-        for c in range(pieces):
-            hot[c * tokens : (c + 1) * tokens, :] = jnp.where(
-                line == slot * pieces + c, 1.0, 0.0
-            ).astype(jnp.bfloat16)
-
-    groups = out_ref.shape[1] // (pieces * LANES)
+        line = lax.broadcasted_iota(jnp.int32, (tokens, places), 1)
+        hot[...] = jnp.where(line == to_column(slot_ref[...]), 1.0, 0.0).astype(jnp.bfloat16)
+
+    columns = pieces * LANES
+    groups = out_ref.shape[1] // columns
     owners = got_ref.shape[0] // groups
-    right = [got_ref[g * owners : (g + 1) * owners].reshape(rows, LANES) for g in range(groups)]
-    picked = jnp.dot(hot[...], jnp.concatenate(right, axis=1), preferred_element_type=jnp.float32)
-    picked = picked.astype(jnp.bfloat16)
     for g in range(groups):
-        for c in range(pieces):
-            out_ref[:, (g * pieces + c) * LANES : (g * pieces + c + 1) * LANES] = picked[
-                c * tokens : (c + 1) * tokens, g * LANES : (g + 1) * LANES
-            ]
+        wide[...] = got_ref[g * owners : (g + 1) * owners].reshape(lines, LANES).astype(jnp.float32)
+        rows = jnp.concatenate(
+            [wide[pl.ds(c, places, stride=pieces), :].astype(jnp.bfloat16) for c in range(pieces)], axis=1
+        )
+        picked = jnp.dot(hot[...], rows, preferred_element_type=jnp.float32)
+        out_ref[:, g * columns : (g + 1) * columns] = picked.astype(jnp.bfloat16)
 
 
 def unpack(slot, got, groups, width):
     tokens = slot.shape[1]
     pieces = width // groups // LANES
     owners = got.shape[0] // groups
-    rows = owners * got.shape[1]
-    step = 2
+    lines = owners * got.shape[1]
+    step = groups // 2
     return pl.pallas_call(
         functools.partial(unpack_kernel, pieces),
         grid=(groups // step,),
@@ -221,7 +207,10 @@
         ],
         out_specs=pl.BlockSpec((tokens, step * pieces * LANES), lambda g: (0, g)),
         out_shape=jax.ShapeDtypeStruct((tokens, width), jnp.bfloat16),
-        scratch_shapes=[pltpu.VMEM((pieces * tokens, rows), jnp.bfloat16)],
+        scratch_shapes=[
+            pltpu.VMEM((tokens, lines // pieces), jnp.bfloat16),
+            pltpu.VMEM((lines, LANES), jnp.float32),
+        ],
         name="unpack",
     )(slot, got)
 

time: 169 us -> 167 us (0.988)
  Pallas kernels: 18.7 us -> 17 us
where the time goes in v7:
time: 167 us; the launch traced here: 166 us
  waiting for transfers between devices  87.8 us (53%)
  starting transfers between devices  39.9 us (24%)
  Pallas kernels  17 us (10%)
  blocking collectives  12.7 us (8%)
  matrix products  5.28 us (3%)
  local copies, waits for them, and re-layouts  3.07 us (2%)
    all_to_all x3, waiting for transfers between devices, exchange(): return lax.all_to_all(x, axes, split_axis=0, concat_axis=0, tiled=True)  87.8 us
    all_to_all x3, starting transfers between devices, exchange(): return lax.all_to_all(x, axes, split_axis=0, concat_axis=0, tiled=True)  39.9 us
    all_gather x1, blocking collectives, per_device(): lax.all_gather(pick(ids.reshape(owners, LANES), cap), 'group', axis=0)  12.7 us
    pallas_call x1, Pallas kernels, lookup(): pl.pallas_call(functools.partial(lookup_kernel, cap), grid=(groups // ste...  6.4 us
    dot_general x1, matrix products, per_device(): lax.dot_general(picker, arrived.reshape(peers * cap, columns), (((0,), (0...  5.28 us
    pallas_call x1, Pallas kernels, pack(): pl.pallas_call(functools.partial(pack_kernel, pieces, owners), grid=(grou...  4.65 us
  transfers between devices with their start and end apart: 3, of which 3 were waited for; matrix products, arithmetic and copies ran while one was open for 5% of the time, Pallas kernels for 7%

profile of v7, /device:TPU:1, one launch (start us, length us, event | category | flops | bytes accessed | tf_op | source)
XLA Modules:
  0.0 166.4 jit_solution(10791583211722469752)
XLA Ops:
  0.6 1.5 slots.1
  2.2 17.1 %all-to-all-start = ((s32[64,1,128]{2,1,0:T(1,128)}), s32[64,1,128]{2,1,0:T(1,128)S(1)}, u32[]{:S(2)}, u32[]{:S(2)}) async-start(s32[64,1,128]{2,1,0:T(1,128)} %bitcast.13), calls=%async_computation | async-start | bytes 65536 | tf_op jit(solution)/shard_map/all_to_all | solution.py:219
  19.3 4.7 %pack.1 = bf16[512,16,128]{2,1,0:T(8,128)(2,1)} custom-call(s32[1,128]{1,0:T(1,128)} %get-tuple-element.6.slot_ref, bf16[128,4096]{1,0:T(8,128)(2,1)} %cot_ref.1), custom_call_target="tpu_custom_call" | custom-call | flops 1073741824 | bytes 3145728 | tf_op jit(solution)/shard_map/pack/pallas_call | solution.py:83
  24.0 6.1 %all-to-all-done = s32[64,1,128]{2,1,0:T(1,128)S(1)} async-done(((s32[64,1,128]{2,1,0:T(1,128)}), s32[64,1,128]{2,1,0:T(1,128)S(1)}, u32[]{:S(2)}, u32[]{:S(2)}) %all-to-all-start) | async-done | bytes 32800 | tf_op jit(solution)/shard_map/all_to_all | solution.py:219
  30.1 0.0 copy-start
  30.1 11.6 %all-to-all-start.2 = ((bf16[512,16,128]{2,1,0:T(8,128)(2,1)}), bf16[512,16,128]{2,1,0:T(8,128)(2,1)S(1)}, u32[]{:S(2)}, u32[]{:S(2)}) async-start(bf16[512,16,128]{2,1,0:T(8,128)(2,1)} %pack.1), calls=%async_computation.2 | async-start | bytes 4194304 | tf_op jit(solution)/shard_map/all_to_all | solution.py:219
  41.7 0.0 copy-done
  41.7 1.4 pick.1
  43.1 12.7 %all-gather.1.words_ref = s32[8,1,128]{2,1,0:T(1,128)} all-gather(s32[1,1,128]{2,1,0:T(1,128)} %bitcast.14), channel_id=2, replica_groups=mesh['group'=8,'vocab'=64] {'group'}, dimensions={0}, use_global_device_ids=true | all-gather | bytes 4608 | tf_op jit(solution)/shard_map/all_gather | solution.py:234
  55.8 6.4 %lookup.1 = bf16[512,16,128]{2,1,0:T(8,128)(2,1)} custom-call(s32[8,1,128]{2,1,0:T(1,128)} %all-gather.1.words_ref, bf16[1002,512]{1,0:T(8,128)(2,1)} %table_ref.1), custom_call_target="tpu_custom_call" | custom-call | flops 2101346304 | bytes 3123200 | tf_op jit(solution)/shard_map/lookup/pallas_call | solution.py:155
  62.2 0.0 copy-start.1
  62.2 36.1 %all-to-all-done.2 = bf16[512,16,128]{2,1,0:T(8,128)(2,1)S(1)} async-done(((bf16[512,16,128]{2,1,0:T(8,128)(2,1)}), bf16[512,16,128]{2,1,0:T(8,128)(2,1)S(1)}, u32[]{:S(2)}, u32[]{:S(2)}) %all-to-all-start.2) | async-done | bytes 2097184 | tf_op jit(solution)/shard_map/all_to_all | solution.py:219
  98.3 11.1 %all-to-all-start.1 = ((bf16[512,16,128]{2,1,0:T(8,128)(2,1)}), bf16[512,16,128]{2,1,0:T(8,128)(2,1)}, u32[]{:S(2)}, u32[]{:S(2)}) async-start(bf16[512,16,128]{2,1,0:T(8,128)(2,1)} %lookup.1), calls=%async_computation.1 | async-start | bytes 4194304 | tf_op jit(solution)/shard_map/all_to_all | solution.py:219
  109.4 0.0 copy-done.1
  109.4 0.1 and.18
  109.5 0.1 shift_right_arithmetic.18
  109.6 0.2 copy.17
  109.8 0.2 sub.13
  109.9 2.6 %reshape.59 = bf16[2048,512]{1,0:T(8,128)(2,1)} reshape(bf16[512,16,128]{2,1,0:T(8,128)(2,1)S(1)} %all-to-all-done.2) | data formatting | bytes 4194304 | tf_op jit(solution)/shard_map/reshape | solution.py:242
  112.5 5.3 %fusion.2 = bf16[1002,512]{1,0:T(8,128)(2,1)} fusion(bf16[2048,512]{1,0:T(8,128)(2,1)} %reshape.59, s32[2048]{0:T(1024)S(1)} %sub.13), kind=kOutput, calls=%fused_computation.3 | convolution fusion | flops 2103911424 | bytes 3131392 | tf_op jit(solution)/shard_map/dot_general | solution.py:240
  117.8 45.6 %all-to-all-done.1.got_ref = bf16[512,16,128]{2,1,0:T(8,128)(2,1)} async-done(((bf16[512,16,128]{2,1,0:T(8,128)(2,1)}), bf16[512,16,128]{2,1,0:T(8,128)(2,1)}, u32[]{:S(2)}, u32[]{:S(2)}) %all-to-all-start.1) | async-done | bytes 2097184 | tf_op jit(solution)/shard_map/all_to_all | solution.py:219
  163.4 3.0 %unpack.1 = bf16[128,4096]{1,0:T(8,128)(2,1)} custom-call(s32[1,128]{1,0:T(1,128)} %get-tuple-element.6.slot_ref, bf16[512,16,128]{2,1,0:T(8,128)(2,1)} %all-to-all-done.1.got_ref), custom_call_target="tpu_custom_call" | custom-call | tf_op jit(solution)/shard_map/unpack/pallas_call | solution.py:201
  (4 shorter events, 0.0 us)
Async XLA Ops:
  2.2 27.9 %all-to-all-start = ((s32[64,1,128]{2,1,0:T(1,128)}), s32[64,1,128]{2,1,0:T(1,128)S(1)}, u32[]{:S(2)}, u32[]{:S(2)}) async-start(s32[64,1,128]{2,1,0:T(1,128)} %bitcast.13), calls=%async_computation | async-start | bytes 65536 | tf_op jit(solution)/shard_map/all_to_all | solution.py:219
  30.1 11.6 %copy-start = (s32[64,1,128]{2,1,0:T(1,128)}, s32[64,1,128]{2,1,0:T(1,128)S(1)}, u32[]{:S(2)}) copy-start(s32[64,1,128]{2,1,0:T(1,128)S(1)} %all-to-all-done) | copy-start | bytes 98308
  30.1 68.2 %all-to-all-start.2 = ((bf16[512,16,128]{2,1,0:T(8,128)(2,1)}), bf16[512,16,128]{2,1,0:T(8,128)(2,1)S(1)}, u32[]{:S(2)}, u32[]{:S(2)}) async-start(bf16[512,16,128]{2,1,0:T(8,128)(2,1)} %pack.1), calls=%async_computation.2 | async-start | bytes 4194304 | tf_op jit(solution)/shard_map/all_to_all | solution.py:219
  62.2 47.2 %copy-start.1 = (s32[8,1,128]{2,1,0:T(1,128)S(1)}, s32[8,1,128]{2,1,0:T(1,128)}, u32[]{:S(2)}) copy-start(s32[8,1,128]{2,1,0:T(1,128)} %all-gather.1.words_ref) | copy-start | bytes 12292
  98.3 65.1 %all-to-all-start.1 = ((bf16[512,16,128]{2,1,0:T(8,128)(2,1)}), bf16[512,16,128]{2,1,0:T(8,128)(2,1)}, u32[]{:S(2)}, u32[]{:S(2)}) async-start(bf16[512,16,128]{2,1,0:T(8,128)(2,1)} %lookup.1), calls=%async_computation.1 | async-start | bytes 4194304 | tf_op jit(solution)/shard_map/all_to_all | solution.py:219

commit v8 on v7

--- a/solution.py
+++ b/solution.py
@@ -47,39 +47,32 @@
     )(shard, row)
 
 
-def pack_kernel(pieces, owners, slot_ref, cot_ref, out_ref, hot):
-    tokens = slot_ref.shape[1]
-    rows = hot.shape[0]
+def pack_kernel(pieces, owners, slot_ref, cot_ref, out_ref, hot, wide):
+    places, tokens = hot.shape
+    lines = wide.shape[1]
 
     @pl.when(pl.program_id(0) == 0)
     def _():
-        line = lax.broadcasted_iota(jnp.int32, (rows, tokens), 0)
+        line = lax.broadcasted_iota(jnp.int32, (places, tokens), 0)
+        hot[...] = jnp.where(line == slot_ref[...], 1.0, 0.0).astype(jnp.bfloat16)
+
+    columns = pieces * LANES
+    for g in range(cot_ref.shape[1] // columns):
+        placed = jnp.dot(
+            hot[...], cot_ref[:, g * columns : (g + 1) * columns], preferred_element_type=jnp.float32
+        )
         for c in range(pieces):
-            hot[:, c * tokens : (c + 1) * tokens] = jnp.where(
-                line == slot_ref[...] * pieces + c, 1.0, 0.0
-            ).astype(jnp.bfloat16)
-
-    groups = cot_ref.shape[1] // (pieces * LANES)
-    right = []
-    for g in range(groups):
-        right.append(
-            jnp.concatenate(
-                [cot_ref[:, (g * pieces + c) * LANES : (g * pieces + c + 1) * LANES] for c in range(pieces)],
-                axis=0,
-            )
-        )
-    placed = jnp.dot(hot[...], jnp.concatenate(right, axis=1), preferred_element_type=jnp.float32)
-    placed = placed.astype(jnp.bfloat16)
-    for g in range(groups):
-        block = placed[:, g * LANES : (g + 1) * LANES]
-        out_ref[g * owners : (g + 1) * owners] = block.reshape(owners, rows // owners, LANES)
+            wide[g % 2, pl.ds(c, places, stride=pieces), :] = placed[:, c * LANES : (c + 1) * LANES]
+        block = wide[g % 2].astype(jnp.bfloat16)
+        out_ref[g * owners : (g + 1) * owners] = block.reshape(owners, lines // owners, LANES)
 
 
 def pack(slot, cotangent, groups, owners, cap):
     tokens, width = cotangent.shape
     pieces = width // groups // LANES
-    rows = owners * cap * pieces
-    step = 2
+    places = owners * cap
+    lines = places * pieces
+    step = groups // 2
     return pl.pallas_call(
         functools.partial(pack_kernel, pieces, owners),
         grid=(groups // step,),
@@ -89,10 +82,13 @@
         ],
         out_specs=pl.BlockSpec((step * owners, cap * pieces, LANES), lambda g: (g, 0, 0)),
         out_shape=jax.ShapeDtypeStruct((groups * owners, cap * pieces, LANES), jnp.bfloat16),
-        scratch_shapes=[pltpu.VMEM((rows, pieces * tokens), jnp.bfloat16)],
+        scratch_shapes=[
+            pltpu.VMEM((places, tokens), jnp.bfloat16),
+            pltpu.VMEM((2, lines, LANES), jnp.float32),
+        ],
         cost_estimate=pl.CostEstimate(
-            flops=2 * rows * pieces * tokens * groups * LANES,
-            bytes_accessed=2 * (tokens * width + groups * rows * LANES),
+            flops=2 * places * tokens * width,
+            bytes_accessed=2 * (tokens * width + groups * lines * LANES),
             transcendentals=0,
         ),
         name="pack",

time: 167 us -> 166 us (level)
  no operation moved by 1% of the time
where the time goes in v8:
time: 166 us
  waiting for transfers between devices  89.3 us (54%)
  starting transfers between devices  38.6 us (23%)
  Pallas kernels  15.5 us (9%)
  blocking collectives  12.8 us (8%)
  matrix products  5.28 us (3%)
  local copies, waits for them, and re-layouts  3.68 us (2%)
    all_to_all x3, waiting for transfers between devices, exchange(): return lax.all_to_all(x, axes, split_axis=0, concat_axis=0, tiled=True)  89.3 us
    all_to_all x3, starting transfers between devices, exchange(): return lax.all_to_all(x, axes, split_axis=0, concat_axis=0, tiled=True)  38.6 us
    all_gather x1, blocking collectives, per_device(): lax.all_gather(pick(ids.reshape(owners, LANES), cap), 'group', axis=0)  12.8 us
    pallas_call x1, Pallas kernels, lookup(): pl.pallas_call(functools.partial(lookup_kernel, cap), grid=(groups // ste...  6.41 us
    dot_general x1, matrix products, per_device(): lax.dot_general(picker, arrived.reshape(peers * cap, columns), (((0,), (0...  5.28 us
  transfers between devices with their start and end apart: 3, of which 3 were waited for; matrix products, arithmetic and copies ran while one was open for 5% of the time, Pallas kernels for 7%

profile of v8, /device:TPU:1, one launch (start us, length us, event | category | flops | bytes accessed | tf_op | source)
XLA Modules:
  0.0 165.9 jit_solution(14788015224776679083)
XLA Ops:
  0.6 1.5 slots.1
  2.2 17.1 %all-to-all-start = ((s32[64,1,128]{2,1,0:T(1,128)}), s32[64,1,128]{2,1,0:T(1,128)S(1)}, u32[]{:S(2)}, u32[]{:S(2)}) async-start(s32[64,1,128]{2,1,0:T(1,128)} %bitcast.13), calls=%async_computation | async-start | bytes 65536 | tf_op jit(solution)/shard_map/all_to_all | solution.py:215
  19.3 3.2 %pack.1 = bf16[512,16,128]{2,1,0:T(8,128)(2,1)} custom-call(s32[1,128]{1,0:T(1,128)} %get-tuple-element.6.slot_ref, bf16[128,4096]{1,0:T(8,128)(2,1)} %cot_ref.1), custom_call_target="tpu_custom_call" | custom-call | flops 268435456 | bytes 3145728 | tf_op jit(solution)/shard_map/pack/pallas_call | solution.py:76
  22.5 7.6 %all-to-all-done = s32[64,1,128]{2,1,0:T(1,128)S(1)} async-done(((s32[64,1,128]{2,1,0:T(1,128)}), s32[64,1,128]{2,1,0:T(1,128)S(1)}, u32[]{:S(2)}, u32[]{:S(2)}) %all-to-all-start) | async-done | bytes 32800 | tf_op jit(solution)/shard_map/all_to_all | solution.py:215
  30.1 0.0 copy-start
  30.1 0.6 copy-done
  30.7 10.3 %all-to-all-start.2 = ((bf16[512,16,128]{2,1,0:T(8,128)(2,1)}), bf16[512,16,128]{2,1,0:T(8,128)(2,1)S(1)}, u32[]{:S(2)}, u32[]{:S(2)}) async-start(bf16[512,16,128]{2,1,0:T(8,128)(2,1)} %pack.1), calls=%async_computation.2 | async-start | bytes 4194304 | tf_op jit(solution)/shard_map/all_to_all | solution.py:215
  41.0 1.4 pick.1
  42.4 12.8 %all-gather.1.words_ref = s32[8,1,128]{2,1,0:T(1,128)} all-gather(s32[1,1,128]{2,1,0:T(1,128)} %bitcast.14), channel_id=2, replica_groups=mesh['group'=8,'vocab'=64] {'group'}, dimensions={0}, use_global_device_ids=true | all-gather | bytes 4608 | tf_op jit(solution)/shard_map/all_gather | solution.py:230
  55.2 6.4 %lookup.1 = bf16[512,16,128]{2,1,0:T(8,128)(2,1)} custom-call(s32[8,1,128]{2,1,0:T(1,128)} %all-gather.1.words_ref, bf16[1002,512]{1,0:T(8,128)(2,1)} %table_ref.1), custom_call_target="tpu_custom_call" | custom-call | flops 2101346304 | bytes 3123200 | tf_op jit(solution)/shard_map/lookup/pallas_call | solution.py:151
  61.6 0.0 copy-start.1
  61.6 36.1 %all-to-all-done.2 = bf16[512,16,128]{2,1,0:T(8,128)(2,1)S(1)} async-done(((bf16[512,16,128]{2,1,0:T(8,128)(2,1)}), bf16[512,16,128]{2,1,0:T(8,128)(2,1)S(1)}, u32[]{:S(2)}, u32[]{:S(2)}) %all-to-all-start.2) | async-done | bytes 2097184 | tf_op jit(solution)/shard_map/all_to_all | solution.py:215
  97.7 11.1 %all-to-all-start.1 = ((bf16[512,16,128]{2,1,0:T(8,128)(2,1)}), bf16[512,16,128]{2,1,0:T(8,128)(2,1)}, u32[]{:S(2)}, u32[]{:S(2)}) async-start(bf16[512,16,128]{2,1,0:T(8,128)(2,1)} %lookup.1), calls=%async_computation.1 | async-start | bytes 4194304 | tf_op jit(solution)/shard_map/all_to_all | solution.py:215
  108.9 0.0 copy-done.1
  108.9 0.1 and.18
  109.0 0.1 shift_right_arithmetic.18
  109.1 0.2 copy.17
  109.2 0.2 sub.13
  109.4 2.6 %reshape.59 = bf16[2048,512]{1,0:T(8,128)(2,1)} reshape(bf16[512,16,128]{2,1,0:T(8,128)(2,1)S(1)} %all-to-all-done.2) | data formatting | bytes 4194304 | tf_op jit(solution)/shard_map/reshape | solution.py:238
  112.0 5.3 %fusion.2 = bf16[1002,512]{1,0:T(8,128)(2,1)} fusion(bf16[2048,512]{1,0:T(8,128)(2,1)} %reshape.59, s32[2048]{0:T(1024)S(1)} %sub.13), kind=kOutput, calls=%fused_computation.3 | convolution fusion | flops 2103911424 | bytes 3131392 | tf_op jit(solution)/shard_map/dot_general | solution.py:236
  117.3 45.6 %all-to-all-done.1.got_ref = bf16[512,16,128]{2,1,0:T(8,128)(2,1)} async-done(((bf16[512,16,128]{2,1,0:T(8,128)(2,1)}), bf16[512,16,128]{2,1,0:T(8,128)(2,1)}, u32[]{:S(2)}, u32[]{:S(2)}) %all-to-all-start.1) | async-done | bytes 2097184 | tf_op jit(solution)/shard_map/all_to_all | solution.py:215
  162.9 3.0 %unpack.1 = bf16[128,4096]{1,0:T(8,128)(2,1)} custom-call(s32[1,128]{1,0:T(1,128)} %get-tuple-element.6.slot_ref, bf16[512,16,128]{2,1,0:T(8,128)(2,1)} %all-to-all-done.1.got_ref), custom_call_target="tpu_custom_call" | custom-call | tf_op jit(solution)/shard_map/unpack/pallas_call | solution.py:197
  (4 shorter events, 0.0 us)
Async XLA Ops:
  2.2 27.9 %all-to-all-start = ((s32[64,1,128]{2,1,0:T(1,128)}), s32[64,1,128]{2,1,0:T(1,128)S(1)}, u32[]{:S(2)}, u32[]{:S(2)}) async-start(s32[64,1,128]{2,1,0:T(1,128)} %bitcast.13), calls=%async_computation | async-start | bytes 65536 | tf_op jit(solution)/shard_map/all_to_all | solution.py:215
  30.1 0.6 copy-start
  30.7 67.0 %all-to-all-start.2 = ((bf16[512,16,128]{2,1,0:T(8,128)(2,1)}), bf16[512,16,128]{2,1,0:T(8,128)(2,1)S(1)}, u32[]{:S(2)}, u32[]{:S(2)}) async-start(bf16[512,16,128]{2,1,0:T(8,128)(2,1)} %pack.1), calls=%async_computation.2 | async-start | bytes 4194304 | tf_op jit(solution)/shard_map/all_to_all | solution.py:215
  61.6 47.2 %copy-start.1 = (s32[8,1,128]{2,1,0:T(1,128)S(1)}, s32[8,1,128]{2,1,0:T(1,128)}, u32[]{:S(2)}) copy-start(s32[8,1,128]{2,1,0:T(1,128)} %all-gather.1.words_ref) | copy-start | bytes 12292
  97.7 65.1 %all-to-all-start.1 = ((bf16[512,16,128]{2,1,0:T(8,128)(2,1)}), bf16[512,16,128]{2,1,0:T(8,128)(2,1)}, u32[]{:S(2)}, u32[]{:S(2)}) async-start(bf16[512,16,128]{2,1,0:T(8,128)(2,1)} %lookup.1), calls=%async_computation.1 | async-start | bytes 4194304 | tf_op jit(solution)/shard_map/all_to_all | solution.py:215

commit v9 on v8

--- a/solution.py
+++ b/solution.py
@@ -93,27 +93,6 @@
         ),
         name="pack",
     )(slot, cotangent)
-
-
-def pick_kernel(ids_ref, out_ref):
-    ids = ids_ref[...]
-    owners, lanes = ids.shape
-    lane = lax.broadcasted_iota(jnp.int32, (owners, lanes), 1)
-    line = lax.broadcasted_iota(jnp.int32, (owners, lanes), 0)
-    out = jnp.zeros((owners, lanes), jnp.int32)
-    for w in range(out_ref.shape[1] // owners):
-        word = jnp.sum(jnp.where(lane == w, ids, 0), axis=1, keepdims=True)
-        out = jnp.where(lane == w * owners + line, word, out)
-    out_ref[...] = jnp.sum(out, axis=0, keepdims=True)
-
-
-def pick(ids, cap):
-    owners = ids.shape[0]
-    return pl.pallas_call(
-        pick_kernel,
-        out_shape=jax.ShapeDtypeStruct((1, cap // 2 * owners), jnp.int32),
-        name="pick",
-    )(ids)
 
 
 def lookup_kernel(cap, words_ref, table_ref, out_ref, lines):
@@ -227,7 +206,8 @@
     packed = pack(slot, cotangent, groups, owners, cap)
     ids, packed = lax.optimization_barrier((ids, packed))
     arrived = exchange(packed, ("group", "vocab"))
-    words = lax.all_gather(pick(ids.reshape(owners, LANES), cap), "group", axis=0)
+    mine = jnp.swapaxes(ids[:, 0, : cap // 2], 0, 1).reshape(1, cap // 2 * owners)
+    words = lax.all_gather(mine, "group", axis=0)
     got = exchange(lookup(words, table, owners, cap), ("group", "vocab"))
     words = words.reshape(groups, cap // 2, owners)
     wanted = jnp.stack([words & 0xFFFF, words >> 16], axis=2).reshape(groups, cap, owners)

time: 166 us -> 166 us (level)
  waiting for transfers between devices: 89.3 us -> 91.2 us
    all_to_all x3, waiting for transfers between devices: 89.3 us -> 91.2 us  [exchange(): return lax.all_to_all(x, axes, split_axis=0, concat_axis=0, tiled=True)]
  transfers between devices with their start and end apart: 3 -> 3, of which waited for: 3 -> 3; matrix products, arithmetic and copies ran while one was open for 5% -> 5% of each run, Pallas kernels for 7% -> 6%
where the time goes in v9:
time: 166 us; the launch traced here: 165 us
  waiting for transfers between devices  91.2 us (55%)
  starting transfers between devices  38.5 us (23%)
  Pallas kernels  14.1 us (8%)
  blocking collectives  12.2 us (7%)
  matrix products  5.28 us (3%)
  local copies, waits for them, and re-layouts  3.21 us (2%)
    all_to_all x3, waiting for transfers between devices, exchange(): return lax.all_to_all(x, axes, split_axis=0, concat_axis=0, tiled=True)  91.2 us
    all_to_all x3, starting transfers between devices, exchange(): return lax.all_to_all(x, axes, split_axis=0, concat_axis=0, tiled=True)  38.5 us
    all_gather x1, blocking collectives, per_device(): words = lax.all_gather(mine, 'group', axis=0)  12.2 us
    pallas_call x1, Pallas kernels, lookup(): pl.pallas_call(functools.partial(lookup_kernel, cap), grid=(groups // ste...  6.4 us
    dot_general x1, matrix products, per_device(): lax.dot_general(picker, arrived.reshape(peers * cap, columns), (((0,), (0...  5.28 us
  transfers between devices with their start and end apart: 3, of which 3 were waited for; matrix products, arithmetic and copies ran while one was open for 5% of the time, Pallas kernels for 6%

profile of v9, /device:TPU:1, one launch (start us, length us, event | category | flops | bytes accessed | tf_op | source)
XLA Modules:
  0.0 165.3 jit_solution(2272139759789395189)
XLA Ops:
  0.6 1.5 slots.1
  2.2 17.1 %all-to-all-start = ((s32[64,1,128]{2,1,0:T(1,128)}), s32[64,1,128]{2,1,0:T(1,128)S(1)}, u32[]{:S(2)}, u32[]{:S(2)}) async-start(s32[64,1,128]{2,1,0:T(1,128)} %bitcast.15), calls=%async_computation | async-start | bytes 65536 | tf_op jit(solution)/shard_map/all_to_all | solution.py:194
  19.3 3.2 %pack.1 = bf16[512,16,128]{2,1,0:T(8,128)(2,1)} custom-call(s32[1,128]{1,0:T(1,128)} %get-tuple-element.6.slot_ref, bf16[128,4096]{1,0:T(8,128)(2,1)} %cot_ref.1), custom_call_target="tpu_custom_call" | custom-call | flops 268435456 | bytes 3145728 | tf_op jit(solution)/shard_map/pack/pallas_call | solution.py:76
  22.5 7.6 %all-to-all-done = s32[64,1,128]{2,1,0:T(1,128)S(1)} async-done(((s32[64,1,128]{2,1,0:T(1,128)}), s32[64,1,128]{2,1,0:T(1,128)S(1)}, u32[]{:S(2)}, u32[]{:S(2)}) %all-to-all-start) | async-done | bytes 32800 | tf_op jit(solution)/shard_map/all_to_all | solution.py:194
  30.1 10.3 %all-to-all-start.2 = ((bf16[512,16,128]{2,1,0:T(8,128)(2,1)}), bf16[512,16,128]{2,1,0:T(8,128)(2,1)S(1)}, u32[]{:S(2)}, u32[]{:S(2)}) async-start(bf16[512,16,128]{2,1,0:T(8,128)(2,1)} %pack.1), calls=%async_computation.2 | async-start | bytes 4194304 | tf_op jit(solution)/shard_map/all_to_all | solution.py:194
  40.4 0.1 copy.19
  40.5 0.1 all_gather_reshape.3
  40.5 12.2 %all_gather.3.words_ref = s32[8,1,128]{2,1,0:T(1,128)} all-gather(s32[1,1,128]{2,1,0:T(1,128)S(1)} %all_gather_reshape.3), channel_id=1, replica_groups=mesh['group'=8,'vocab'=64] {'group'}, dimensions={0}, use_global_device_ids=true | all-gather | bytes 4608 | tf_op jit(solution)/shard_map/all_gather | solution.py:210
  52.7 6.4 %lookup.1 = bf16[512,16,128]{2,1,0:T(8,128)(2,1)} custom-call(s32[8,1,128]{2,1,0:T(1,128)} %all_gather.3.words_ref, bf16[1002,512]{1,0:T(8,128)(2,1)} %table_ref.1), custom_call_target="tpu_custom_call" | custom-call | flops 2101346304 | bytes 3123200 | tf_op jit(solution)/shard_map/lookup/pallas_call | solution.py:130
  59.1 0.0 copy-start
  59.1 38.0 %all-to-all-done.2 = bf16[512,16,128]{2,1,0:T(8,128)(2,1)S(1)} async-done(((bf16[512,16,128]{2,1,0:T(8,128)(2,1)}), bf16[512,16,128]{2,1,0:T(8,128)(2,1)S(1)}, u32[]{:S(2)}, u32[]{:S(2)}) %all-to-all-start.2) | async-done | bytes 2097184 | tf_op jit(solution)/shard_map/all_to_all | solution.py:194
  97.1 11.1 %all-to-all-start.1 = ((bf16[512,16,128]{2,1,0:T(8,128)(2,1)}), bf16[512,16,128]{2,1,0:T(8,128)(2,1)}, u32[]{:S(2)}, u32[]{:S(2)}) async-start(bf16[512,16,128]{2,1,0:T(8,128)(2,1)} %lookup.1), calls=%async_computation.1 | async-start | bytes 4194304 | tf_op jit(solution)/shard_map/all_to_all | solution.py:194
  108.2 0.0 copy-done
  108.3 0.1 and.18
  108.4 0.1 shift_right_arithmetic.18
  108.4 0.2 copy.22
  108.6 0.2 sub.13
  108.8 2.6 %reshape.55 = bf16[2048,512]{1,0:T(8,128)(2,1)} reshape(bf16[512,16,128]{2,1,0:T(8,128)(2,1)S(1)} %all-to-all-done.2) | data formatting | bytes 4194304 | tf_op jit(solution)/shard_map/reshape | solution.py:218
  111.3 5.3 %fusion.2 = bf16[1002,512]{1,0:T(8,128)(2,1)} fusion(bf16[2048,512]{1,0:T(8,128)(2,1)} %reshape.55, s32[2048]{0:T(1024)S(1)} %sub.13), kind=kOutput, calls=%fused_computation.3 | convolution fusion | flops 2103911424 | bytes 3131392 | tf_op jit(solution)/shard_map/dot_general | solution.py:216
  116.6 45.6 %all-to-all-done.1.got_ref = bf16[512,16,128]{2,1,0:T(8,128)(2,1)} async-done(((bf16[512,16,128]{2,1,0:T(8,128)(2,1)}), bf16[512,16,128]{2,1,0:T(8,128)(2,1)}, u32[]{:S(2)}, u32[]{:S(2)}) %all-to-all-start.1) | async-done | bytes 2097184 | tf_op jit(solution)/shard_map/all_to_all | solution.py:194
  162.2 3.0 %unpack.1 = bf16[128,4096]{1,0:T(8,128)(2,1)} custom-call(s32[1,128]{1,0:T(1,128)} %get-tuple-element.6.slot_ref, bf16[512,16,128]{2,1,0:T(8,128)(2,1)} %all-to-all-done.1.got_ref), custom_call_target="tpu_custom_call" | custom-call | tf_op jit(solution)/shard_map/unpack/pallas_call | solution.py:176
  (4 shorter events, 0.0 us)
Async XLA Ops:
  2.2 27.9 %all-to-all-start = ((s32[64,1,128]{2,1,0:T(1,128)}), s32[64,1,128]{2,1,0:T(1,128)S(1)}, u32[]{:S(2)}, u32[]{:S(2)}) async-start(s32[64,1,128]{2,1,0:T(1,128)} %bitcast.15), calls=%async_computation | async-start | bytes 65536 | tf_op jit(solution)/shard_map/all_to_all | solution.py:194
  30.1 67.0 %all-to-all-start.2 = ((bf16[512,16,128]{2,1,0:T(8,128)(2,1)}), bf16[512,16,128]{2,1,0:T(8,128)(2,1)S(1)}, u32[]{:S(2)}, u32[]{:S(2)}) async-start(bf16[512,16,128]{2,1,0:T(8,128)(2,1)} %pack.1), calls=%async_computation.2 | async-start | bytes 4194304 | tf_op jit(solution)/shard_map/all_to_all | solution.py:194
  59.1 49.1 %copy-start = (s32[8,1,128]{2,1,0:T(1,128)S(1)}, s32[8,1,128]{2,1,0:T(1,128)}, u32[]{:S(2)}) copy-start(s32[8,1,128]{2,1,0:T(1,128)} %all_gather.3.words_ref) | copy-start | bytes 12292
  97.1 65.1 %all-to-all-start.1 = ((bf16[512,16,128]{2,1,0:T(8,128)(2,1)}), bf16[512,16,128]{2,1,0:T(8,128)(2,1)}, u32[]{:S(2)}, u32[]{:S(2)}) async-start(bf16[512,16,128]{2,1,0:T(8,128)(2,1)} %lookup.1), calls=%async_computation.1 | async-start | bytes 4194304 | tf_op jit(solution)/shard_map/all_to_all | solution.py:194

commit v10 on v9

--- a/solution.py
+++ b/solution.py
@@ -95,7 +95,12 @@
     )(slot, cotangent)
 
 
-def lookup_kernel(cap, words_ref, table_ref, out_ref, lines):
+def lookup_kernel(cap, slot_ref, words_ref, table_ref, out_ref, hot_ref, lines):
+    @pl.when(pl.program_id(0) == 0)
+    def _():
+        place = lax.broadcasted_iota(jnp.int32, hot_ref.shape, 1)
+        hot_ref[...] = jnp.where(place == to_column(slot_ref[...]), 1.0, 0.0).astype(jnp.bfloat16)
+
     groups = words_ref.shape[0]
     devices = out_ref.shape[0]
     rows, columns = table_ref.shape
@@ -122,7 +127,8 @@
     out_ref[...] = lines[...].astype(jnp.bfloat16).reshape(out_ref.shape)
 
 
-def lookup(words, table, owners, cap):
+def lookup(slot, words, table, owners, cap):
+    tokens = slot.shape[1]
     groups = words.shape[0]
     rows, columns = table.shape
     pieces = columns // LANES
@@ -131,11 +137,18 @@
         functools.partial(lookup_kernel, cap),
         grid=(groups // step,),
         in_specs=[
+            pl.BlockSpec((1, tokens), lambda g: (0, 0)),
             pl.BlockSpec((step, 1, words.shape[2]), lambda g: (g, 0, 0)),
             pl.BlockSpec((rows, columns), lambda g: (0, 0)),
         ],
-        out_specs=pl.BlockSpec((step * owners, cap * pieces, LANES), lambda g: (g, 0, 0)),
-        out_shape=jax.ShapeDtypeStruct((groups * owners, cap * pieces, LANES), jnp.bfloat16),
+        out_specs=[
+            pl.BlockSpec((step * owners, cap * pieces, LANES), lambda g: (g, 0, 0)),
+            pl.BlockSpec((tokens, owners * cap), lambda g: (0, 0)),
+        ],
+        out_shape=[
+            jax.ShapeDtypeStruct((groups * owners, cap * pieces, LANES), jnp.bfloat16),
+            jax.ShapeDtypeStruct((tokens, owners * cap), jnp.bfloat16),
+        ],
         scratch_shapes=[pltpu.VMEM((step * owners * cap * pieces, LANES), jnp.float32)],
         cost_estimate=pl.CostEstimate(
             flops=2 * groups * owners * cap * rows * columns,
@@ -143,18 +156,12 @@
             transcendentals=0,
         ),
         name="lookup",
-    )(words, table)
-
-
-def unpack_kernel(pieces, slot_ref, got_ref, out_ref, hot, wide):
-    tokens, places = hot.shape
+    )(slot, words, table)
+
+
+def unpack_kernel(pieces, hot_ref, got_ref, out_ref, wide):
+    places = hot_ref.shape[1]
     lines = wide.shape[0]
-
-    @pl.when(pl.program_id(0) == 0)
-    def _():
-        line = lax.broadcasted_iota(jnp.int32, (tokens, places), 1)
-        hot[...] = jnp.where(line == to_column(slot_ref[...]), 1.0, 0.0).astype(jnp.bfloat16)
-
     columns = pieces * LANES
     groups = out_ref.shape[1] // columns
     owners = got_ref.shape[0] // groups
@@ -163,12 +170,12 @@
         rows = jnp.concatenate(
             [wide[pl.ds(c, places, stride=pieces), :].astype(jnp.bfloat16) for c in range(pieces)], axis=1
         )
-        picked = jnp.dot(hot[...], rows, preferred_element_type=jnp.float32)
+        picked = jnp.dot(hot_ref[...], rows, preferred_element_type=jnp.float32)
         out_ref[:, g * columns : (g + 1) * columns] = picked.astype(jnp.bfloat16)
 
 
-def unpack(slot, got, groups, width):
-    tokens = slot.shape[1]
+def unpack(hot, got, groups, width):
+    tokens = hot.shape[0]
     pieces = width // groups // LANES
     owners = got.shape[0] // groups
     lines = owners * got.shape[1]
@@ -177,17 +184,14 @@
         functools.partial(unpack_kernel, pieces),
         grid=(groups // step,),
         in_specs=[
-            pl.BlockSpec((1, tokens), lambda g: (0, 0)),
+            pl.BlockSpec(hot.shape, lambda g: (0, 0)),
             pl.BlockSpec((step * owners, got.shape[1], LANES), lambda g: (g, 0, 0)),
         ],
         out_specs=pl.BlockSpec((tokens, step * pieces * LANES), lambda g: (0, g)),
         out_shape=jax.ShapeDtypeStruct((tokens, width), jnp.bfloat16),
-        scratch_shapes=[
-            pltpu.VMEM((tokens, lines // pieces), jnp.bfloat16),
-            pltpu.VMEM((lines, LANES), jnp.float32),
-        ],
+        scratch_shapes=[pltpu.VMEM((lines, LANES), jnp.float32)],
         name="unpack",
-    )(slot, got)
+    )(hot, got)
 
 
 def exchange(x, axes):
@@ -208,7 +212,8 @@
     arrived = exchange(packed, ("group", "vocab"))
     mine = jnp.swapaxes(ids[:, 0, : cap // 2], 0, 1).reshape(1, cap // 2 * owners)
     words = lax.all_gather(mine, "group", axis=0)
-    got = exchange(lookup(words, table, owners, cap), ("group", "vocab"))
+    found, hot = lookup(slot, words, table, owners, cap)
+    got = exchange(found, ("group", "vocab"))
     words = words.reshape(groups, cap // 2, owners)
     wanted = jnp.stack([words & 0xFFFF, words >> 16], axis=2).reshape(groups, cap, owners)
     wanted = jnp.swapaxes(wanted, 1, 2).reshape(-1) - 1
@@ -219,7 +224,7 @@
         (((0,), (0,)), ((), ())),
         preferred_element_type=jnp.float32,
     )
-    embeds = unpack(slot, got, groups, width)
+    embeds = unpack(hot, got, groups, width)
     return (embeds, table_grad.astype(jnp.bfloat16))
 
 

time: 166 us -> 166 us (level)
  no operation moved by 1% of the time
where the time goes in v10:
time: 166 us; the launch traced here: 165 us
  waiting for transfers between devices  90.6 us (55%)
  starting transfers between devices  38.7 us (23%)
  Pallas kernels  14.1 us (8%)
  blocking collectives  12.6 us (8%)
  matrix products  5.28 us (3%)
  local copies, waits for them, and re-layouts  3.22 us (2%)
    all_to_all x3, waiting for transfers between devices, exchange(): return lax.all_to_all(x, axes, split_axis=0, concat_axis=0, tiled=True)  90.6 us
    all_to_all x3, starting transfers between devices, exchange(): return lax.all_to_all(x, axes, split_axis=0, concat_axis=0, tiled=True)  38.7 us
    all_gather x1, blocking collectives, per_device(): words = lax.all_gather(mine, 'group', axis=0)  12.6 us
    pallas_call x1, Pallas kernels, lookup(): pl.pallas_call(functools.partial(lookup_kernel, cap), grid=(groups // ste...  6.56 us
    dot_general x1, matrix products, per_device(): lax.dot_general(picker, arrived.reshape(peers * cap, columns), (((0,), (0...  5.28 us
  transfers between devices with their start and end apart: 3, of which 3 were waited for; matrix products, arithmetic and copies ran while one was open for 5% of the time, Pallas kernels for 6%

profile of v10, /device:TPU:1, one launch (start us, length us, event | category | flops | bytes accessed | tf_op | source)
XLA Modules:
  0.0 165.3 jit_solution(8349845822907577633)
XLA Ops:
  0.6 1.5 slots.1
  2.2 17.1 %all-to-all-start = ((s32[64,1,128]{2,1,0:T(1,128)}), s32[64,1,128]{2,1,0:T(1,128)S(1)}, u32[]{:S(2)}, u32[]{:S(2)}) async-start(s32[64,1,128]{2,1,0:T(1,128)} %bitcast.15), calls=%async_computation | async-start | bytes 65536 | tf_op jit(solution)/shard_map/all_to_all | solution.py:198
  19.3 3.1 %pack.1 = bf16[512,16,128]{2,1,0:T(8,128)(2,1)} custom-call(s32[1,128]{1,0:T(1,128)} %get-tuple-element.8.slot_ref, bf16[128,4096]{1,0:T(8,128)(2,1)} %cot_ref.1), custom_call_target="tpu_custom_call" | custom-call | flops 268435456 | bytes 3145728 | tf_op jit(solution)/shard_map/pack/pallas_call | solution.py:76
  22.5 7.6 %all-to-all-done = s32[64,1,128]{2,1,0:T(1,128)S(1)} async-done(((s32[64,1,128]{2,1,0:T(1,128)}), s32[64,1,128]{2,1,0:T(1,128)S(1)}, u32[]{:S(2)}, u32[]{:S(2)}) %all-to-all-start) | async-done | bytes 32800 | tf_op jit(solution)/shard_map/all_to_all | solution.py:198
  30.1 10.3 %all-to-all-start.2 = ((bf16[512,16,128]{2,1,0:T(8,128)(2,1)}), bf16[512,16,128]{2,1,0:T(8,128)(2,1)S(1)}, u32[]{:S(2)}, u32[]{:S(2)}) async-start(bf16[512,16,128]{2,1,0:T(8,128)(2,1)} %pack.1), calls=%async_computation.2 | async-start | bytes 4194304 | tf_op jit(solution)/shard_map/all_to_all | solution.py:198
  40.4 0.1 copy.19
  40.5 0.1 all_gather_reshape.3
  40.5 12.6 %all_gather.3.words_ref = s32[8,1,128]{2,1,0:T(1,128)} all-gather(s32[1,1,128]{2,1,0:T(1,128)S(1)} %all_gather_reshape.3), channel_id=1, replica_groups=mesh['group'=8,'vocab'=64] {'group'}, dimensions={0}, use_global_device_ids=true | all-gather | bytes 4608 | tf_op jit(solution)/shard_map/all_gather | solution.py:214
  53.2 6.6 %lookup.1 = (bf16[512,16,128]{2,1,0:T(8,128)(2,1)}, bf16[128,256]{1,0:T(8,128)(2,1)}) custom-call(s32[1,128]{1,0:T(1,128)} %get-tuple-element.8.slot_ref, s32[8,1,128]{2,1,0:T(1,128)} %all_gather.3.words_ref, bf16[1002,512]{1,0:T(8,128)(2,1)} %table_ref.1), custom_call_target="tpu_custom_call" | custom-call | flops 2101346304 | bytes 3123200 | tf_op jit(solution)/shard_map/lookup/pallas_call | solution.py:136
  59.7 37.4 %all-to-all-done.2 = bf16[512,16,128]{2,1,0:T(8,128)(2,1)S(1)} async-done(((bf16[512,16,128]{2,1,0:T(8,128)(2,1)}), bf16[512,16,128]{2,1,0:T(8,128)(2,1)S(1)}, u32[]{:S(2)}, u32[]{:S(2)}) %all-to-all-start.2) | async-done | bytes 2097184 | tf_op jit(solution)/shard_map/all_to_all | solution.py:198
  97.1 0.0 copy-start
  97.1 11.2 %all-to-all-start.1 = ((bf16[512,16,128]{2,1,0:T(8,128)(2,1)}), bf16[512,16,128]{2,1,0:T(8,128)(2,1)}, u32[]{:S(2)}, u32[]{:S(2)}) async-start(bf16[512,16,128]{2,1,0:T(8,128)(2,1)} %get-tuple-element.12), calls=%async_computation.1 | async-start | bytes 4194304 | tf_op jit(solution)/shard_map/all_to_all | solution.py:198
  108.4 0.0 copy-done
  108.4 0.1 and.18
  108.5 0.1 shift_right_arithmetic.18
  108.6 0.2 copy.22
  108.7 0.2 sub.13
  108.9 2.6 %reshape.55 = bf16[2048,512]{1,0:T(8,128)(2,1)} reshape(bf16[512,16,128]{2,1,0:T(8,128)(2,1)S(1)} %all-to-all-done.2) | data formatting | bytes 4194304 | tf_op jit(solution)/shard_map/reshape | solution.py:223
  111.5 5.3 %fusion.2 = bf16[1002,512]{1,0:T(8,128)(2,1)} fusion(bf16[2048,512]{1,0:T(8,128)(2,1)} %reshape.55, s32[2048]{0:T(1024)S(1)} %sub.13), kind=kOutput, calls=%fused_computation.3 | convolution fusion | flops 2103911424 | bytes 3131392 | tf_op jit(solution)/shard_map/dot_general | solution.py:221
  116.8 45.6 %all-to-all-done.1.got_ref = bf16[512,16,128]{2,1,0:T(8,128)(2,1)} async-done(((bf16[512,16,128]{2,1,0:T(8,128)(2,1)}), bf16[512,16,128]{2,1,0:T(8,128)(2,1)}, u32[]{:S(2)}, u32[]{:S(2)}) %all-to-all-start.1) | async-done | bytes 2097184 | tf_op jit(solution)/shard_map/all_to_all | solution.py:198
  162.4 2.9 %unpack.1 = bf16[128,4096]{1,0:T(8,128)(2,1)} custom-call(bf16[128,256]{1,0:T(8,128)(2,1)} %get-tuple-element.11.hot_ref, bf16[512,16,128]{2,1,0:T(8,128)(2,1)} %all-to-all-done.1.got_ref), custom_call_target="tpu_custom_call" | custom-call | tf_op jit(solution)/shard_map/unpack/pallas_call | solution.py:183
  (4 shorter events, 0.0 us)
Async XLA Ops:
  2.2 27.9 %all-to-all-start = ((s32[64,1,128]{2,1,0:T(1,128)}), s32[64,1,128]{2,1,0:T(1,128)S(1)}, u32[]{:S(2)}, u32[]{:S(2)}) async-start(s32[64,1,128]{2,1,0:T(1,128)} %bitcast.15), calls=%async_computation | async-start | bytes 65536 | tf_op jit(solution)/shard_map/all_to_all | solution.py:198
  30.1 67.0 %all-to-all-start.2 = ((bf16[512,16,128]{2,1,0:T(8,128)(2,1)}), bf16[512,16,128]{2,1,0:T(8,128)(2,1)S(1)}, u32[]{:S(2)}, u32[]{:S(2)}) async-start(bf16[512,16,128]{2,1,0:T(8,128)(2,1)} %pack.1), calls=%async_computation.2 | async-start | bytes 4194304 | tf_op jit(solution)/shard_map/all_to_all | solution.py:198
  97.1 11.3 %copy-start = (s32[8,1,128]{2,1,0:T(1,128)S(1)}, s32[8,1,128]{2,1,0:T(1,128)}, u32[]{:S(2)}) copy-start(s32[8,1,128]{2,1,0:T(1,128)} %all_gather.3.words_ref) | copy-start | bytes 12292
  97.1 65.3 %all-to-all-start.1 = ((bf16[512,16,128]{2,1,0:T(8,128)(2,1)}), bf16[512,16,128]{2,1,0:T(8,128)(2,1)}, u32[]{:S(2)}, u32[]{:S(2)}) async-start(bf16[512,16,128]{2,1,0:T(8,128)(2,1)} %get-tuple-element.12), calls=%async_computation.1 | async-start | bytes 4194304 | tf_op jit(solution)/shard_map/all_to_all | solution.py:198

commit v11 on v10

--- a/solution.py
+++ b/solution.py
@@ -161,14 +161,14 @@
 
 def unpack_kernel(pieces, hot_ref, got_ref, out_ref, wide):
     places = hot_ref.shape[1]
-    lines = wide.shape[0]
+    lines = wide.shape[1]
     columns = pieces * LANES
     groups = out_ref.shape[1] // columns
     owners = got_ref.shape[0] // groups
     for g in range(groups):
-        wide[...] = got_ref[g * owners : (g + 1) * owners].reshape(lines, LANES).astype(jnp.float32)
+        wide[g % 2] = got_ref[g * owners : (g + 1) * owners].reshape(lines, LANES).astype(jnp.float32)
         rows = jnp.concatenate(
-            [wide[pl.ds(c, places, stride=pieces), :].astype(jnp.bfloat16) for c in range(pieces)], axis=1
+            [wide[g % 2, pl.ds(c, places, stride=pieces), :].astype(jnp.bfloat16) for c in range(pieces)], axis=1
         )
         picked = jnp.dot(hot_ref[...], rows, preferred_element_type=jnp.float32)
         out_ref[:, g * columns : (g + 1) * columns] = picked.astype(jnp.bfloat16)
@@ -189,7 +189,7 @@
         ],
         out_specs=pl.BlockSpec((tokens, step * pieces * LANES), lambda g: (0, g)),
         out_shape=jax.ShapeDtypeStruct((tokens, width), jnp.bfloat16),
-        scratch_shapes=[pltpu.VMEM((lines, LANES), jnp.float32)],
+        scratch_shapes=[pltpu.VMEM((2, lines, LANES), jnp.float32)],
         name="unpack",
     )(hot, got)
 

time: 166 us -> 166 us (level)
  no operation moved by 1% of the time
where the time goes in v11:
time: 166 us; the launch traced here: 165 us
  waiting for transfers between devices  90.6 us (55%)
  starting transfers between devices  38.7 us (23%)
  Pallas kernels  14.2 us (9%)
  blocking collectives  12.6 us (8%)
  matrix products  5.28 us (3%)
  local copies, waits for them, and re-layouts  3.22 us (2%)
    all_to_all x3, waiting for transfers between devices, exchange(): return lax.all_to_all(x, axes, split_axis=0, concat_axis=0, tiled=True)  90.6 us
    all_to_all x3, starting transfers between devices, exchange(): return lax.all_to_all(x, axes, split_axis=0, concat_axis=0, tiled=True)  38.7 us
    all_gather x1, blocking collectives, per_device(): words = lax.all_gather(mine, 'group', axis=0)  12.6 us
    pallas_call x1, Pallas kernels, lookup(): pl.pallas_call(functools.partial(lookup_kernel, cap), grid=(groups // ste...  6.56 us
    dot_general x1, matrix products, per_device(): lax.dot_general(picker, arrived.reshape(peers * cap, columns), (((0,), (0...  5.28 us
  transfers between devices with their start and end apart: 3, of which 3 were waited for; matrix products, arithmetic and copies ran while one was open for 5% of the time, Pallas kernels for 6%

profile of v11, /device:TPU:1, one launch (start us, length us, event | category | flops | bytes accessed | tf_op | source)
XLA Modules:
  0.0 165.3 jit_solution(10854761530752616642)
XLA Ops:
  0.6 1.5 slots.1
  2.2 17.1 %all-to-all-start = ((s32[64,1,128]{2,1,0:T(1,128)}), s32[64,1,128]{2,1,0:T(1,128)S(1)}, u32[]{:S(2)}, u32[]{:S(2)}) async-start(s32[64,1,128]{2,1,0:T(1,128)} %bitcast.15), calls=%async_computation | async-start | bytes 65536 | tf_op jit(solution)/shard_map/all_to_all | solution.py:198
  19.3 3.1 %pack.1 = bf16[512,16,128]{2,1,0:T(8,128)(2,1)} custom-call(s32[1,128]{1,0:T(1,128)} %get-tuple-element.8.slot_ref, bf16[128,4096]{1,0:T(8,128)(2,1)} %cot_ref.1), custom_call_target="tpu_custom_call" | custom-call | flops 268435456 | bytes 3145728 | tf_op jit(solution)/shard_map/pack/pallas_call | solution.py:76
  22.5 7.6 %all-to-all-done = s32[64,1,128]{2,1,0:T(1,128)S(1)} async-done(((s32[64,1,128]{2,1,0:T(1,128)}), s32[64,1,128]{2,1,0:T(1,128)S(1)}, u32[]{:S(2)}, u32[]{:S(2)}) %all-to-all-start) | async-done | bytes 32800 | tf_op jit(solution)/shard_map/all_to_all | solution.py:198
  30.1 10.3 %all-to-all-start.2 = ((bf16[512,16,128]{2,1,0:T(8,128)(2,1)}), bf16[512,16,128]{2,1,0:T(8,128)(2,1)S(1)}, u32[]{:S(2)}, u32[]{:S(2)}) async-start(bf16[512,16,128]{2,1,0:T(8,128)(2,1)} %pack.1), calls=%async_computation.2 | async-start | bytes 4194304 | tf_op jit(solution)/shard_map/all_to_all | solution.py:198
  40.4 0.1 copy.19
  40.5 0.1 all_gather_reshape.3
  40.5 12.6 %all_gather.3.words_ref = s32[8,1,128]{2,1,0:T(1,128)} all-gather(s32[1,1,128]{2,1,0:T(1,128)S(1)} %all_gather_reshape.3), channel_id=1, replica_groups=mesh['group'=8,'vocab'=64] {'group'}, dimensions={0}, use_global_device_ids=true | all-gather | bytes 4608 | tf_op jit(solution)/shard_map/all_gather | solution.py:214
  53.2 6.6 %lookup.1 = (bf16[512,16,128]{2,1,0:T(8,128)(2,1)}, bf16[128,256]{1,0:T(8,128)(2,1)}) custom-call(s32[1,128]{1,0:T(1,128)} %get-tuple-element.8.slot_ref, s32[8,1,128]{2,1,0:T(1,128)} %all_gather.3.words_ref, bf16[1002,512]{1,0:T(8,128)(2,1)} %table_ref.1), custom_call_target="tpu_custom_call" | custom-call | flops 2101346304 | bytes 3123200 | tf_op jit(solution)/shard_map/lookup/pallas_call | solution.py:136
  59.7 37.4 %all-to-all-done.2 = bf16[512,16,128]{2,1,0:T(8,128)(2,1)S(1)} async-done(((bf16[512,16,128]{2,1,0:T(8,128)(2,1)}), bf16[512,16,128]{2,1,0:T(8,128)(2,1)S(1)}, u32[]{:S(2)}, u32[]{:S(2)}) %all-to-all-start.2) | async-done | bytes 2097184 | tf_op jit(solution)/shard_map/all_to_all | solution.py:198
  97.1 0.0 copy-start
  97.1 11.2 %all-to-all-start.1 = ((bf16[512,16,128]{2,1,0:T(8,128)(2,1)}), bf16[512,16,128]{2,1,0:T(8,128)(2,1)}, u32[]{:S(2)}, u32[]{:S(2)}) async-start(bf16[512,16,128]{2,1,0:T(8,128)(2,1)} %get-tuple-element.12), calls=%async_computation.1 | async-start | bytes 4194304 | tf_op jit(solution)/shard_map/all_to_all | solution.py:198
  108.4 0.0 copy-done
  108.4 0.1 and.18
  108.5 0.1 shift_right_arithmetic.18
  108.6 0.2 copy.22
  108.7 0.2 sub.13
  108.9 2.6 %reshape.55 = bf16[2048,512]{1,0:T(8,128)(2,1)} reshape(bf16[512,16,128]{2,1,0:T(8,128)(2,1)S(1)} %all-to-all-done.2) | data formatting | bytes 4194304 | tf_op jit(solution)/shard_map/reshape | solution.py:223
  111.5 5.3 %fusion.2 = bf16[1002,512]{1,0:T(8,128)(2,1)} fusion(bf16[2048,512]{1,0:T(8,128)(2,1)} %reshape.55, s32[2048]{0:T(1024)S(1)} %sub.13), kind=kOutput, calls=%fused_computation.3 | convolution fusion | flops 2103911424 | bytes 3131392 | tf_op jit(solution)/shard_map/dot_general | solution.py:221
  116.8 45.6 %all-to-all-done.1.got_ref = bf16[512,16,128]{2,1,0:T(8,128)(2,1)} async-done(((bf16[512,16,128]{2,1,0:T(8,128)(2,1)}), bf16[512,16,128]{2,1,0:T(8,128)(2,1)}, u32[]{:S(2)}, u32[]{:S(2)}) %all-to-all-start.1) | async-done | bytes 2097184 | tf_op jit(solution)/shard_map/all_to_all | solution.py:198
  162.4 2.9 %unpack.1 = bf16[128,4096]{1,0:T(8,128)(2,1)} custom-call(bf16[128,256]{1,0:T(8,128)(2,1)} %get-tuple-element.11.hot_ref, bf16[512,16,128]{2,1,0:T(8,128)(2,1)} %all-to-all-done.1.got_ref), custom_call_target="tpu_custom_call" | custom-call | tf_op jit(solution)/shard_map/unpack/pallas_call | solution.py:183
  (4 shorter events, 0.0 us)
Async XLA Ops:
  2.2 27.9 %all-to-all-start = ((s32[64,1,128]{2,1,0:T(1,128)}), s32[64,1,128]{2,1,0:T(1,128)S(1)}, u32[]{:S(2)}, u32[]{:S(2)}) async-start(s32[64,1,128]{2,1,0:T(1,128)} %bitcast.15), calls=%async_computation | async-start | bytes 65536 | tf_op jit(solution)/shard_map/all_to_all | solution.py:198
  30.1 67.0 %all-to-all-start.2 = ((bf16[512,16,128]{2,1,0:T(8,128)(2,1)}), bf16[512,16,128]{2,1,0:T(8,128)(2,1)S(1)}, u32[]{:S(2)}, u32[]{:S(2)}) async-start(bf16[512,16,128]{2,1,0:T(8,128)(2,1)} %pack.1), calls=%async_computation.2 | async-start | bytes 4194304 | tf_op jit(solution)/shard_map/all_to_all | solution.py:198
  97.1 11.3 %copy-start = (s32[8,1,128]{2,1,0:T(1,128)S(1)}, s32[8,1,128]{2,1,0:T(1,128)}, u32[]{:S(2)}) copy-start(s32[8,1,128]{2,1,0:T(1,128)} %all_gather.3.words_ref) | copy-start | bytes 12292
  97.1 65.3 %all-to-all-start.1 = ((bf16[512,16,128]{2,1,0:T(8,128)(2,1)}), bf16[512,16,128]{2,1,0:T(8,128)(2,1)}, u32[]{:S(2)}, u32[]{:S(2)}) async-start(bf16[512,16,128]{2,1,0:T(8,128)(2,1)} %get-tuple-element.12), calls=%async_computation.1 | async-start | bytes 4194304 | tf_op jit(solution)/shard_map/all_to_all | solution.py:198
